TPU v7x, 32 devices: a whole 2x2x4 slice. The times are simulated.
32 devices in a mesh: ctx: 8 (over y, x, core), fsdp: 4 (over z).
Axes of the slice: x: 2, y: 2, z: 4, core: 2. Of those that a mesh axis runs over, the one named last changes fastest.
Arguments:
- tokens: bfloat16 [4, 1024, 2048], P('fsdp', 'ctx'), may hold values from -6 to 6
- cotangent: bfloat16 [4, 1024, 2048], P('fsdp', 'ctx'), may hold values from -6 to 6
- pairing: int32 [8, 2], replicated, may hold values from 0 to 15, as said below
- norm_attn: float32 [2048], P('fsdp'), may hold values from 0.5 to 1.5
- w_query: bfloat16 [2048, 2048], P('fsdp'), may hold values from -0.125 to 0.125
- w_key: bfloat16 [2048, 512], P('fsdp'), may hold values from -0.125 to 0.125
- w_value: bfloat16 [2048, 512], P('fsdp'), may hold values from -0.125 to 0.125
- w_out: bfloat16 [2048, 2048], P('fsdp'), may hold values from -0.5 to 0.5
- norm_mlp: float32 [2048], P('fsdp'), may hold values from 0.5 to 1.5
- w_gate: bfloat16 [2048, 8192], P('fsdp'), may hold values from -0.125 to 0.125
- w_up: bfloat16 [2048, 8192], P('fsdp'), may hold values from -0.125 to 0.125
- w_down: bfloat16 [8192, 2048], P('fsdp'), may hold values from -0.0625 to 0.0625
Outputs:
- output: bfloat16 [4, 1024, 2048], P('fsdp', 'ctx')
- d_tokens: bfloat16 [4, 1024, 2048], P('fsdp', 'ctx')
- grad_norm_attn: float32 [2048], P('fsdp')
- grad_query: float32 [2048, 2048], P('fsdp')
- grad_key: float32 [2048, 512], P('fsdp')
- grad_value: float32 [2048, 512], P('fsdp')
- grad_out: float32 [2048, 2048], P('fsdp')
- grad_norm_mlp: float32 [2048], P('fsdp')
- grad_gate: float32 [2048, 8192], P('fsdp')
- grad_up: float32 [2048, 8192], P('fsdp')
- grad_down: float32 [8192, 2048], P('fsdp')
Inputs may be any that keep to these rules, and one draw needn't show every extreme that they name: `pairing`: each of the 16 block numbers appears exactly once; each row holds a block number b and its mirror 16 - 1 - b, in either order.
All inputs are finite; a program needn't handle non-finite values.
Results may differ from a plain program's by a relative error of at most 0.035.
Values may be sent and summed in bfloat16 or wider, within the bound.
A program may use at most 448 MiB of HBM per device.

v0:
```python
import math

import jax
import jax.numpy as jnp
from jax import lax
from jax.sharding import PartitionSpec as P

HEAD_DIM = 64
KBLK = 512


EPS = 1e-05
THETA = 500000.0


def frequencies(head_width):
    evens = jnp.arange(0, head_width, 2, dtype=jnp.float32)
    inverse = 1.0 / THETA ** (evens / head_width)
    wavelen = 2.0 * math.pi / inverse
    smooth = (8192.0 / wavelen - 1.0) / 3.0
    middle = (1.0 - smooth) * inverse / 32.0 + smooth * inverse
    return jnp.where(wavelen < 2048.0, inverse, jnp.where(wavelen > 8192.0, inverse / 32.0, middle))


def rotation(positions, head_width):
    angles = positions.astype(jnp.float32)[:, None] * frequencies(head_width)[None, :]
    cosine = jnp.concatenate([jnp.cos(angles), jnp.cos(angles)], axis=1)[:, None, :]
    sine = jnp.concatenate([jnp.sin(angles), jnp.sin(angles)], axis=1)[:, None, :]
    return (cosine, sine)


def rotate(tensor, cosine, sine):
    middle = tensor.shape[-1] // 2
    turned = jnp.concatenate([-tensor[..., middle:], tensor[..., :middle]], axis=-1)
    return tensor * cosine + turned * sine


def unrotate(gradient, cosine, sine):
    middle = gradient.shape[-1] // 2
    moved = gradient * sine
    back_turn = jnp.concatenate([moved[..., middle:], -moved[..., :middle]], axis=-1)
    return gradient * cosine + back_turn


def slot_positions(pairing, seq_length, block_len):
    flattened = pairing.reshape(-1)
    slots = jnp.arange(seq_length, dtype=jnp.int32)
    owning = slots // block_len
    labels = jnp.arange(flattened.shape[0], dtype=jnp.int32)
    anchor = jnp.sum(jnp.where(owning[:, None] == labels[None, :], flattened[None, :], 0), axis=1)
    return anchor * block_len + slots % block_len


def product(left, right):
    return jnp.dot(left, right, preferred_element_type=jnp.float32)


def product_t(left, right):
    return lax.dot_general(
        left, right, (((1,), (1,)), ((), ())), preferred_element_type=jnp.float32
    )


def tokens_t(left, right):
    return lax.dot_general(
        left, right, (((0,), (0,)), ((), ())), preferred_element_type=jnp.float32
    )


def own_columns(matrix, rows):
    return lax.dynamic_slice_in_dim(matrix, lax.axis_index("fsdp") * rows, rows, 1)


def pair_fold(totals, pieces):
    first_rows = totals[0].shape[0]
    second_rows = totals[1].shape[0]
    first = tokens_t(own_columns(pieces[0], first_rows), pieces[1])
    second = tokens_t(own_columns(pieces[2], second_rows), pieces[3])
    return (first, second)


def norm_back(upstream, gain, unit, scale):
    weighted = upstream * gain
    return scale * (weighted - unit * jnp.mean(weighted * unit, axis=1, keepdims=True))


def on_device(
    tokens,
    cotangent,
    pairing,
    norm_attn,
    w_query,
    w_key,
    w_value,
    w_out,
    norm_mlp,
    w_gate,
    w_up,
    w_down,
):
    inputs = tokens[0].astype(jnp.float32)
    tok_rows = inputs.shape[0]
    seq_length = tok_rows * lax.axis_size("ctx")
    heads_kv = w_key.shape[1] // HEAD_DIM
    group_size = w_query.shape[1] // w_key.shape[1]
    all_pos = slot_positions(pairing, seq_length, tok_rows // 2)
    own_pos = lax.dynamic_slice_in_dim(all_pos, lax.axis_index("ctx") * tok_rows, tok_rows)
    cosine, sine = rotation(own_pos, HEAD_DIM)
    factor = HEAD_DIM ** (-0.5)
    gain_attn, query_full, key_full, value_full, out_full = (
        lax.all_gather(norm_attn.astype(jnp.bfloat16), "fsdp", axis=0, tiled=True).astype(
            norm_attn.dtype
        ),
        lax.all_gather(w_query, "fsdp", axis=0, tiled=True),
        lax.all_gather(w_key, "fsdp", axis=0, tiled=True),
        lax.all_gather(w_value, "fsdp", axis=0, tiled=True),
        lax.all_gather(w_out, "fsdp", axis=0, tiled=True),
    )
    scale_attn = lax.rsqrt(jnp.mean(inputs * inputs, axis=1, keepdims=True) + EPS)
    unit_attn = inputs * scale_attn
    normed_attn = (unit_attn * gain_attn).astype(jnp.bfloat16)
    query_rot = rotate(
        product(normed_attn, query_full).reshape(tok_rows, -1, HEAD_DIM), cosine, sine
    )
    queries = query_rot.astype(jnp.bfloat16).reshape(tok_rows, heads_kv, group_size, HEAD_DIM)
    key_rot = rotate(
        product(normed_attn, key_full).reshape(tok_rows, heads_kv, HEAD_DIM), cosine, sine
    )
    keys_local = key_rot.astype(jnp.bfloat16).reshape(tok_rows, heads_kv * HEAD_DIM)
    values_local = product(normed_attn, value_full).astype(jnp.bfloat16)
    keys_all, values_all = (
        lax.all_gather(keys_local, "ctx", axis=0, tiled=True),
        lax.all_gather(values_local, "ctx", axis=0, tiled=True),
    )
    block_count = seq_length // KBLK
    key_blocks = keys_all.reshape(block_count, KBLK, heads_kv, HEAD_DIM)
    value_blocks = values_all.reshape(block_count, KBLK, heads_kv, HEAD_DIM)
    pos_blocks = all_pos.reshape(block_count, KBLK)

    def scores(key_blk, pos_blk):
        logits = jnp.einsum("qhgd,khd->hgqk", queries, key_blk, preferred_element_type=jnp.float32)
        allowed = pos_blk[None, :] <= own_pos[:, None]
        return (jnp.where(allowed, logits * factor, -1e30), allowed)

    def statistics(carry, item):
        running, total = carry
        score_blk, allowed = scores(item[0], item[1])
        newest = jnp.maximum(running, jnp.max(score_blk, axis=-1))
        added = jnp.sum(jnp.where(allowed, jnp.exp(score_blk - newest[..., None]), 0.0), axis=-1)
        return ((newest, total * jnp.exp(running - newest) + added), None)

    start_top = jnp.full((heads_kv, group_size, tok_rows), -1e30, jnp.float32)
    start_sum = jnp.zeros((heads_kv, group_size, tok_rows), jnp.float32)
    (running, total), _ = lax.scan(statistics, (start_top, start_sum), (key_blocks, pos_blocks))
    log_total = running + jnp.log(total)

    def weights_of(score_blk, allowed):
        return jnp.where(allowed, jnp.exp(score_blk - log_total[..., None]), 0.0)

    def attend(acc, item):
        key_blk, value_blk, pos_blk = item
        score_blk, allowed = scores(key_blk, pos_blk)
        probs_low = weights_of(score_blk, allowed).astype(jnp.bfloat16)
        return (
            acc
            + jnp.einsum(
                "hgqk,khd->qhgd", probs_low, value_blk, preferred_element_type=jnp.float32
            ),
            None,
        )

    start_acc = jnp.zeros((tok_rows, heads_kv, group_size, HEAD_DIM), jnp.float32)
    attended, _ = lax.scan(attend, start_acc, (key_blocks, value_blocks, pos_blocks))
    attended_low = attended.reshape(tok_rows, -1).astype(jnp.bfloat16)
    resid = inputs + product(attended_low, out_full)
    gain_mlp, gate_full, up_full, down_full = (
        lax.all_gather(norm_mlp.astype(jnp.bfloat16), "fsdp", axis=0, tiled=True).astype(
            norm_mlp.dtype
        ),
        lax.all_gather(w_gate, "fsdp", axis=0, tiled=True),
        lax.all_gather(w_up, "fsdp", axis=0, tiled=True),
        lax.all_gather(w_down, "fsdp", axis=0, tiled=True),
    )
    scale_mlp = lax.rsqrt(jnp.mean(resid * resid, axis=1, keepdims=True) + EPS)
    unit_mlp = resid * scale_mlp
    normed_mlp = (unit_mlp * gain_mlp).astype(jnp.bfloat16)
    gate_pre = product(normed_mlp, gate_full)
    up_pre = product(normed_mlp, up_full)
    sigma = jax.nn.sigmoid(gate_pre)
    swish = gate_pre * sigma
    hidden = (swish * up_pre).astype(jnp.bfloat16)
    output = resid + product(hidden, down_full)
    upstream = cotangent[0]
    gain_mlp, gate_full, up_full, down_full = (
        lax.all_gather(norm_mlp.astype(jnp.bfloat16), "fsdp", axis=0, tiled=True).astype(
            norm_mlp.dtype
        ),
        lax.all_gather(w_gate, "fsdp", axis=0, tiled=True),
        lax.all_gather(w_up, "fsdp", axis=0, tiled=True),
        lax.all_gather(w_down, "fsdp", axis=0, tiled=True),
    )
    d_hidden = product_t(upstream, down_full)
    d_gate = (d_hidden * up_pre * sigma * (1.0 + gate_pre * (1.0 - sigma))).astype(jnp.bfloat16)
    d_up = (d_hidden * swish).astype(jnp.bfloat16)
    d_normed_mlp = product_t(d_gate, gate_full) + product_t(d_up, up_full)
    gate_up_pair = jnp.concatenate([d_gate, d_up], axis=1)
    ff_width = w_gate.shape[1]
    down_rows = w_down.shape[0]
    model_rows = w_gate.shape[0]
    start_down = jnp.zeros((down_rows, upstream.shape[1]), jnp.float32)
    start_pair = jnp.zeros((model_rows, gate_up_pair.shape[1]), jnp.float32)
    grad_down, grad_pair = pair_fold(
        (start_down, start_pair),
        (
            lax.all_gather(hidden, "fsdp", axis=0, tiled=True),
            lax.all_gather(upstream, "fsdp", axis=0, tiled=True),
            lax.all_gather(normed_mlp, "fsdp", axis=0, tiled=True),
            lax.all_gather(gate_up_pair, "fsdp", axis=0, tiled=True),
        ),
    )
    grad_gate = grad_pair[:, :ff_width]
    grad_up = grad_pair[:, ff_width:]
    gain_mlp_term = jnp.sum(d_normed_mlp * unit_mlp, axis=0)
    d_resid = upstream.astype(jnp.float32) + norm_back(d_normed_mlp, gain_mlp, unit_mlp, scale_mlp)
    d_resid_low = d_resid.astype(jnp.bfloat16)
    gain_attn, query_full, key_full, value_full, out_full = (
        lax.all_gather(norm_attn.astype(jnp.bfloat16), "fsdp", axis=0, tiled=True).astype(
            norm_attn.dtype
        ),
        lax.all_gather(w_query, "fsdp", axis=0, tiled=True),
        lax.all_gather(w_key, "fsdp", axis=0, tiled=True),
        lax.all_gather(w_value, "fsdp", axis=0, tiled=True),
        lax.all_gather(w_out, "fsdp", axis=0, tiled=True),
    )
    d_attended = (
        product_t(d_resid_low, out_full)
        .astype(jnp.bfloat16)
        .reshape(tok_rows, heads_kv, group_size, HEAD_DIM)
    )
    delta = jnp.einsum("qhgd,qhgd->hgq", d_attended.astype(jnp.float32), attended)

    def backward_step(carry, item):
        key_blk, value_blk, pos_blk = item
        score_blk, allowed = scores(key_blk, pos_blk)
        probs = weights_of(score_blk, allowed)
        grad_val = jnp.einsum(
            "hgqk,qhgd->khd",
            probs.astype(jnp.bfloat16),
            d_attended,
            preferred_element_type=jnp.float32,
        )
        d_probs = jnp.einsum(
            "qhgd,khd->hgqk", d_attended, value_blk, preferred_element_type=jnp.float32
        )
        d_score = (probs * (d_probs - delta[..., None]) * factor).astype(jnp.bfloat16)
        carry = carry + jnp.einsum(
            "hgqk,khd->qhgd", d_score, key_blk, preferred_element_type=jnp.float32
        )
        grad_keyblk = jnp.einsum(
            "hgqk,qhgd->khd", d_score, queries, preferred_element_type=jnp.float32
        )
        return (carry, (grad_keyblk, grad_val))

    d_query_rot, (key_terms, value_terms) = lax.scan(
        backward_step, start_acc, (key_blocks, value_blocks, pos_blocks)
    )
    key_sum, value_sum = (
        lax.psum_scatter(
            key_terms.reshape(seq_length, -1).astype(jnp.bfloat16),
            "ctx",
            scatter_dimension=0,
            tiled=True,
        ).astype(jnp.float32),
        lax.psum_scatter(
            value_terms.reshape(seq_length, -1).astype(jnp.bfloat16),
            "ctx",
            scatter_dimension=0,
            tiled=True,
        ).astype(jnp.float32),
    )
    d_query = (
        unrotate(d_query_rot.reshape(tok_rows, -1, HEAD_DIM), cosine, sine)
        .reshape(tok_rows, -1)
        .astype(jnp.bfloat16)
    )
    d_key = (
        unrotate(key_sum.reshape(tok_rows, heads_kv, HEAD_DIM), cosine, sine)
        .reshape(tok_rows, -1)
        .astype(jnp.bfloat16)
    )
    d_value_low = value_sum.astype(jnp.bfloat16)
    d_normed_attn = (
        product_t(d_query, query_full)
        + product_t(d_key, key_full)
        + product_t(d_value_low, value_full)
    )
    joined = jnp.concatenate([d_query, d_key, d_value_low], axis=1)
    out_rows = w_out.shape[0]
    query_rows = w_query.shape[0]
    start_out = jnp.zeros((out_rows, d_resid_low.shape[1]), jnp.float32)
    start_joined = jnp.zeros((query_rows, joined.shape[1]), jnp.float32)
    grad_out, grad_joined = pair_fold(
        (start_out, start_joined),
        (
            lax.all_gather(attended_low, "fsdp", axis=0, tiled=True),
            lax.all_gather(d_resid_low, "fsdp", axis=0, tiled=True),
            lax.all_gather(normed_attn, "fsdp", axis=0, tiled=True),
            lax.all_gather(joined, "fsdp", axis=0, tiled=True),
        ),
    )
    query_width = w_query.shape[1]
    key_width = w_key.shape[1]
    grad_query = grad_joined[:, :query_width]
    grad_key = grad_joined[:, query_width : query_width + key_width]
    grad_value = grad_joined[:, query_width + key_width :]
    gain_attn_term = jnp.sum(d_normed_attn * unit_attn, axis=0)
    d_inputs = d_resid + norm_back(d_normed_attn, gain_attn, unit_attn, scale_attn)
    gain_attn_part, gain_mlp_part = (
        lax.psum_scatter(gain_attn_term, "fsdp", scatter_dimension=0, tiled=True),
        lax.psum_scatter(gain_mlp_term, "fsdp", scatter_dimension=0, tiled=True),
    )
    summed = (
        lax.psum(gain_attn_part.astype(jnp.bfloat16), "ctx").astype(jnp.float32),
        lax.psum(grad_query.astype(jnp.bfloat16), "ctx").astype(jnp.float32),
        lax.psum(grad_key.astype(jnp.bfloat16), "ctx").astype(jnp.float32),
        lax.psum(grad_value.astype(jnp.bfloat16), "ctx").astype(jnp.float32),
        lax.psum(grad_out.astype(jnp.bfloat16), "ctx").astype(jnp.float32),
        lax.psum(gain_mlp_part.astype(jnp.bfloat16), "ctx").astype(jnp.float32),
        lax.psum(grad_gate.astype(jnp.bfloat16), "ctx").astype(jnp.float32),
        lax.psum(grad_up.astype(jnp.bfloat16), "ctx").astype(jnp.float32),
        lax.psum(grad_down.astype(jnp.bfloat16), "ctx").astype(jnp.float32),
    )
    return (
        output.astype(jnp.bfloat16)[None],
        d_inputs.astype(jnp.bfloat16)[None],
        summed[0],
        summed[1],
        summed[2],
        summed[3],
        summed[4],
        summed[5],
        summed[6],
        summed[7],
        summed[8],
    )


def solution(mesh):
    return jax.shard_map(
        on_device,
        mesh=mesh,
        in_specs=(
            P("fsdp", "ctx", None),
            P("fsdp", "ctx", None),
            P(),
            P("fsdp"),
            P("fsdp", None),
            P("fsdp", None),
            P("fsdp", None),
            P("fsdp", None),
            P("fsdp"),
            P("fsdp", None),
            P("fsdp", None),
            P("fsdp", None),
        ),
        out_specs=(
            P("fsdp", "ctx", None),
            P("fsdp", "ctx", None),
            P("fsdp"),
            P("fsdp", None),
            P("fsdp", None),
            P("fsdp", None),
            P("fsdp", None),
            P("fsdp"),
            P("fsdp", None),
            P("fsdp", None),
            P("fsdp", None),
        ),
        check_vma=False,
    )
```

profile of v0, /device:TPU:17, one launch (start us, length us, event | category | flops | bytes accessed | tf_op | source)
XLA Modules:
  0.0 3505.6 jit_solution(8441512161050424623)
XLA Ops:
  9.4 7.5 all-gather.1
  19.5 35.7 %all-gather.21.cloned.1.call-done = bf16[2048,512]{1,0:T(8,128)(2,1)} async-done(((bf16[512,512]{1,0:T(8,128)(2,1)}), bf16[2048,512]{1,0:T(8,128)(2,1)}) %all-gather.21.cloned.1.call-update) | async-done | bytes 2097168 | tf_op jit(solution)/shard_map/all_gather | solution.py:116
  59.3 42.2 %all-gather.25.cloned.1.call-done = bf16[2048,512]{1,0:T(8,128)(2,1)} async-done(((bf16[512,512]{1,0:T(8,128)(2,1)}), bf16[2048,512]{1,0:T(8,128)(2,1)}) %all-gather.25.cloned.1.call-update) | async-done | bytes 2097168 | tf_op jit(solution)/shard_map/all_gather | solution.py:115
  109.6 9.4 all-gather.2
  119.0 9.0 all-gather.23.cloned.1.call-done
  135.2 18.7 all-gather.27.cloned.1.call-done
  158.0 144.8 %all-gather.29.cloned.1.call-done = bf16[2048,2048]{1,0:T(8,128)(2,1)} async-done(((bf16[512,2048]{1,0:T(8,128)(2,1)}), bf16[2048,2048]{1,0:T(8,128)(2,1)}) %all-gather.29.cloned.1.call-update) | async-done | bytes 8388624 | tf_op jit(solution)/shard_map/all_gather | solution.py:114
  302.8 12.3 copy.73
  315.1 6.5 fusion.98
  321.9 19.0 while.39
  322.1 4.7 fusion.186
  341.0 10.2 while.40
  346.0 5.0 fusion.192
  353.2 98.9 %all-gather.31.cloned.1.call-done = bf16[2048,2048]{1,0:T(8,128)(2,1)} async-done(((bf16[512,2048]{1,0:T(8,128)(2,1)}), bf16[2048,2048]{1,0:T(8,128)(2,1)}) %all-gather.31.cloned.1.call-update) | async-done | bytes 8388624 | tf_op jit(solution)/shard_map/all_gather | solution.py:117
  452.1 4.9 multiply_reduce_fusion.2
  458.2 555.1 %all-gather.33.cloned.1.call-done = bf16[2048,8192]{1,0:T(8,128)(2,1)} async-done(((bf16[512,8192]{1,0:T(8,128)(2,1)}), bf16[2048,8192]{1,0:T(8,128)(2,1)}) %all-gather.33.cloned.1.call-update) | async-done | bytes 33554448 | tf_op jit(solution)/shard_map/all_gather | solution.py:180
  1013.3 18.7 fusion.122
  1032.1 542.5 %all-gather.35.cloned.1.call-done = bf16[2048,8192]{1,0:T(8,128)(2,1)} async-done(((bf16[512,8192]{1,0:T(8,128)(2,1)}), bf16[2048,8192]{1,0:T(8,128)(2,1)}) %all-gather.35.cloned.1.call-update) | async-done | bytes 33554448 | tf_op jit(solution)/shard_map/all_gather | solution.py:181
  1574.5 18.7 fusion.123
  1593.3 542.5 %all-gather.37.cloned.1.call-done = bf16[8192,2048]{1,0:T(8,128)(2,1)} async-done(((bf16[2048,2048]{1,0:T(8,128)(2,1)}), bf16[8192,2048]{1,0:T(8,128)(2,1)}) %all-gather.37.cloned.1.call-update) | async-done | bytes 33554448 | tf_op jit(solution)/shard_map/all_gather | solution.py:182
  2135.7 21.2 multiply_convert_fusion
  2157.0 17.3 fusion.124
  2174.3 18.5 multiply_reduce_fusion
  2195.3 7.3 convolution_convert_fusion.4
  2205.3 35.4 %while.41 = (s32[]{:T(128)}, f32[128,8,4,64]{0,3,2,1:T(8,128)S(1)}, bf16[2,512,8,64]{1,3,2,0:T(8,128)(2,1)}, bf16[2,512,8,64]{1,3,2,0:T(8,128)(2,1)}, bf16[2,512...) while((s32[]{:T(128)}, f32[128,8,4,64]{0,3,2,1:T(8,128)S(1)}, ...), condition=%wide.region_11.12_spmd.clone, body=%wide.region_10.11_spmd.clone.sunk | while | flops 1370030080 | bytes 125557568 | solution.py:264
  2215.1 5.0 fusion.206
  2232.6 5.0 fusion.206
  2258.3 26.1 reduce-scatter.7.cloned.1.call-done
  2285.5 38.6 %reduce-scatter.9.cloned.1.call-done = bf16[128,512]{1,0:T(8,128)(2,1)} async-done(((bf16[1024,512]{1,0:T(8,128)(2,1)}), bf16[128,512]{1,0:T(8,128)(2,1)}) %reduce-scatter.9.cloned.1.call-update) | async-done | bytes 131088
  2332.8 36.1 %all-gather.43.cloned.1.call-done = bf16[512,2048]{0,1:T(8,128)(2,1)} async-done(((bf16[128,2048]{0,1:T(8,128)(2,1)}), bf16[512,2048]{0,1:T(8,128)(2,1)}) %all-gather.43.cloned.1.call-update) | async-done | bytes 2097168 | tf_op jit(solution)/shard_map/all_gather | solution.py:305
  2368.8 48.6 %all-gather.45.cloned.1.call-done = bf16[512,2048]{1,0:T(8,128)(2,1)} async-done(((bf16[128,2048]{1,0:T(8,128)(2,1)}), bf16[512,2048]{1,0:T(8,128)(2,1)}) %all-gather.45.cloned.1.call-update) | async-done | bytes 2097168 | tf_op jit(solution)/shard_map/all_gather | solution.py:306
  2421.8 41.8 %all-gather.39.cloned.1.call-done = bf16[512,2048]{1,0:T(8,128)(2,1)} async-done(((bf16[128,2048]{1,0:T(8,128)(2,1)}), bf16[512,2048]{1,0:T(8,128)(2,1)}) %all-gather.39.cloned.1.call-update) | async-done | bytes 2097168 | tf_op jit(solution)/shard_map/all_gather | solution.py:307
  2463.6 62.7 %all-gather.41.cloned.1.call-done = bf16[512,3072]{0,1:T(8,128)(2,1)} async-done(((bf16[128,3072]{0,1:T(8,128)(2,1)}), bf16[512,3072]{0,1:T(8,128)(2,1)}) %all-gather.41.cloned.1.call-update) | async-done | bytes 3145744 | tf_op jit(solution)/shard_map/all_gather | solution.py:308
  2532.7 40.6 %all-gather.53.cloned.1.call-done = bf16[1,512,2048]{2,1,0:T(8,128)(2,1)} async-done(((bf16[1,128,2048]{2,1,0:T(8,128)(2,1)}), bf16[1,512,2048]{2,1,0:T(8,128)(2,1)}) %all-gather.53.cloned.1.call-update) | async-done | bytes 2097168 | tf_op jit(solution)/shard_map/all_gather | solution.py:216
  2573.3 149.4 %all-gather.51.cloned.1.call-done = bf16[512,8192]{1,0:T(8,128)(2,1)} async-done(((bf16[128,8192]{1,0:T(8,128)(2,1)}), bf16[512,8192]{1,0:T(8,128)(2,1)}) %all-gather.51.cloned.1.call-update) | async-done | bytes 8388624 | tf_op jit(solution)/shard_map/all_gather | solution.py:215
  2722.7 10.1 convolution_convert_fusion.1
  2732.7 36.0 %all-gather.47.cloned.1.call-done = bf16[512,2048]{1,0:T(8,128)(2,1)} async-done(((bf16[128,2048]{1,0:T(8,128)(2,1)}), bf16[512,2048]{1,0:T(8,128)(2,1)}) %all-gather.47.cloned.1.call-update) | async-done | bytes 2097168 | tf_op jit(solution)/shard_map/all_gather | solution.py:217
  2768.7 287.2 %all-gather.49.cloned.1.call-done = bf16[512,16384]{1,0:T(8,128)(2,1)} async-done(((bf16[128,16384]{1,0:T(8,128)(2,1)}), bf16[512,16384]{1,0:T(8,128)(2,1)}) %all-gather.49.cloned.1.call-update) | async-done | bytes 16777232 | tf_op jit(solution)/shard_map/all_gather | solution.py:218
  3056.0 16.0 convolution_convert_fusion
  3071.9 11.9 fusion.118
  3085.7 6.3 fusion.125
  3092.1 17.1 fusion.65
  3112.0 13.4 all-reduce.2
  3125.6 15.5 all-reduce.3
  3144.9 307.3 %all-reduce.7.cloned.1.call-done = (bf16[512,2048]{1,0:T(8,128)(2,1)}, bf16[512,512]{1,0:T(8,128)(2,1)}, bf16[512,512]{1,0:T(8,128)(2,1)}, bf16[512,2048]{1,0:T(...) async-done(((bf16[512,2048]{1,0:T(8,128)(2,1)}, bf16[512,512]{1,0:T(8,128)(2,1)}, bf16[512,512]{1,0:T(8,128)(2,1)}, ...) | async-done | bytes 30408720 | tf_op jit(solution)/shard_map/psum | solution.py:324
  3463.4 11.7 convert_element_type.198
  3475.1 11.7 convert_element_type.199
  3486.9 11.7 convert_element_type.201
  (231 shorter events, 137.5 us)
Async XLA Ops:
  7.2 97.3 %copy-start.5 = (bf16[1,128,2048]{2,1,0:T(8,128)(2,1)S(1)}, bf16[1,128,2048]{2,1,0:T(8,128)(2,1)}, u32[]{:S(2)}) copy-start(bf16[1,128,2048]{2,1,0:T(8,128)(2,1)} %param.18) | copy-start | bytes 1572868
  7.2 48.1 %all-gather.21.cloned.1.call-start = ((), (), s32[]{:S(2)}) async-start(), calls=%async_computation.2 | async-start | bytes 2621440 | tf_op jit(solution)/shard_map/all_gather | solution.py:116
  7.9 93.6 %all-gather.25.cloned.1.call-start = ((), (), s32[]{:S(2)}) async-start(), calls=%async_computation.4 | async-start | bytes 2621440 | tf_op jit(solution)/shard_map/all_gather | solution.py:115
  8.7 119.4 %all-gather.23.cloned.1.call-start = ((), (), s32[]{:S(2)}) async-start(), calls=%async_computation.3 | async-start | bytes 1179648 | tf_op jit(solution)/shard_map/all_gather | solution.py:133
  17.0 298.1 %copy-start.23 = (f32[4,1,512]{2,1,0:T(1,128)}, f32[4,1,512]{2,1,0:T(1,128)S(1)}, u32[]{:S(2)}) copy-start(f32[4,1,512]{2,1,0:T(1,128)S(1)} %convert_element_type.203) | copy-start | bytes 24580
  18.2 296.9 %copy-start.28 = (f32[128]{0:T(128)}, f32[128]{0:T(128)S(1)}, u32[]{:S(2)}) copy-start(f32[128]{0:T(128)S(1)} %add_rsqrt_fusion.1) | copy-start | bytes 1540
  19.5 82.0 %copy-start.13 = (bf16[128,2048]{1,0:T(8,128)(2,1)}, bf16[128,2048]{1,0:T(8,128)(2,1)S(1)}, u32[]{:S(2)}) copy-start(bf16[128,2048]{1,0:T(8,128)(2,1)S(1)} %fusion.74) | copy-start | bytes 1572868
  58.0 95.9 %all-gather.27.cloned.1.call-start = ((), (), s32[]{:S(2)}) async-start(), calls=%async_computation.5 | async-start | bytes 1179648 | tf_op jit(solution)/shard_map/all_gather | solution.py:132
  59.3 262.4 %copy-start.18 = (f32[128,64]{0,1:T(8,128)}, f32[128,64]{0,1:T(8,128)S(1)}, u32[]{:S(2)}) copy-start(f32[128,64]{0,1:T(8,128)S(1)} %pad_maximum_fusion.5) | copy-start | bytes 98308
  59.3 262.4 %copy-start.20 = (f32[128,64]{0,1:T(8,128)}, f32[128,64]{0,1:T(8,128)S(1)}, u32[]{:S(2)}) copy-start(f32[128,64]{0,1:T(8,128)S(1)} %pad_maximum_fusion.4) | copy-start | bytes 98308
  106.0 196.8 %all-gather.29.cloned.1.call-start = ((), (), s32[]{:S(2)}) async-start(), calls=%async_computation.6 | async-start | bytes 10485760 | tf_op jit(solution)/shard_map/all_gather | solution.py:114
  106.6 345.5 %all-gather.31.cloned.1.call-start = ((), (), s32[]{:S(2)}) async-start(), calls=%async_computation.7 | async-start | bytes 10485760 | tf_op jit(solution)/shard_map/all_gather | solution.py:117
  107.2 906.2 %all-gather.33.cloned.1.call-start = ((), (), s32[]{:S(2)}) async-start(), calls=%async_computation.8 | async-start | bytes 41943040 | tf_op jit(solution)/shard_map/all_gather | solution.py:180
  107.9 1466.6 %all-gather.35.cloned.1.call-start = ((), (), s32[]{:S(2)}) async-start(), calls=%async_computation.9 | async-start | bytes 41943040 | tf_op jit(solution)/shard_map/all_gather | solution.py:181
  108.7 2027.0 %all-gather.37.cloned.1.call-start = ((), (), s32[]{:S(2)}) async-start(), calls=%async_computation.10 | async-start | bytes 41943040 | tf_op jit(solution)/shard_map/all_gather | solution.py:182
  109.4 2174.9 %reduce-scatter.7.cloned.1.call-start = ((), (), s32[]{:S(2)}) async-start(), calls=%async_computation.19 | async-start | bytes 1179648
  119.0 2073.9 %copy-start.25 = (f32[4,1,512]{2,1,0:T(1,128)}, f32[4,1,512]{2,1,0:T(1,128)S(1)}, u32[]{:S(2)}) copy-start(f32[4,1,512]{2,1,0:T(1,128)S(1)} %convert_element_type.204) | copy-start | bytes 24580
  457.1 1735.8 %copy-start.30 = (f32[128]{0:T(128)}, f32[128]{0:T(128)S(1)}, u32[]{:S(2)}) copy-start(f32[128]{0:T(128)S(1)} %add_rsqrt_fusion) | copy-start | bytes 1540
  458.2 1116.3 %copy-start.8 = (bf16[128,2048]{1,0:T(8,128)(2,1)}, bf16[128,2048]{1,0:T(8,128)(2,1)S(1)}, u32[]{:S(2)}) copy-start(bf16[128,2048]{1,0:T(8,128)(2,1)S(1)} %multiply_convert_fusion.3) | copy-start | bytes 1572868
  2157.0 17.4 copy-start.3
  2174.3 18.6 copy-start.11
  2192.9 12.4 copy-start.32
  2229.3 8.3 copy-start.1
  2229.3 8.3 copy-start.16
  2240.7 17.1 copy-start.19
  2248.2 9.9 copy-start.21
  2248.2 75.9 %reduce-scatter.9.cloned.1.call-start = ((), (), s32[]{:S(2)}) async-start(), calls=%async_computation.20 | async-start | bytes 1179648
  2255.8 113.0 %all-gather.43.cloned.1.call-start = ((), (), s32[]{:S(2)}) async-start(), calls=%async_computation.13 | async-start | bytes 2621440 | tf_op jit(solution)/shard_map/all_gather | solution.py:305
  2256.4 161.0 %all-gather.45.cloned.1.call-start = ((), (), s32[]{:S(2)}) async-start(), calls=%async_computation.14 | async-start | bytes 2621440 | tf_op jit(solution)/shard_map/all_gather | solution.py:306
  2257.2 206.4 %all-gather.39.cloned.1.call-start = ((), (), s32[]{:S(2)}) async-start(), calls=%async_computation.11 | async-start | bytes 2621440 | tf_op jit(solution)/shard_map/all_gather | solution.py:307
  2257.7 268.5 %all-gather.41.cloned.1.call-start = ((), (), s32[]{:S(2)}) async-start(), calls=%async_computation.12 | async-start | bytes 3932160 | tf_op jit(solution)/shard_map/all_gather | solution.py:308
  2326.1 247.2 %all-gather.53.cloned.1.call-start = ((), (), s32[]{:S(2)}) async-start(), calls=%async_computation.18 | async-start | bytes 2621440 | tf_op jit(solution)/shard_map/all_gather | solution.py:216
  2326.7 396.0 %all-gather.51.cloned.1.call-start = ((), (), s32[]{:S(2)}) async-start(), calls=%async_computation.17 | async-start | bytes 10485760 | tf_op jit(solution)/shard_map/all_gather | solution.py:215
  2327.3 441.5 %all-gather.47.cloned.1.call-start = ((), (), s32[]{:S(2)}) async-start(), calls=%async_computation.15 | async-start | bytes 2621440 | tf_op jit(solution)/shard_map/all_gather | solution.py:217
  2327.8 728.1 %all-gather.49.cloned.1.call-start = ((), (), s32[]{:S(2)}) async-start(), calls=%async_computation.16 | async-start | bytes 20971520 | tf_op jit(solution)/shard_map/all_gather | solution.py:218
  2332.5 1119.7 %all-reduce.7.cloned.1.call-start = ((), (), s32[]{:S(2)}) async-start(), calls=%async_computation.21 | async-start | bytes 60817408 | tf_op jit(solution)/shard_map/psum | solution.py:324
  3092.0 17.2 copy-start.10
  3092.1 18.1 copy-start.6
  3092.1 18.1 copy-start.9
  3092.1 18.1 copy-start.22
  3092.1 18.1 copy-start.24
  3092.1 18.1 copy-start.29
  3109.2 33.0 copy-start.7
  3109.2 33.0 copy-start.12
  3109.2 33.0 copy-start.26
  3109.3 33.0 copy-start.31
  3109.3 33.0 copy-start.33
  3452.2 8.6 copy-start.14
  (13 other events, 45.5 us)
Sparse Core Ops, SparseCore 0:
  9.6 45.6 all-gather.20
  56.8 44.6 all-gather.24
  104.0 23.9 all-gather.22
  130.3 23.5 all-gather.26
  155.3 147.3 all-gather.28
  304.2 147.8 all-gather.30
  453.7 559.6 all-gather.32
  1014.9 559.5 all-gather.34
  1576.1 559.5 all-gather.36
  2248.4 35.9 reduce-scatter.6
  2288.1 35.9 reduce-scatter.8
  2326.1 42.6 all-gather.42
  2371.0 46.4 all-gather.44
  2418.9 44.6 all-gather.38
  2465.6 60.6 all-gather.40
  2527.7 45.5 all-gather.52
  2574.7 147.8 all-gather.50
  2724.1 44.5 all-gather.46
  2770.9 285.0 all-gather.48
  3084.0 368.2 all-reduce.6
where the time goes:
time: 3510 us
  waiting for transfers between devices  3070 us (87%)
  matrix products  229 us (7%)
  other arithmetic  76.9 us (2%)
  local copies, waits for them, and re-layouts  64.7 us (2%)
  blocking collectives  45.8 us (1%)
    all_gather x1, waiting for transfers between devices, on_device(): lax.all_gather(w_gate, 'fsdp', axis=0, tiled=True)  555 us
    all_gather x1, waiting for transfers between devices, on_device(): lax.all_gather(w_down, 'fsdp', axis=0, tiled=True)  542 us
    all_gather x1, waiting for transfers between devices, on_device(): lax.all_gather(w_up, 'fsdp', axis=0, tiled=True)  542 us
    psum x1, waiting for transfers between devices, on_device(): lax.psum(grad_query.astype(jnp.bfloat16), 'ctx').astype(jnp.float32)  307 us
    all_gather x1, waiting for transfers between devices, on_device(): lax.all_gather(gate_up_pair, 'fsdp', axis=0, tiled=True)  287 us
    all_gather x1, waiting for transfers between devices, on_device(): lax.all_gather(hidden, 'fsdp', axis=0, tiled=True)  149 us
    all_gather x1, waiting for transfers between devices, on_device(): lax.all_gather(w_query, 'fsdp', axis=0, tiled=True)  145 us
    all_gather x1, waiting for transfers between devices, on_device(): lax.all_gather(w_out, 'fsdp', axis=0, tiled=True)  98.9 us
  transfers between devices with their start and end apart: 20, of which 20 were waited for; matrix products, arithmetic and copies ran while one was open for 5% of the time, Pallas kernels for 0%

commit v1 on v0

v1 whole, which is shorter than its diff:
```python
import math

import jax
import jax.numpy as jnp
from jax import lax
from jax.sharding import PartitionSpec as P

HEAD_DIM = 64


EPS = 1e-05
THETA = 500000.0


def frequencies(head_width):
    evens = jnp.arange(0, head_width, 2, dtype=jnp.float32)
    inverse = 1.0 / THETA ** (evens / head_width)
    wavelen = 2.0 * math.pi / inverse
    smooth = (8192.0 / wavelen - 1.0) / 3.0
    middle = (1.0 - smooth) * inverse / 32.0 + smooth * inverse
    return jnp.where(wavelen < 2048.0, inverse, jnp.where(wavelen > 8192.0, inverse / 32.0, middle))


def rotation(positions, head_width):
    angles = positions.astype(jnp.float32)[:, None] * frequencies(head_width)[None, :]
    cosine = jnp.concatenate([jnp.cos(angles), jnp.cos(angles)], axis=1)[:, None, :]
    sine = jnp.concatenate([jnp.sin(angles), jnp.sin(angles)], axis=1)[:, None, :]
    return (cosine, sine)


def rotate(tensor, cosine, sine):
    middle = tensor.shape[-1] // 2
    turned = jnp.concatenate([-tensor[..., middle:], tensor[..., :middle]], axis=-1)
    return tensor * cosine + turned * sine


def unrotate(gradient, cosine, sine):
    middle = gradient.shape[-1] // 2
    moved = gradient * sine
    back_turn = jnp.concatenate([moved[..., middle:], -moved[..., :middle]], axis=-1)
    return gradient * cosine + back_turn


def slot_positions(pairing, seq_length, block_len):
    flattened = pairing.reshape(-1)
    slots = jnp.arange(seq_length, dtype=jnp.int32)
    owning = slots // block_len
    labels = jnp.arange(flattened.shape[0], dtype=jnp.int32)
    anchor = jnp.sum(jnp.where(owning[:, None] == labels[None, :], flattened[None, :], 0), axis=1)
    return anchor * block_len + slots % block_len


def product(left, right):
    return jnp.dot(left, right, preferred_element_type=jnp.float32)


def product_t(left, right):
    return lax.dot_general(
        left, right, (((1,), (1,)), ((), ())), preferred_element_type=jnp.float32
    )


def tokens_t(left, right):
    return lax.dot_general(
        left, right, (((0,), (0,)), ((), ())), preferred_element_type=jnp.float32
    )


def norm_back(upstream, gain, unit, scale):
    weighted = upstream * gain
    return scale * (weighted - unit * jnp.mean(weighted * unit, axis=1, keepdims=True))


def gather(array, axis):
    return lax.all_gather(array, axis, axis=0, tiled=True)


def scatter_sum(array, axis):
    return lax.psum_scatter(array, axis, scatter_dimension=0, tiled=True)


def einsum(spec, left, right):
    return jnp.einsum(spec, left, right, preferred_element_type=jnp.float32)


def exchange(pieces, axis):
    count = pieces.shape[0]
    me = lax.axis_index(axis)
    parts = [pieces[0]] * count
    own = lax.dynamic_index_in_dim(pieces, me, 0, keepdims=True)
    received = [own]
    for shift in range(1, count):
        target = lax.rem(me + shift, count)
        piece = lax.dynamic_index_in_dim(pieces, target, 0, keepdims=True)
        received.append(lax.ppermute(piece, axis, [(i, (i + shift) % count) for i in range(count)]))
    out = jnp.zeros_like(pieces)
    for shift, piece in enumerate(received):
        source = lax.rem(me + count - shift, count)
        out = lax.dynamic_update_slice_in_dim(out, piece, source, 0)
    return out


def on_device(
    tokens,
    cotangent,
    pairing,
    norm_attn,
    w_query,
    w_key,
    w_value,
    w_out,
    norm_mlp,
    w_gate,
    w_up,
    w_down,
):
    n_ctx, n_fsdp = lax.axis_size("ctx"), lax.axis_size("fsdp")
    ctx = lax.axis_index("ctx")
    own_tokens = tokens[0]
    tok_rows, width = own_tokens.shape
    length = tok_rows * n_ctx
    rows_model = w_gate.shape[0]
    low = jnp.bfloat16

    query_width = w_query.shape[1] // n_ctx
    heads_kv = w_key.shape[1] // HEAD_DIM
    kv_here = max(1, heads_kv // n_ctx)
    sharers = max(1, n_ctx // heads_kv)
    kv_width = kv_here * HEAD_DIM
    group = query_width // kv_width
    kv_start = (ctx // sharers) * kv_width

    def columns(matrix, start, size):
        return lax.dynamic_slice_in_dim(matrix, start, size, 1)

    joined = jnp.concatenate(
        [
            columns(w_query, ctx * query_width, query_width),
            columns(w_key, kv_start, kv_width),
            columns(w_value, kv_start, kv_width),
        ],
        axis=1,
    )
    w_joined = gather(joined, "fsdp")
    sequence = gather(own_tokens, "ctx")
    gains = lax.all_gather(jnp.stack([norm_attn, norm_mlp]), "fsdp", axis=1, tiled=True)
    gain_attn, gain_mlp = gains[0], gains[1]
    out_width = width // n_ctx
    w_out_cols = gather(columns(w_out, ctx * out_width, out_width), "fsdp")
    w_out_rows = lax.all_to_all(w_out_cols, "ctx", 0, 1, tiled=True)

    ff_rows = w_down.shape[0]
    chunk = ff_rows // n_ctx
    pieces = jnp.stack(
        [w.reshape(rows_model, n_fsdp, n_ctx, chunk) for w in (w_gate, w_up)], axis=0
    )
    pieces = lax.dynamic_index_in_dim(pieces, ctx, 3, keepdims=False)
    pieces = exchange(pieces.transpose(2, 0, 1, 3), "fsdp")
    pieces = pieces.transpose(1, 0, 2, 3).reshape(1, 2, width, chunk)
    w_pair = gather(pieces, "ctx")
    down_cut = w_down.reshape(n_ctx, chunk, width)
    upstream = cotangent[0]
    upstream_all = gather(upstream, "fsdp")

    all_pos = slot_positions(pairing, length, tok_rows // 2)
    cosine, sine = rotation(all_pos, HEAD_DIM)
    factor = HEAD_DIM ** (-0.5)
    wide = sequence.astype(jnp.float32)
    scale_attn = lax.rsqrt(jnp.mean(wide * wide, axis=1, keepdims=True) + EPS)
    normed_attn = (wide * scale_attn * gain_attn).astype(low)
    projected = product(normed_attn, w_joined)
    query_pre = projected[:, :query_width].reshape(length, -1, HEAD_DIM)
    key_pre = projected[:, query_width : query_width + kv_width].reshape(length, -1, HEAD_DIM)
    values = projected[:, query_width + kv_width :].reshape(length, -1, HEAD_DIM).astype(low)
    queries = rotate(query_pre, cosine, sine).astype(low).reshape(length, kv_here, group, HEAD_DIM)
    keys = rotate(key_pre, cosine, sine).astype(low)
    logits = einsum("qhgd,khd->hgqk", queries, keys)
    allowed = all_pos[None, :] <= all_pos[:, None]
    scores = jnp.where(allowed, logits * factor, -1e30)
    largest = jnp.max(scores, axis=-1, keepdims=True)
    expo = jnp.where(allowed, jnp.exp(scores - largest), 0.0)
    probs = expo / jnp.sum(expo, axis=-1, keepdims=True)
    probs_low = probs.astype(low)
    attended = einsum("hgqk,khd->qhgd", probs_low, values)
    attended_low = attended.reshape(length, query_width).astype(low)
    projected_out = scatter_sum(product(attended_low, w_out_rows).astype(low), "ctx")
    inputs = own_tokens.astype(jnp.float32)
    resid = inputs + projected_out.astype(jnp.float32)

    scale_mlp = lax.rsqrt(jnp.mean(resid * resid, axis=1, keepdims=True) + EPS)
    unit_mlp = resid * scale_mlp
    normed_mlp = gather((unit_mlp * gain_mlp).astype(low), "fsdp")
    both = einsum("td,cgdf->gctf", normed_mlp, w_pair)
    gate_pre, up_pre = both[0], both[1]
    sigma = jax.nn.sigmoid(gate_pre)
    swish = gate_pre * sigma
    hidden = (swish * up_pre).astype(low)
    d_hidden = einsum("td,cfd->ctf", upstream_all, down_cut)
    d_gate = (d_hidden * up_pre * sigma * (1.0 + gate_pre * (1.0 - sigma))).astype(low)
    d_up = (d_hidden * swish).astype(low)
    d_pair = jnp.stack([d_gate, d_up])
    d_normed_part = einsum("gctf,cgdf->td", d_pair, w_pair).astype(low)
    d_normed_mlp = scatter_sum(d_normed_part, "fsdp").astype(jnp.float32)
    down_part = einsum("ctf,cfd->td", hidden, down_cut).astype(low)
    output = resid + scatter_sum(down_part, "fsdp").astype(jnp.float32)
    grad_down = lax.psum(einsum("ctf,td->cfd", hidden, upstream_all).astype(low), "ctx")
    grad_pair = einsum("td,gctf->cgdf", normed_mlp, d_pair).astype(low)
    grad_pair = scatter_sum(grad_pair, "ctx").reshape(2, n_fsdp, rows_model, chunk)
    grad_pair = exchange(grad_pair.transpose(1, 0, 2, 3), "fsdp")
    grad_pair = lax.all_gather(grad_pair, "ctx", axis=0)
    grad_pair = grad_pair.transpose(2, 3, 1, 0, 4).reshape(2, rows_model, -1).astype(jnp.float32)

    gain_mlp_term = jnp.sum(d_normed_mlp * unit_mlp, axis=0)
    d_resid = upstream.astype(jnp.float32) + norm_back(d_normed_mlp, gain_mlp, unit_mlp, scale_mlp)
    d_resid_low = gather(d_resid.astype(low), "ctx")

    d_attended = product_t(d_resid_low, w_out_rows).astype(low)
    d_attended = d_attended.reshape(length, kv_here, group, HEAD_DIM)
    d_probs = einsum("qhgd,khd->hgqk", d_attended, values)
    delta = jnp.sum(probs * d_probs, axis=-1, keepdims=True)
    d_score = (probs * (d_probs - delta) * factor).astype(low)
    d_query_rot = einsum("hgqk,khd->qhgd", d_score, keys)
    d_key_rot = einsum("hgqk,qhgd->khd", d_score, queries)
    d_value = einsum("hgqk,qhgd->khd", probs_low, d_attended)
    d_query = unrotate(d_query_rot.reshape(length, -1, HEAD_DIM), cosine, sine)
    d_key = unrotate(d_key_rot, cosine, sine)
    d_joined = jnp.concatenate(
        [part.reshape(length, -1).astype(low) for part in (d_query, d_key, d_value)], axis=1
    )
    d_normed_part = product_t(d_joined, w_joined).astype(low)
    d_normed_attn = scatter_sum(d_normed_part, "ctx").astype(jnp.float32)
    grad_out = tokens_t(attended_low, d_resid_low).astype(low)
    grad_out = lax.all_to_all(grad_out, "ctx", 1, 0, tiled=True)
    grad_joined = tokens_t(normed_attn, d_joined).astype(low)
    grad_attn = scatter_sum(jnp.concatenate([grad_joined, grad_out], axis=1), "fsdp")
    grad_attn = lax.all_gather(grad_attn, "ctx", axis=0).astype(jnp.float32)

    def spread(part):
        return part.transpose(1, 0, 2).reshape(part.shape[1], -1)

    def shared(part):
        return jnp.sum(part.reshape(n_ctx // sharers, sharers, *part.shape[1:]), axis=1)

    at = query_width
    grad_query = spread(grad_attn[:, :, :at])
    grad_key = spread(shared(grad_attn[:, :, at : at + kv_width]))
    grad_value = spread(shared(grad_attn[:, :, at + kv_width : at + 2 * kv_width]))
    grad_out = spread(grad_attn[:, :, at + 2 * kv_width :])

    unit_attn = inputs * lax.rsqrt(jnp.mean(inputs * inputs, axis=1, keepdims=True) + EPS)
    scale_own = lax.rsqrt(jnp.mean(inputs * inputs, axis=1, keepdims=True) + EPS)
    gain_attn_term = jnp.sum(d_normed_attn * unit_attn, axis=0)
    d_inputs = d_resid + norm_back(d_normed_attn, gain_attn, unit_attn, scale_own)
    terms = lax.psum(jnp.stack([gain_attn_term, gain_mlp_term]), ("ctx", "fsdp"))
    terms = lax.dynamic_slice_in_dim(terms, lax.axis_index("fsdp") * rows_model, rows_model, 1)
    return (
        output.astype(low)[None],
        d_inputs.astype(low)[None],
        terms[0],
        grad_query,
        grad_key,
        grad_value,
        grad_out,
        terms[1],
        grad_pair[0],
        grad_pair[1],
        grad_down.reshape(ff_rows, width).astype(jnp.float32),
    )


def solution(mesh):
    return jax.shard_map(
        on_device,
        mesh=mesh,
        in_specs=(
            P("fsdp", "ctx", None),
            P("fsdp", "ctx", None),
            P(),
            P("fsdp"),
            P("fsdp", None),
            P("fsdp", None),
            P("fsdp", None),
            P("fsdp", None),
            P("fsdp"),
            P("fsdp", None),
            P("fsdp", None),
            P("fsdp", None),
        ),
        out_specs=(
            P("fsdp", "ctx", None),
            P("fsdp", "ctx", None),
            P("fsdp"),
            P("fsdp", None),
            P("fsdp", None),
            P("fsdp", None),
            P("fsdp", None),
            P("fsdp"),
            P("fsdp", None),
            P("fsdp", None),
            P("fsdp", None),
        ),
        check_vma=False,
    )
```

time: 3510 us -> 1330 us (0.38)
  waiting for transfers between devices: 3070 us -> 826 us
  local copies, waits for them, and re-layouts: 64.7 us -> 197 us
  matrix products: 229 us -> 135 us
    all_gather x17 -> x9, waiting for transfers between devices: 2690 us -> 296 us  [the longest x7 232 us: gather(): return lax.all_gather(array, axis, axis=0, tiled=True)]
    psum x1 -> x0, waiting for transfers between devices: 307 us -> none  [on_device(): lax.psum(grad_query.astype(jnp.bfloat16), 'ctx').astype(jnp.float32)]
    unnamed x22 -> x16, waiting for transfers between devices: 72.6 us -> 313 us
    reduce_scatter x0 -> x5, waiting for transfers between devices: none -> 105 us  [scatter_sum(): return lax.psum_scatter(array, axis, scatter_dimension=0, tiled=True)]
    ppermute x0 -> x6, waiting for transfers between devices: none -> 89.1 us  [exchange(): lax.ppermute(piece, axis, [(i, (i + shift) % count) for i in range(count)])]
    unnamed x76 -> x128, local copies, waits for them, and re-layouts: 25 us -> 110 us
    dot_general x7 -> x2, matrix products: 73.4 us -> 8.33 us  [product_t(): lax.dot_general(left, right, (((1,), (1,)), ((), ())), preferred_element_...]
    dot_general x14 -> x12, matrix products: 51.7 us -> 113 us  [einsum(): return jnp.einsum(spec, left, right, preferred_element_type=jnp.float32)]
  transfers between devices with their start and end apart: 20 -> 23, of which waited for: 20 -> 20; matrix products, arithmetic and copies ran while one was open for 5% -> 15% of each run, Pallas kernels for 0% -> 0%
where the time goes in v1:
time: 1330 us; the launch traced here: 1320 us
  waiting for transfers between devices  826 us (62%)
  local copies, waits for them, and re-layouts  197 us (15%)
  matrix products  135 us (10%)
  other arithmetic  77.2 us (6%)
  blocking collectives  51.6 us (4%)
  between operations  15.3 us (1%)
  starting transfers between devices  14.7 us (1%)
    unnamed x16, waiting for transfers between devices  313 us
    all_gather x7, waiting for transfers between devices, gather(): return lax.all_gather(array, axis, axis=0, tiled=True)  232 us
    dot_general x12, matrix products, einsum(): return jnp.einsum(spec, left, right, preferred_element_type=jnp.float32)  113 us
    unnamed x128, local copies, waits for them, and re-layouts  110 us
    reduce_scatter x5, waiting for transfers between devices, scatter_sum(): return lax.psum_scatter(array, axis, scatter_dimension=0, tiled=True)  105 us
    ppermute x6, waiting for transfers between devices, exchange(): lax.ppermute(piece, axis, [(i, (i + shift) % count) for i in range(count)])  89.1 us
    psum x1, blocking collectives, on_device(): lax.psum(jnp.stack([gain_attn_term, gain_mlp_term]), ('ctx', 'fsdp'))  42.8 us
    all_gather x1, waiting for transfers between devices, on_device(): grad_attn = lax.all_gather(grad_attn, 'ctx', axis=0).astype(jnp.float32)  32.3 us
  transfers between devices with their start and end apart: 23, of which 20 were waited for; matrix products, arithmetic and copies ran while one was open for 15% of the time, Pallas kernels for 0%

profile of v1, /device:TPU:17, one launch (start us, length us, event | category | flops | bytes accessed | tf_op | source)
XLA Modules:
  0.0 1317.0 jit_solution(15779058006814760388)
XLA Ops:
  14.9 8.8 all_gather.45
  23.8 15.1 %all-gather.15.cloned.1.call-done = bf16[2048,256]{1,0:T(8,128)(2,1)} async-done(((bf16[512,256]{1,0:T(8,128)(2,1)}), bf16[2048,256]{1,0:T(8,128)(2,1)}) %all-gather.15.cloned.1.call-update) | async-done | bytes 1048592 | tf_op jit(solution)/shard_map/all_gather | solution.py:75
  44.5 16.2 %all-to-all-done = bf16[8,256,256]{2,1,0:T(8,128)(2,1)S(1)} async-done(((bf16[8,256,256]{2,1,0:T(8,128)(2,1)}), bf16[8,256,256]{2,1,0:T(8,128)(2,1)S(1)}, u32[]{:S(2)}, u32[]{:S(2)}) %all-to-all-start) | async-done | bytes 1048608 | tf_op jit(solution)/shard_map/all_to_all | solution.py:150
  61.2 21.6 %all-gather.25.cloned.1.call-done = bf16[1,1024,2048]{2,1,0:T(8,128)(2,1)} async-done(((bf16[1,128,2048]{2,1,0:T(8,128)(2,1)}), bf16[1,1024,2048]{2,1,0:T(8,128)(2,1)}) %all-gather.25.cloned.1.call-update) | async-done | bytes 4194320 | tf_op jit(solution)/shard_map/all_gather | solution.py:75
  85.9 34.6 %all-gather.13.cloned.1.call-done = bf16[2048,384]{1,0:T(8,128)(2,1)} async-done(((bf16[512,384]{1,0:T(8,128)(2,1)}), bf16[2048,384]{1,0:T(8,128)(2,1)}) %all-gather.13.cloned.1.call-update) | async-done | bytes 1572880 | tf_op jit(solution)/shard_map/all_gather | solution.py:75
  137.0 5.6 fusion.47
  147.0 51.2 %reduce-scatter.9.cloned.1.call-done = bf16[128,2048]{1,0:T(8,128)(2,1)} async-done(((bf16[1024,2048]{1,0:T(8,128)(2,1)}), bf16[128,2048]{1,0:T(8,128)(2,1)}) %reduce-scatter.9.cloned.1.call-update) | async-done | bytes 524304 | tf_op jit(solution)/shard_map/reduce_scatter | solution.py:79
  201.7 12.0 copy.172
  213.7 11.9 copy.173
  236.5 20.0 %collective-permute-done = bf16[1,2,512,256]{3,2,1,0:T(8,128)(2,1)} collective-permute-done((bf16[1,2,512,256]{3,2,1,0:T(8,128)(2,1)}, bf16[1,2,512,256]{3,2,1,0:T(8,128)(2,1)}, u32[]{:S(2)}, u32[]{:S(2)}) %collective-permute-start) | collective-permute-done | bytes 524320 | tf_op jit(solution)/shard_map/ppermute | solution.py:95
  258.4 19.8 %collective-permute-done.1 = bf16[1,2,512,256]{3,2,1,0:T(8,128)(2,1)} collective-permute-done((bf16[1,2,512,256]{3,2,1,0:T(8,128)(2,1)}, bf16[1,2,512,256]{3,2,1,0:T(8,128)(2,1)}, u32[]{:S(2)}, u32[]{:S(2)}) %collective-permute-start.1) | collective-permute-done | bytes 524320 | tf_op jit(solution)/shard_map/ppermute | solution.py:95
  280.1 9.3 collective-permute-done.2
  292.1 93.1 %all-gather.17.cloned.1.call-done = bf16[8,2,2048,256]{3,2,1,0:T(8,128)(2,1)} async-done(((bf16[1,2,2048,256]{3,2,1,0:T(8,128)(2,1)}), bf16[8,2,2048,256]{3,2,1,0:T(8,128)(2,1)}) %all-gather.17.cloned.1.call-update) | async-done | bytes 16777232 | tf_op jit(solution)/shard_map/all_gather | solution.py:75
  385.2 15.3 %convolution_bitcast_fusion = f32[2,8,512,256]{2,3,0,1:T(8,128)} fusion(bf16[8,2,2048,256]{3,2,1,0:T(8,128)(2,1)} %all-gather.17.cloned.1.call-done, bf16[512,2048]{1,0:T(8,128)(2,1)} %all-gather.19.cloned.1.call-done), kind=kOutput, calls=%fused_computation.64 | convolution fusion | flops 8589934592 | bytes 27262976 | tf_op jit(solution)/shard_map/td,cgdf->gctf/dot_general | solution.py:83
  400.5 30.6 %all-gather.27.cloned.1.call-done = bf16[1,512,2048]{2,1,0:T(8,128)(2,1)} async-done(((bf16[1,128,2048]{2,1,0:T(8,128)(2,1)}), bf16[1,512,2048]{2,1,0:T(8,128)(2,1)}) %all-gather.27.cloned.1.call-update) | async-done | bytes 2097168 | tf_op jit(solution)/shard_map/all_gather | solution.py:75
  431.0 12.6 fusion.43
  445.7 13.9 %bitcast_convert_fusion = bf16[512,2048]{1,0:T(8,128)(2,1)} fusion(bf16[8,2,2048,256]{3,2,1,0:T(8,128)(2,1)} %all-gather.17.cloned.1.call-done, bf16[1,8,512,256]{2,3,1,0:T(8,128)(2,1)S(1)} %get-tuple-element.80, bf16[1,8,512,256]{2,3,1,0:T(8,128)(2,1)S(1)} %get-tuple-element.79), kind=kOutput, calls=%fused_computation.51 | convolution fusion | flops 8593080320 | bytes 23068672 | tf_op jit(solution)/shard_map/gctf,cgdf->td/dot_general | solution.py:83
  459.6 43.4 %reduce-scatter.13.cloned.1.call-done = bf16[128,2048]{1,0:T(8,128)(2,1)} async-done(((bf16[512,2048]{1,0:T(8,128)(2,1)}), bf16[128,2048]{1,0:T(8,128)(2,1)}) %reduce-scatter.13.cloned.1.call-update) | async-done | bytes 524304 | tf_op jit(solution)/shard_map/reduce_scatter | solution.py:79
  507.6 37.2 %all-gather.21.cloned.1.call-done = bf16[1024,2048]{1,0:T(8,128)(2,1)} async-done(((bf16[128,2048]{1,0:T(8,128)(2,1)}), bf16[1024,2048]{1,0:T(8,128)(2,1)}) %all-gather.21.cloned.1.call-update) | async-done | bytes 4194320 | tf_op jit(solution)/shard_map/all_gather | solution.py:75
  548.8 10.0 fusion.62
  558.8 9.7 fusion
  568.5 9.4 fusion.10
  577.9 4.8 bitcast_multiply_fusion.11
  599.2 6.1 all-to-all-done.1
  608.7 12.3 convolution_convert_fusion
  621.0 12.5 convert_bitcast_fusion.1
  639.6 12.1 bitcast_convert_fusion.1
  651.8 10.8 reduce-scatter.17.cloned.1.call-done
  663.3 311.6 %all-reduce.4.cloned.1.call-done = (bf16[8,2,2048,256]{2,3,0,1:T(8,128)(2,1)}, bf16[2048,2048]{1,0:T(8,128)(2,1)}) async-done(((bf16[8,2,2048,256]{2,3,0,1:T(8,128)(2,1)}, bf16[2048,2048]{1,0:T(8,128)(2,1)}), (bf16[8,2,2048,256]{2,3,0,1:T(8,128)(2,1)}, bf16[2048,2048]{1,0:T(8,128)(2,1)})) %all-reduce.4.cloned.1.call-update) | async-done | bytes 25165840
  986.6 7.8 collective-permute-done.3
  995.3 21.8 %collective-permute-done.4 = bf16[1,2,512,256]{3,2,1,0:T(8,128)(2,1)S(1)} collective-permute-done((bf16[1,2,512,256]{3,2,1,0:T(8,128)(2,1)S(1)}, bf16[1,2,512,256]{3,2,1,0:T(8,128)(2,1)S(1)}, u32[]{:S(2)}, u32[]{:S(2)}) %collective-permute-start.4) | collective-permute-done | bytes 524320 | tf_op jit(solution)/shard_map/ppermute | solution.py:95
  1017.9 10.4 collective-permute-done.5
  1029.2 11.9 convert_element_type.211
  1042.6 42.8 %psum.14 = f32[2,2048]{1,0:T(2,128)S(1)} all-reduce(f32[2,2048]{1,0:T(2,128)S(1)} %pad_maximum_fusion.9), channel_id=1, replica_groups=mesh['ctx'=8,'fsdp'=4] {'ctx','fsdp'}, use_global_device_ids=true, to_apply=%region_15.16 | all-reduce | flops 4096 | bytes 32768 | tf_op jit(solution)/shard_map/psum | solution.py:254
  1089.2 32.3 %all-gather.29.cloned.1.call-done = bf16[4096,640]{0,1:T(8,128)(2,1)} async-done(((bf16[512,640]{0,1:T(8,128)(2,1)}), bf16[4096,640]{0,1:T(8,128)(2,1)}) %all-gather.29.cloned.1.call-update) | async-done | bytes 5242896 | tf_op jit(solution)/shard_map/all_gather | solution.py:236
  1121.6 8.0 convert_element_type.216
  1129.5 15.9 %copy.221 = f32[80,8,8,512]{3,2,1,0:T(8,128)S(1)} copy(f32[80,8,8,512]{3,1,2,0:T(8,128)} %bitcast.370) | data formatting | bytes 20971520
  1145.5 4.7 slice_bitcast_fusion
  1152.1 5.5 copy.195
  1157.6 6.2 copy.223
  1169.9 5.6 copy.192
  1175.5 6.2 copy.222
  1181.7 31.7 %all-gather.23.cloned.1.call-done = bf16[8,4,2,512,256]{4,3,2,1,0:T(8,128)(2,1)} async-done(((bf16[1,4,2,512,256]{4,3,2,1,0:T(8,128)(2,1)}), bf16[8,4,2,512,256]{4,3,2,1,0:T(8,128)(2,1)}) %all-gather.23.cloned.1.call-update) | async-done | bytes 16777232 | tf_op jit(solution)/shard_map/all_gather | solution.py:210
  1213.3 21.6 %copy.197 = bf16[8,4,2,512,256]{3,4,0,1,2:T(8,128)(2,1)} copy(bf16[8,4,2,512,256]{4,3,2,1,0:T(8,128)(2,1)} %all-gather.23.cloned.1.call-done) | data formatting | bytes 33554432 | tf_op jit(solution)/shard_map/all_gather | solution.py:210
  1235.0 18.8 %convert_bitcast_fusion = f32[2,512,4,8,256]{1,4,3,2,0:T(8,128)} fusion(bf16[8,4,2,512,256]{3,4,0,1,2:T(8,128)(2,1)} %copy.197), kind=kLoop, calls=%fused_computation | loop fusion | flops 8388608 | bytes 50331648 | tf_op jit(solution)/shard_map/convert_element_type | solution.py:211
  1253.8 21.3 %fusion.114 = (f32[1,512,4,8,256]{1,4,3,2,0:T(8,128)}, f32[1,512,4,8,256]{1,4,3,2,0:T(8,128)}) fusion(f32[2,512,4,8,256]{1,4,3,2,0:T(8,128)} %convert_bitcast_fusion), kind=kLoop, calls=%fused_computation.199 | loop fusion | bytes 67108864 | tf_op jit(solution)/shard_map/slice | solution.py:266
  1275.1 17.4 %copy.201 = f32[512,8192]{1,0:T(8,128)} copy(f32[512,8192]{0,1:T(8,128)} %bitcast.367) | data formatting | bytes 33554432
  1292.5 17.6 %copy.200 = f32[512,8192]{1,0:T(8,128)} copy(f32[512,8192]{0,1:T(8,128)} %bitcast.366) | data formatting | bytes 33554432
  (233 shorter events, 122.9 us)
Async XLA Ops:
  7.2 31.7 %all-gather.15.cloned.1.call-start = ((), (), s32[]{:S(2)}) async-start(), calls=%async_computation.8 | async-start | bytes 1310720 | tf_op jit(solution)/shard_map/all_gather | solution.py:75
  9.5 73.3 %all-gather.25.cloned.1.call-start = ((), (), s32[]{:S(2)}) async-start(), calls=%async_computation.18 | async-start | bytes 4718592 | tf_op jit(solution)/shard_map/all_gather | solution.py:75
  10.3 110.2 %all-gather.13.cloned.1.call-start = ((), (), s32[]{:S(2)}) async-start(), calls=%async_computation.7 | async-start | bytes 1966080 | tf_op jit(solution)/shard_map/all_gather | solution.py:75
  38.9 21.8 %all-to-all-start = ((bf16[8,256,256]{2,1,0:T(8,128)(2,1)}), bf16[8,256,256]{2,1,0:T(8,128)(2,1)S(1)}, u32[]{:S(2)}, u32[]{:S(2)}) async-start(bf16[8,256,256]{2,1,0:T(8,128)(2,1)} %bitcast.391), calls=%async_computation | async-start | bytes 2097152 | tf_op jit(solution)/shard_map/all_to_all | solution.py:150
  43.2 155.0 %reduce-scatter.9.cloned.1.call-start = ((), (), s32[]{:S(2)}) async-start(), calls=%async_computation.9 | async-start | bytes 4718592 | tf_op jit(solution)/shard_map/reduce_scatter | solution.py:79
  43.8 81.7 %copy-start.23 = (f32[1024,32]{0,1:T(8,128)}, f32[1024,32]{0,1:T(8,128)S(1)}, u32[]{:S(2)}) copy-start(f32[1024,32]{0,1:T(8,128)S(1)} %get-tuple-element.106) | copy-start | bytes 393220
  43.8 81.7 %copy-start.24 = (f32[1024,32]{0,1:T(8,128)}, f32[1024,32]{0,1:T(8,128)S(1)}, u32[]{:S(2)}) copy-start(f32[1024,32]{0,1:T(8,128)S(1)} %get-tuple-element.105) | copy-start | bytes 393220
  44.5 80.7 %copy-start.34 = (f32[1,2048]{1,0:T(1,128)}, f32[1,2048]{1,0:T(1,128)S(1)}, u32[]{:S(2)}) copy-start(f32[1,2048]{1,0:T(1,128)S(1)} %get-tuple-element.104) | copy-start | bytes 24580
  44.5 460.8 %copy-start.32 = (f32[1,2048]{1,0:T(1,128)}, f32[1,2048]{1,0:T(1,128)S(1)}, u32[]{:S(2)}) copy-start(f32[1,2048]{1,0:T(1,128)S(1)} %get-tuple-element.103) | copy-start | bytes 24580
  61.2 81.4 %copy-start.15 = (bf16[256,8,256]{0,2,1:T(8,128)(2,1)}, bf16[256,8,256]{0,2,1:T(8,128)(2,1)S(1)}, u32[]{:S(2)}) copy-start(bf16[256,8,256]{0,2,1:T(8,128)(2,1)S(1)} %copy.171) | copy-start | bytes 3145732
  85.9 39.3 %copy-start.39 = (f32[1024]{0:T(1024)}, f32[1024]{0:T(1024)S(1)}, u32[]{:S(2)}) copy-start(f32[1024]{0:T(1024)S(1)} %add_rsqrt_fusion) | copy-start | bytes 12292
  146.7 51.5 %copy-start.4 = (bf16[1,128,2048]{2,1,0:T(8,128)(2,1)S(1)}, bf16[1,128,2048]{2,1,0:T(8,128)(2,1)}, u32[]{:S(2)}) copy-start(bf16[1,128,2048]{2,1,0:T(8,128)(2,1)} %param.12) | copy-start | bytes 1572868
  146.8 145.3 %all-gather.19.cloned.1.call-start = ((), (), s32[]{:S(2)}) async-start(), calls=%async_computation.11 | async-start | bytes 2621440 | tf_op jit(solution)/shard_map/all_gather | solution.py:75
  199.5 305.7 %copy-start.37 = (f32[128]{0:T(128)}, f32[128]{0:T(128)S(1)}, u32[]{:S(2)}) copy-start(f32[128]{0:T(128)S(1)} %add_rsqrt_fusion.2) | copy-start | bytes 1540
  201.6 183.6 %all-gather.17.cloned.1.call-start = ((), (), s32[]{:S(2)}) async-start(), calls=%async_computation.10 | async-start | bytes 18874368 | tf_op jit(solution)/shard_map/all_gather | solution.py:75
  230.1 26.4 %collective-permute-start = (bf16[1,2,512,256]{3,2,1,0:T(8,128)(2,1)}, bf16[1,2,512,256]{3,2,1,0:T(8,128)(2,1)}, u32[]{:S(2)}, u32[]{:S(2)}) collective-permute-start(bf16[1,2,512,256]{3,2,1,0:T(8,128)(2,1)} %bitcast.394), channel_id=1, source_target_pairs={{0,1},{1,2},{2,3},{3,0},{4,5},{5,6},{6,7},{7,4},{8,9},{9,10},{10,1... | collective-permute-start | bytes 1572872 | tf_op jit(solution)/shard_map/ppermute | solution.py:95
  232.4 45.9 %collective-permute-start.1 = (bf16[1,2,512,256]{3,2,1,0:T(8,128)(2,1)}, bf16[1,2,512,256]{3,2,1,0:T(8,128)(2,1)}, u32[]{:S(2)}, u32[]{:S(2)}) collective-permute-start(bf16[1,2,512,256]{3,2,1,0:T(8,128)(2,1)} %bitcast.393), channel_id=1, source_target_pairs={{0,2},{1,3},{2,0},{3,1},{4,6},{5,7},{6,4},{7,5},{8,10},{9,11},{10,... | collective-permute-start | bytes 1572872 | tf_op jit(solution)/shard_map/ppermute | solution.py:95
  232.8 56.6 %collective-permute-start.2 = (bf16[1,2,512,256]{3,2,1,0:T(8,128)(2,1)S(1)}, bf16[1,2,512,256]{3,2,1,0:T(8,128)(2,1)}, u32[]{:S(2)}, u32[]{:S(2)}) collective-permute-start(bf16[1,2,512,256]{3,2,1,0:T(8,128)(2,1)S(1)} %bitcast.392), channel_id=1, source_target_pairs={{0,3},{1,0},{2,1},{3,2},{4,7},{5,4},{6,5},{7,6},{8,11},{9,8},{10,9... | collective-permute-start | bytes 1572872 | tf_op jit(solution)/shard_map/ppermute | solution.py:95
  291.3 139.8 %all-gather.27.cloned.1.call-start = ((), (), s32[]{:S(2)}) async-start(), calls=%async_computation.19 | async-start | bytes 2621440 | tf_op jit(solution)/shard_map/all_gather | solution.py:75
  292.0 211.1 %reduce-scatter.13.cloned.1.call-start = ((), (), s32[]{:S(2)}) async-start(), calls=%async_computation.13 | async-start | bytes 2621440 | tf_op jit(solution)/shard_map/reduce_scatter | solution.py:79
  445.7 57.4 %copy-start.6 = (bf16[128,2048]{1,0:T(8,128)(2,1)S(1)}, bf16[128,2048]{1,0:T(8,128)(2,1)}, u32[]{:S(2)}) copy-start(bf16[128,2048]{1,0:T(8,128)(2,1)} %reduce-scatter.9.cloned.1.call-done) | copy-start | bytes 1572868
  445.7 59.6 %copy-start.12 = (bf16[1,128,2048]{2,1,0:T(8,128)(2,1)S(1)}, bf16[1,128,2048]{2,1,0:T(8,128)(2,1)}, u32[]{:S(2)}) copy-start(bf16[1,128,2048]{2,1,0:T(8,128)(2,1)} %param.13) | copy-start | bytes 1572868
  459.6 85.2 %all-gather.21.cloned.1.call-start = ((), (), s32[]{:S(2)}) async-start(), calls=%async_computation.14 | async-start | bytes 4718592 | tf_op jit(solution)/shard_map/all_gather | solution.py:75
  505.3 43.5 %copy-start.41 = (f32[128]{0:T(128)}, f32[128]{0:T(128)S(1)}, u32[]{:S(2)}) copy-start(f32[128]{0:T(128)S(1)} %broadcast_multiply_fusion.1) | copy-start | bytes 1540
  544.8 14.0 %slice-start = ((s8[16777216]{0:T(1024)(128)(4,1)}), s8[4194304]{0:T(1024)(128)(4,1)S(1)}, s32[]{:S(2)}) async-start(s8[16777216]{0:T(1024)(128)(4,1)} %bitcast.364), calls=%async_computation.22 | async-start | bytes 8388608
  589.6 15.6 %all-to-all-start.1 = ((bf16[256,8,256]{0,2,1:T(8,128)(2,1)}), bf16[256,8,256]{0,2,1:T(8,128)(2,1)S(1)}, u32[]{:S(2)}, u32[]{:S(2)}) async-start(bf16[256,8,256]{0,2,1:T(8,128)(2,1)} %bitcast.83), calls=%async_computation.5 | async-start | bytes 2097152 | tf_op jit(solution)/shard_map/all_to_all | solution.py:233
  593.4 69.3 %reduce-scatter.17.cloned.1.call-start = ((), (), s32[]{:S(2)}) async-start(), calls=%async_computation.16 | async-start | bytes 3276800 | tf_op jit(solution)/shard_map/reduce_scatter | solution.py:79
  608.6 12.3 copy-start.44
  608.7 366.2 %all-reduce.4.cloned.1.call-start = ((), (), s32[]{:S(2)}) async-start(), calls=%async_computation.21 | async-start | bytes 50331648
  608.7 12.3 copy-start.50
  608.7 12.3 copy-start.52
  633.5 407.6 %reduce-scatter.15.cloned.1.call-start = ((), (), s32[]{:S(2)}) async-start(), calls=%async_computation.15 | async-start | bytes 4718592 | tf_op jit(solution)/shard_map/reduce_scatter | solution.py:79
  639.5 23.2 %copy-start.46 = (u32[32]{0:T(128)S(1)}, u32[32]{0:T(128)}, u32[]{:S(2)}) copy-start(u32[32]{0:T(128)} %constant.263) | copy-start | bytes 388
  639.5 446.5 %reduce-scatter.11.cloned.1.call-start = ((), (), s32[]{:S(2)}) async-start(), calls=%async_computation.12 | async-start | bytes 2621440 | tf_op jit(solution)/shard_map/reduce_scatter | solution.py:79
  651.8 469.8 %all-gather.29.cloned.1.call-start = ((), (), s32[]{:S(2)}) async-start(), calls=%async_computation.20 | async-start | bytes 5898240 | tf_op jit(solution)/shard_map/all_gather | solution.py:236
  662.7 550.7 %all-gather.23.cloned.1.call-start = ((), (), s32[]{:S(2)}) async-start(), calls=%async_computation.17 | async-start | bytes 18874368 | tf_op jit(solution)/shard_map/all_gather | solution.py:210
  981.7 12.7 collective-permute-start.3
  982.9 34.1 %collective-permute-start.4 = (bf16[1,2,512,256]{3,2,1,0:T(8,128)(2,1)S(1)}, bf16[1,2,512,256]{3,2,1,0:T(8,128)(2,1)S(1)}, u32[]{:S(2)}, u32[]{:S(2)}) collective-permute-start(bf16[1,2,512,256]{3,2,1,0:T(8,128)(2,1)S(1)} %get-tuple-element.86), channel_id=1, source_target_pairs={{0,2},{1,3},{2,0},{3,1},{4,6},{5,7},{6,4},{7,5},{8,10},{9,11},{10,... | collective-permute-start | bytes 1572872 | tf_op jit(solution)/shard_map/ppermute | solution.py:95
  983.2 45.1 %collective-permute-start.5 = (bf16[1,2,512,256]{3,2,1,0:T(8,128)(2,1)S(1)}, bf16[1,2,512,256]{3,2,1,0:T(8,128)(2,1)S(1)}, u32[]{:S(2)}, u32[]{:S(2)}) collective-permute-start(bf16[1,2,512,256]{3,2,1,0:T(8,128)(2,1)S(1)} %get-tuple-element.85), channel_id=1, source_target_pairs={{0,3},{1,0},{2,1},{3,2},{4,7},{5,4},{6,5},{7,6},{8,11},{9,8},{10,9... | collective-permute-start | bytes 1572872 | tf_op jit(solution)/shard_map/ppermute | solution.py:95
  1029.1 11.9 copy-start.5
  1029.1 13.4 %copy-start.36 = (f32[2048]{0:T(1024)S(1)}, f32[2048]{0:T(1024)}, u32[]{:S(2)}) copy-start(f32[2048]{0:T(1024)} %get-tuple-element.66) | copy-start | bytes 24580
  1029.2 56.9 %copy-start.7 = (bf16[128,2048]{1,0:T(8,128)(2,1)S(1)}, bf16[128,2048]{1,0:T(8,128)(2,1)}, u32[]{:S(2)}) copy-start(bf16[128,2048]{1,0:T(8,128)(2,1)} %reduce-scatter.9.cloned.1.call-done) | copy-start | bytes 1572868
  1029.2 56.9 %copy-start.11 = (bf16[128,2048]{1,0:T(8,128)(2,1)S(1)}, bf16[128,2048]{1,0:T(8,128)(2,1)}, u32[]{:S(2)}) copy-start(bf16[128,2048]{1,0:T(8,128)(2,1)} %reduce-scatter.13.cloned.1.call-done) | copy-start | bytes 1572868
  1029.2 56.9 %copy-start.13 = (bf16[1,128,2048]{2,1,0:T(8,128)(2,1)S(1)}, bf16[1,128,2048]{2,1,0:T(8,128)(2,1)}, u32[]{:S(2)}) copy-start(bf16[1,128,2048]{2,1,0:T(8,128)(2,1)} %param.13) | copy-start | bytes 1572868
  1029.2 56.9 %copy-start.33 = (f32[1,2048]{1,0:T(1,128)S(1)}, f32[1,2048]{1,0:T(1,128)}, u32[]{:S(2)}) copy-start(f32[1,2048]{1,0:T(1,128)} %copy-done.32) | copy-start | bytes 24580
  1029.2 56.9 %copy-start.38 = (f32[128]{0:T(128)S(1)}, f32[128]{0:T(128)}, u32[]{:S(2)}) copy-start(f32[128]{0:T(128)} %copy-done.37) | copy-start | bytes 1540
  1029.2 56.9 %copy-start.42 = (f32[128]{0:T(128)S(1)}, f32[128]{0:T(128)}, u32[]{:S(2)}) copy-start(f32[128]{0:T(128)} %copy-done.41) | copy-start | bytes 1540
  1292.5 17.6 %copy-start.1 = (bf16[512,2048]{1,0:T(8,128)(2,1)S(1)}, bf16[512,2048]{1,0:T(8,128)(2,1)}, u32[]{:S(2)}) copy-start(bf16[512,2048]{1,0:T(8,128)(2,1)} %param.19) | copy-start | bytes 6291460
  (32 other events, 120.8 us)
Sparse Core Ops, SparseCore 0:
  10.2 28.6 all-gather.14
  40.8 41.9 all-gather.24
  84.9 35.5 all-gather.12
  146.9 51.3 reduce-scatter.8
  201.7 71.0 all-gather.18
  291.4 93.7 all-gather.16
  386.8 44.1 all-gather.26
  459.7 43.3 reduce-scatter.12
  507.7 37.0 all-gather.20
  608.8 53.8 reduce-scatter.16
  667.2 307.6 all-reduce.3
  979.1 51.4 reduce-scatter.14
  1032.9 44.2 reduce-scatter.10
  1079.0 42.4 all-gather.28
  1123.4 89.8 all-gather.22

commit v2 on v1

v2 whole, which is shorter than its diff:
```python
import functools
import math

import jax
import jax.numpy as jnp
from jax import lax
from jax.experimental import pallas as pl
from jax.experimental.pallas import tpu as pltpu
from jax.sharding import PartitionSpec as P

HEAD_DIM = 64


EPS = 1e-05
THETA = 500000.0


def frequencies(head_width):
    evens = jnp.arange(0, head_width, 2, dtype=jnp.float32)
    inverse = 1.0 / THETA ** (evens / head_width)
    wavelen = 2.0 * math.pi / inverse
    smooth = (8192.0 / wavelen - 1.0) / 3.0
    middle = (1.0 - smooth) * inverse / 32.0 + smooth * inverse
    return jnp.where(wavelen < 2048.0, inverse, jnp.where(wavelen > 8192.0, inverse / 32.0, middle))


def rotation(positions, head_width):
    angles = positions.astype(jnp.float32)[:, None] * frequencies(head_width)[None, :]
    cosine = jnp.concatenate([jnp.cos(angles), jnp.cos(angles)], axis=1)[:, None, :]
    sine = jnp.concatenate([jnp.sin(angles), jnp.sin(angles)], axis=1)[:, None, :]
    return (cosine, sine)


def rotate(tensor, cosine, sine):
    middle = tensor.shape[-1] // 2
    turned = jnp.concatenate([-tensor[..., middle:], tensor[..., :middle]], axis=-1)
    return tensor * cosine + turned * sine


def unrotate(gradient, cosine, sine):
    middle = gradient.shape[-1] // 2
    moved = gradient * sine
    back_turn = jnp.concatenate([moved[..., middle:], -moved[..., :middle]], axis=-1)
    return gradient * cosine + back_turn


def slot_positions(pairing, seq_length, block_len):
    flattened = pairing.reshape(-1)
    slots = jnp.arange(seq_length, dtype=jnp.int32)
    owning = slots // block_len
    labels = jnp.arange(flattened.shape[0], dtype=jnp.int32)
    anchor = jnp.sum(jnp.where(owning[:, None] == labels[None, :], flattened[None, :], 0), axis=1)
    return anchor * block_len + slots % block_len


def product(left, right):
    return jnp.dot(left, right, preferred_element_type=jnp.float32)


def product_t(left, right):
    return lax.dot_general(
        left, right, (((1,), (1,)), ((), ())), preferred_element_type=jnp.float32
    )


def tokens_t(left, right):
    return lax.dot_general(
        left, right, (((0,), (0,)), ((), ())), preferred_element_type=jnp.float32
    )


LOW = jnp.bfloat16
MESH = pl.DeviceIdType.MESH
ANY = pl.BlockSpec(memory_space=pl.ANY)
VMEM = pl.BlockSpec(memory_space=pltpu.VMEM)


def norm_back(upstream, gain, unit, scale):
    weighted = upstream * gain
    return scale * (weighted - unit * jnp.mean(weighted * unit, axis=1, keepdims=True))


def gather(array, axis):
    return lax.all_gather(array, axis, axis=0, tiled=True)


def scatter_sum(array, axis):
    return lax.psum_scatter(array, axis, scatter_dimension=0, tiled=True)


def einsum(spec, left, right):
    return jnp.einsum(spec, left, right, preferred_element_type=jnp.float32)


def by_permutes(piece_for, axis):
    count, me = lax.axis_size(axis), lax.axis_index(axis)
    own = piece_for(me)
    rows = own.shape[0]
    out = jnp.zeros((count * rows, *own.shape[1:]), own.dtype)
    out = lax.dynamic_update_slice_in_dim(out, own, me * rows, 0)
    for shift in range(1, count):
        piece = piece_for(lax.rem(me + shift, count))
        piece = lax.ppermute(piece, axis, [(i, (i + shift) % count) for i in range(count)])
        out = lax.dynamic_update_slice_in_dim(out, piece, lax.rem(me + count - shift, count) * rows, 0)
    return out


def swap_order(array, first, second):
    size = array.shape[1] // (first * second)
    parts = []
    for b in range(second):
        for a in range(first):
            at = (a * second + b) * size
            parts.append(array[:, at : at + size])
    return jnp.concatenate(parts, axis=1)


class Links:
    def __init__(self, n_ctx, n_fsdp, send_sems, recv_sems):
        self.n_ctx, self.n_fsdp = n_ctx, n_fsdp
        self.ctx, self.fsdp = lax.axis_index("ctx"), lax.axis_index("fsdp")
        self.send_sems, self.recv_sems = send_sems, recv_sems
        self.used = 0
        core = self.ctx % 2
        flips = [self.flip(d) for d in range(1, n_ctx.bit_length() - 1)]
        backward = flips[::-1]
        self.order = [(1 - core) * a + core * b for a, b in zip(flips, backward)]
        self.sibling = self.flip(0)

    def flip(self, digit):
        return 2**digit * (1 - 2 * ((self.ctx // 2**digit) % 2))

    def greet(self, cube=False, plane=False, line=False, whole_line=False):
        barrier = pltpu.get_barrier_semaphore()
        count = 0

        def hail(ctx, fsdp):
            pl.semaphore_signal(barrier, inc=1, device_id=(ctx, fsdp), device_id_type=MESH)

        if plane:
            for shift in range(1, self.n_ctx):
                hail(lax.rem(self.ctx + shift, self.n_ctx), self.fsdp)
            count += self.n_ctx - 1
        elif cube:
            for step in self.order + [self.sibling]:
                hail(self.ctx + step, self.fsdp)
            count += len(self.order) + 1
        if whole_line:
            for shift in range(1, self.n_fsdp):
                hail(self.ctx, lax.rem(self.fsdp + shift, self.n_fsdp))
            count += self.n_fsdp - 1
        if line and not whole_line:
            for step in (-1, 1):
                inside = jnp.logical_and(self.fsdp + step >= 0, self.fsdp + step < self.n_fsdp)

                @pl.when(inside)
                def _():
                    hail(self.ctx, self.fsdp + step)

            ends = jnp.logical_or(self.fsdp == 0, self.fsdp == self.n_fsdp - 1)
            pl.when(ends)(lambda: pl.semaphore_wait(barrier, count + 1))
            pl.when(jnp.logical_not(ends))(lambda: pl.semaphore_wait(barrier, count + 2))
        else:
            pl.semaphore_wait(barrier, count)

    def copy(self, source, target, ctx, fsdp):
        slot = self.used
        self.used += 1
        return pltpu.make_async_remote_copy(
            src_ref=source,
            dst_ref=target,
            send_sem=self.send_sems.at[slot],
            recv_sem=self.recv_sems.at[slot],
            device_id=(ctx, fsdp),
            device_id_type=MESH,
        )


def rows_of(ref, index, rows):
    return ref.at[pl.ds(pl.multiple_of(index * rows, rows), rows)]


def cube_gather(links, ref, rows, between=None):
    held, sent = [0], []
    to_sibling = []

    def share(offset):
        block = rows_of(ref, links.ctx + offset, rows)
        copy = links.copy(block, block, links.ctx + links.sibling, links.fsdp)
        copy.start()
        to_sibling.append(copy)

    for stage, step in enumerate(links.order):
        copies = []
        for offset in held:
            block = rows_of(ref, links.ctx + offset, rows)
            copy = links.copy(block, block, links.ctx + step, links.fsdp)
            copy.start()
            copies.append(copy)
        for offset in held if stage == 0 else held[len(held) // 2 :]:
            share(offset)
        if stage == 0 and between is not None:
            between()
        for copy in copies:
            copy.wait_recv()
        sent += copies
        held = held + [offset + step for offset in held]
    for offset in held[len(held) // 2 :] if links.order else held:
        share(offset)
    for copy in to_sibling:
        copy.wait_recv()
    for copy in sent + to_sibling:
        copy.wait_send()


def cube_slots(n_ctx):
    return n_ctx - 1


def cube_sum(links, part, stage_ref, land, rows):
    offsets = [0]
    theirs = [0]
    for step, other in zip(links.order, links.order[::-1]):
        offsets = offsets + [offset + step for offset in offsets]
        theirs = theirs + [offset + other for offset in theirs]
    sent = []
    copies = []
    for at, offset in enumerate(theirs):
        source = rows_of(part, links.ctx + links.sibling + offset, rows)
        copy = links.copy(source, land.at[pl.ds(at * rows, rows)], links.ctx + links.sibling, links.fsdp)
        copy.start()
        copies.append(copy)
    sums = {}
    stage_at, land_at = 0, len(offsets)
    pending = copies
    first = True
    for level in range(len(links.order) + 1):
        last = level == len(links.order)
        count = len(offsets)
        half = count // 2
        step = None if last else links.order[len(links.order) - 1 - level]
        onward = []
        for at in list(range(half, count)) + list(range(half)) if not last else [0]:
            pending[at].wait_recv()
            if first:
                base = rows_of(part, links.ctx + offsets[at], rows)[...].astype(jnp.float32)
            else:
                base = sums[at]
            start = pending_land + at * rows if not first else at * rows
            total = base + land[pl.ds(start, rows), :].astype(jnp.float32)
            if not last and at >= half:
                slot = stage_ref.at[pl.ds(stage_at * rows, rows)]
                slot[...] = total.astype(LOW)
                copy = links.copy(
                    slot, land.at[pl.ds((land_at + at - half) * rows, rows)], links.ctx + step, links.fsdp
                )
                copy.start()
                onward.append(copy)
                stage_at += 1
            else:
                sums[at] = total
        sent += pending
        pending = onward
        pending_land = land_at * rows
        land_at += half
        offsets = offsets[:half] if not last else offsets
        first = False
    for copy in sent:
        copy.wait_send()
    return sums[0]


def line_gather(links, refs, rows):
    count, me = links.n_fsdp, links.fsdp
    sends = []
    for hop in range(count - 1):
        receives = []
        for ref, size in zip(refs, rows):
            up_block = rows_of(ref, me - hop, size)
            down_block = rows_of(ref, me + hop, size)
            up = links.copy(up_block, up_block, links.ctx, me + 1)
            down = links.copy(down_block, down_block, links.ctx, me - 1)
            up_ok = jnp.logical_and(me >= hop, me < count - 1)
            down_ok = jnp.logical_and(me <= count - 1 - hop, me > 0)
            pl.when(up_ok)(up.start)
            pl.when(down_ok)(down.start)
            sends += [(up_ok, up), (down_ok, down)]
            receives += [(me >= hop + 1, up), (me <= count - 2 - hop, down)]
        for ok, copy in receives:
            pl.when(ok)(copy.wait_recv)

    def finish():
        for ok, copy in sends:
            pl.when(ok)(copy.wait_send)

    return finish


def line_sum(links, part, stage_ref, land, total, rows):
    count, me = links.n_fsdp, links.fsdp
    flows = []
    for hop in range(count - 1):
        for side in (0, 1):
            goal = count - 1 - hop if side == 0 else hop
            slot = (side * (count - 1) + hop) * rows
            landing = land.at[pl.ds(slot, rows)]
            staging = stage_ref.at[pl.ds(slot, rows)]
            onward = links.copy(staging, landing, links.ctx, me + 1 if side == 0 else me - 1)
            fed = me > 0 if side == 0 else me < count - 1
            passes = me < goal if side == 0 else me > goal
            flows.append((side, goal, landing, staging, onward, fed, passes))
    for side, goal, landing, staging, onward, fed, passes in flows:

        @pl.when(jnp.logical_and(passes, jnp.logical_not(fed)))
        def _():
            staging[...] = part[pl.ds(goal * rows, rows), :]
            onward.start()

    def steps():
        total[...] = rows_of(part, me, rows)[...].astype(jnp.float32)
        lower = me < count // 2
        for near in (0, 1):

            @pl.when(lower if near == 0 else jnp.logical_not(lower))
            def _():
                for hop in range(count - 1):
                    for way in (near, 1 - near):
                        side, goal, landing, staging, onward, fed, passes = flows[2 * hop + way]

                        @pl.when(jnp.logical_and(passes, fed))
                        def _():
                            onward.wait_recv()
                            own = part[pl.ds(goal * rows, rows), :].astype(jnp.float32)
                            staging[...] = (own + landing[...].astype(jnp.float32)).astype(LOW)
                            onward.start()

        for side, goal, landing, staging, onward, fed, passes in flows:

            @pl.when(jnp.logical_and(me == goal, fed))
            def _():
                onward.wait_recv()
                total[...] += landing[...].astype(jnp.float32)

        for side, goal, landing, staging, onward, fed, passes in flows:
            pl.when(passes)(onward.wait_send)

    return steps


def communicate(kernel, collective_id, name, operands, in_specs, outs, out_specs, scratch, copies, busy):
    return pl.pallas_call(
        kernel,
        out_shape=outs,
        in_specs=in_specs,
        out_specs=out_specs,
        scratch_shapes=scratch
        + [pltpu.SemaphoreType.DMA((copies,)), pltpu.SemaphoreType.DMA((copies,))],
        compiler_params=pltpu.CompilerParams(
            collective_id=collective_id, has_side_effects=True, vmem_limit_bytes=48 << 20
        ),
        cost_estimate=pl.CostEstimate(flops=0, bytes_accessed=busy * 3_000_000, transcendentals=0),
        name=name,
    )(*operands)


def front_kernel(
    n_ctx,
    n_fsdp,
    own,
    w_query,
    kv,
    w_out,
    gains,
    seq,
    q_all,
    kv_all,
    gains_all,
    cols_all,
    out_rows,
    local_sems,
    send_sems,
    recv_sems,
):
    links = Links(n_ctx, n_fsdp, send_sems, recv_sems)
    rows, weight_rows, query_width = own.shape[0], kv.shape[0], q_all.shape[1]
    head_rows, out_width = out_rows.shape[0], cols_all.shape[1]

    def cut(ref, size):
        return ref.at[:, pl.ds(pl.multiple_of(links.ctx * size, size), size)]

    local = [
        (own, rows_of(seq, links.ctx, rows)),
        (cut(w_query, query_width), rows_of(q_all, links.fsdp, weight_rows)),
        (kv, rows_of(kv_all, links.fsdp, weight_rows)),
        (gains, rows_of(gains_all, links.fsdp, gains.shape[0])),
        (cut(w_out, out_width), rows_of(cols_all, links.fsdp, weight_rows)),
    ]
    local = [pltpu.make_async_copy(a, b, local_sems.at[i]) for i, (a, b) in enumerate(local)]
    for copy in local:
        copy.start()
    links.greet(plane=True, line=True)
    for copy in local:
        copy.wait()
    ends = []

    def between():
        refs = [gains_all, q_all, kv_all, cols_all]
        ends.append(line_gather(links, refs, [gains.shape[0]] + [weight_rows] * 3))

    cube_gather(links, seq, rows, between)
    column = cut(out_rows, out_width)
    mine = pltpu.make_async_copy(rows_of(cols_all, links.ctx, head_rows), column, local_sems.at[0])
    mine.start()
    copies = []
    for shift in range(1, n_ctx):
        target = lax.rem(links.ctx + shift, n_ctx)
        copy = links.copy(rows_of(cols_all, target, head_rows), column, target, links.fsdp)
        copy.start()
        copies.append(copy)
    for copy in copies:
        copy.wait()
    mine.wait()
    for end in ends:
        end()


def front(n_ctx, n_fsdp, own, w_query, kv, w_out, gains):
    rows, width = own.shape
    weight_rows = kv.shape[0]
    total = weight_rows * n_fsdp
    query_width, out_width = w_query.shape[1] // n_ctx, width // n_ctx
    shape = lambda *dims: jax.ShapeDtypeStruct(dims, LOW)
    return communicate(
        functools.partial(front_kernel, n_ctx, n_fsdp),
        1,
        "front",
        (own, w_query, kv, w_out, gains),
        [ANY] * 5,
        [
            shape(rows * n_ctx, width),
            shape(total, query_width),
            shape(total, kv.shape[1]),
            jax.ShapeDtypeStruct((gains.shape[0] * n_fsdp, gains.shape[1]), jnp.float32),
            shape(total, out_width),
            shape(total // n_ctx, width),
        ],
        [ANY] * 6,
        [pltpu.SemaphoreType.DMA((5,))],
        2 * (n_ctx - 1) + 8 * (n_fsdp - 1),
        50,
    )


def middle_kernel(
    n_ctx, n_fsdp, part, own, gain, resid, normed, staged, land, send_sems, recv_sems
):
    links = Links(n_ctx, n_fsdp, send_sems, recv_sems)
    rows = own.shape[0]
    links.greet(cube=True, line=True)
    value = cube_sum(links, part, staged, land, rows) + own[...].astype(jnp.float32)
    resid[...] = value
    scale = lax.rsqrt(jnp.mean(value * value, axis=1, keepdims=True) + EPS)
    block = swap_order((value * scale * gain[...]).astype(LOW), n_fsdp, n_ctx)
    rows_of(normed, links.fsdp, rows)[...] = block
    line_gather(links, [normed], [rows])()


def middle(n_ctx, n_fsdp, part, own, gain):
    rows, width = own.shape
    return communicate(
        functools.partial(middle_kernel, n_ctx, n_fsdp),
        2,
        "middle",
        (part, own, gain),
        [VMEM] * 3,
        [
            jax.ShapeDtypeStruct((rows, width), jnp.float32),
            jax.ShapeDtypeStruct((rows * n_fsdp, width), LOW),
        ],
        [VMEM] * 2,
        [
            pltpu.VMEM(((n_ctx // 2 - 1) * rows, width), LOW),
            pltpu.VMEM(((n_ctx - 1) * rows, width), LOW),
        ],
        n_ctx - 1 + 2 * (n_fsdp - 1),
        60,
    )


def turn_kernel(
    n_ctx, n_fsdp, part, upstream, resid, gain, d_resid, seq, term, staged, land, total, send_sems, recv_sems
):
    links = Links(n_ctx, n_fsdp, send_sems, recv_sems)
    rows = upstream.shape[0]
    links.greet(cube=True, line=True)
    line_sum(links, part, staged, land, total, rows)()
    d_normed = swap_order(total[...], n_ctx, n_fsdp)
    value = resid[...]
    scale = lax.rsqrt(jnp.mean(value * value, axis=1, keepdims=True) + EPS)
    unit = value * scale
    term[...] = jnp.sum(d_normed * unit, axis=0, keepdims=True)
    value = upstream[...].astype(jnp.float32) + norm_back(d_normed, gain[...], unit, scale)
    d_resid[...] = value
    rows_of(seq, links.ctx, rows)[...] = value.astype(LOW)
    cube_gather(links, seq, rows)


def turn(n_ctx, n_fsdp, part, upstream, resid, gain):
    rows, width = upstream.shape
    return communicate(
        functools.partial(turn_kernel, n_ctx, n_fsdp),
        3,
        "turn",
        (part, upstream, resid, gain),
        [VMEM] * 4,
        [
            jax.ShapeDtypeStruct((rows, width), jnp.float32),
            jax.ShapeDtypeStruct((rows * n_ctx, width), LOW),
            jax.ShapeDtypeStruct((1, width), jnp.float32),
        ],
        [VMEM] * 3,
        [
            pltpu.VMEM((2 * (n_fsdp - 1) * rows, width), LOW),
            pltpu.VMEM((2 * (n_fsdp - 1) * rows, width), LOW),
            pltpu.VMEM((rows, width), jnp.float32),
        ],
        n_ctx - 1 + 2 * (n_fsdp - 1),
        65,
    )


def last_kernel(
    n_ctx,
    n_fsdp,
    part,
    down_part,
    own,
    resid,
    d_resid,
    gain,
    d_own,
    output,
    term,
    staged,
    land,
    down_staged,
    down_land,
    total,
    send_sems,
    recv_sems,
):
    links = Links(n_ctx, n_fsdp, send_sems, recv_sems)
    rows = own.shape[0]
    links.greet(cube=True, line=True)
    finish = line_sum(links, down_part, down_staged, down_land, total, rows)
    d_normed = cube_sum(links, part, staged, land, rows)
    value = own[...].astype(jnp.float32)
    scale = lax.rsqrt(jnp.mean(value * value, axis=1, keepdims=True) + EPS)
    unit = value * scale
    term[...] = jnp.sum(d_normed * unit, axis=0, keepdims=True)
    d_own[...] = (d_resid[...] + norm_back(d_normed, gain[...], unit, scale)).astype(LOW)
    finish()
    output[...] = (resid[...] + total[...]).astype(LOW)


def last(n_ctx, n_fsdp, part, down_part, own, resid, d_resid, gain):
    rows, width = own.shape
    return communicate(
        functools.partial(last_kernel, n_ctx, n_fsdp),
        4,
        "last",
        (part, down_part, own, resid, d_resid, gain),
        [VMEM] * 6,
        [
            jax.ShapeDtypeStruct((rows, width), LOW),
            jax.ShapeDtypeStruct((rows, width), LOW),
            jax.ShapeDtypeStruct((1, width), jnp.float32),
        ],
        [VMEM] * 3,
        [
            pltpu.VMEM(((n_ctx // 2 - 1) * rows, width), LOW),
            pltpu.VMEM(((n_ctx - 1) * rows, width), LOW),
            pltpu.VMEM((2 * (n_fsdp - 1) * rows, width), LOW),
            pltpu.VMEM((2 * (n_fsdp - 1) * rows, width), LOW),
            pltpu.VMEM((rows, width), jnp.float32),
        ],
        n_ctx - 1 + 2 * (n_fsdp - 1),
        45,
    )


def tail_kernel(
    n_ctx,
    n_fsdp,
    gate,
    up,
    down,
    joined,
    out_part,
    gate_all,
    up_all,
    down_all,
    attn_all,
    attn_part,
    staged,
    land,
    total,
    attn_low,
    local_sems,
    send_sems,
    recv_sems,
):
    links = Links(n_ctx, n_fsdp, send_sems, recv_sems)
    strip, ff_rows = gate.shape[0] // n_fsdp, gate.shape[1]
    down_rows, rows = down.shape[0], joined.shape[0] // n_fsdp
    head_rows, joined_width = out_part.shape[0], joined.shape[1]
    out_width = attn_part.shape[1] - joined_width

    def place(ref, ctx, fsdp):
        return ref.at[
            pl.ds(pl.multiple_of(ctx * strip, strip), strip),
            pl.ds(pl.multiple_of(fsdp * ff_rows, ff_rows), ff_rows),
        ]

    def out_column(ctx):
        return out_part.at[:, pl.ds(pl.multiple_of(ctx * out_width, out_width), out_width)]

    def out_place(ctx):
        return attn_part.at[
            pl.ds(pl.multiple_of(ctx * head_rows, head_rows), head_rows), pl.ds(joined_width, out_width)
        ]

    local = [
        (down, rows_of(down_all, links.ctx, down_rows)),
        (rows_of(gate, links.fsdp, strip), place(gate_all, links.ctx, links.fsdp)),
        (rows_of(up, links.fsdp, strip), place(up_all, links.ctx, links.fsdp)),
        (joined, attn_part.at[:, pl.ds(0, joined_width)]),
        (out_column(links.ctx), out_place(links.ctx)),
    ]
    local = [pltpu.make_async_copy(a, b, local_sems.at[i]) for i, (a, b) in enumerate(local)]
    for copy in local:
        copy.start()
    links.greet(plane=True, line=True, whole_line=True)
    to_shards, to_plane = [], []
    for shift in range(1, n_fsdp):
        target = lax.rem(links.fsdp + shift, n_fsdp)
        for source, goal in ((gate, gate_all), (up, up_all)):
            copy = links.copy(
                rows_of(source, target, strip), place(goal, links.ctx, links.fsdp), links.ctx, target
            )
            copy.start()
            to_shards.append(copy)
    for shift in range(1, n_ctx):
        target = lax.rem(links.ctx + shift, n_ctx)
        copy = links.copy(out_column(target), out_place(links.ctx), target, links.fsdp)
        copy.start()
        to_plane.append(copy)
    for copy in local:
        copy.wait()
    cube_gather(links, down_all, down_rows)
    for copy in to_plane + to_shards:
        copy.wait()
    finish = line_sum(links, attn_part, staged, land, total, rows)
    cube_gather(links, gate_all, strip, finish)
    cube_gather(links, up_all, strip)
    attn_low[...] = total[...].astype(LOW)
    mine = pltpu.make_async_copy(attn_low, rows_of(attn_all, links.ctx, rows), local_sems.at[0])
    mine.start()
    mine.wait()
    cube_gather(links, attn_all, rows)


def tail(n_ctx, n_fsdp, gate, up, down, joined, out_part):
    strip, ff_rows = gate.shape[0] // n_fsdp, gate.shape[1]
    rows = joined.shape[0] // n_fsdp
    attn_width = joined.shape[1] + out_part.shape[1] // n_ctx
    shape = lambda *dims: jax.ShapeDtypeStruct(dims, LOW)
    return communicate(
        functools.partial(tail_kernel, n_ctx, n_fsdp),
        5,
        "tail",
        (gate, up, down, joined, out_part),
        [ANY] * 5,
        [
            shape(strip * n_ctx, ff_rows * n_fsdp),
            shape(strip * n_ctx, ff_rows * n_fsdp),
            shape(down.shape[0] * n_ctx, down.shape[1]),
            shape(rows * n_ctx, attn_width),
        ],
        [ANY] * 4,
        [
            pltpu.VMEM((rows * n_fsdp, attn_width), LOW),
            pltpu.VMEM((2 * (n_fsdp - 1) * rows, attn_width), LOW),
            pltpu.VMEM((2 * (n_fsdp - 1) * rows, attn_width), LOW),
            pltpu.VMEM((rows, attn_width), jnp.float32),
            pltpu.VMEM((rows, attn_width), LOW),
            pltpu.SemaphoreType.DMA((5,)),
        ],
        5 * (n_ctx - 1) + 4 * (n_fsdp - 1),
        150,
    )


def spread_kernel(parts, widths, gathered, *outs):
    at = 0
    for out, width, sharers in zip(outs, widths, parts):
        pieces = []
        for i in range(0, gathered.shape[0], sharers):
            piece = gathered[i, :, at : at + width].astype(jnp.float32)
            for j in range(1, sharers):
                piece = piece + gathered[i + j, :, at : at + width].astype(jnp.float32)
            pieces.append(piece)
        out[...] = jnp.concatenate(pieces, axis=1)
        at += width


def spread(gathered, widths, sharers):
    n_ctx, rows, joined = gathered.shape
    step = 2 * max(sharers)
    tile = min(rows, 256)
    return pl.pallas_call(
        functools.partial(spread_kernel, sharers, widths),
        grid=(n_ctx // step, rows // tile),
        in_specs=[pl.BlockSpec((step, tile, joined), lambda i, j: (i, j, 0))],
        out_specs=[
            pl.BlockSpec((tile, step // s * w), lambda i, j: (j, i)) for w, s in zip(widths, sharers)
        ],
        out_shape=[
            jax.ShapeDtypeStruct((rows, n_ctx // s * w), jnp.float32) for w, s in zip(widths, sharers)
        ],
        compiler_params=pltpu.CompilerParams(vmem_limit_bytes=32 << 20),
        name="spread",
    )(gathered)


def on_device(
    tokens,
    cotangent,
    pairing,
    norm_attn,
    w_query,
    w_key,
    w_value,
    w_out,
    norm_mlp,
    w_gate,
    w_up,
    w_down,
):
    n_ctx, n_fsdp = lax.axis_size("ctx"), lax.axis_size("fsdp")
    ctx = lax.axis_index("ctx")
    own_tokens = tokens[0]
    tok_rows, width = own_tokens.shape
    length = tok_rows * n_ctx
    rows_model = w_gate.shape[0]
    low = LOW

    query_width = w_query.shape[1] // n_ctx
    heads_kv = w_key.shape[1] // HEAD_DIM
    kv_here = max(1, heads_kv // n_ctx)
    sharers = max(1, n_ctx // heads_kv)
    kv_width = kv_here * HEAD_DIM
    group = query_width // kv_width
    kv_start = (ctx // sharers) * kv_width

    def columns(matrix, start, size):
        return lax.dynamic_slice_in_dim(matrix, start, size, 1)

    kv = jnp.concatenate([columns(w_key, kv_start, kv_width), columns(w_value, kv_start, kv_width)], axis=1)
    gains = jnp.zeros((8, rows_model), jnp.float32).at[0].set(norm_attn).at[1].set(norm_mlp)
    sequence, w_q, w_kv, gains, _, w_out_rows = front(
        n_ctx, n_fsdp, own_tokens, w_query, kv, w_out, gains
    )
    gains = gains.reshape(n_fsdp, 8, rows_model)
    gain_attn, gain_mlp = gains[:, 0].reshape(1, -1), gains[:, 1].reshape(1, -1)
    out_width = width // n_ctx

    ff_rows = w_down.shape[0]
    strip = rows_model // n_ctx
    upstream = cotangent[0]
    w_gate, w_up, upstream, sequence = lax.optimization_barrier((w_gate, w_up, upstream, sequence))

    def strips(matrix):
        piece = lambda fsdp: lax.dynamic_slice(matrix, (ctx * strip, fsdp * ff_rows), (strip, ff_rows))
        return by_permutes(piece, "fsdp")

    gate_full = gather(strips(w_gate), "ctx")
    up_full = gather(strips(w_up), "ctx")
    upstream_all = by_permutes(lambda fsdp: upstream, "fsdp")

    all_pos = slot_positions(pairing, length, tok_rows // 2)
    cosine, sine = rotation(all_pos, HEAD_DIM)
    factor = HEAD_DIM ** (-0.5)
    wide = sequence.astype(jnp.float32)
    scale_attn = lax.rsqrt(jnp.mean(wide * wide, axis=1, keepdims=True) + EPS)
    normed_attn = (wide * scale_attn * gain_attn).astype(low)
    w_joined = jnp.concatenate([w_q, w_kv], axis=1)
    projected = product(normed_attn, w_joined)
    query_pre = projected[:, :query_width].reshape(length, -1, HEAD_DIM)
    key_pre = projected[:, query_width : query_width + kv_width].reshape(length, -1, HEAD_DIM)
    values = projected[:, query_width + kv_width :].reshape(length, -1, HEAD_DIM).astype(low)
    queries = rotate(query_pre, cosine, sine).astype(low).reshape(length, kv_here, group, HEAD_DIM)
    keys = rotate(key_pre, cosine, sine).astype(low)
    logits = einsum("qhgd,khd->hgqk", queries, keys)
    allowed = all_pos[None, :] <= all_pos[:, None]
    scores = jnp.where(allowed, logits * factor, -1e30)
    largest = jnp.max(scores, axis=-1, keepdims=True)
    expo = jnp.where(allowed, jnp.exp(scores - largest), 0.0)
    probs = expo / jnp.sum(expo, axis=-1, keepdims=True)
    probs_low = probs.astype(low)
    attended = einsum("hgqk,khd->qhgd", probs_low, values)
    attended_low = attended.reshape(length, query_width).astype(low)
    resid, normed_mlp = middle(
        n_ctx, n_fsdp, product(attended_low, w_out_rows).astype(low), own_tokens, gain_mlp
    )

    gate_pre = product(normed_mlp, gate_full)
    up_pre = product(normed_mlp, up_full)
    sigma = jax.nn.sigmoid(gate_pre)
    swish = gate_pre * sigma
    hidden = (swish * up_pre).astype(low)
    d_hidden = product_t(upstream_all, w_down)
    d_gate = (d_hidden * up_pre * sigma * (1.0 + gate_pre * (1.0 - sigma))).astype(low)
    d_up = (d_hidden * swish).astype(low)
    d_part = (product_t(d_gate, gate_full) + product_t(d_up, up_full)).astype(low)
    grad_gate = tokens_t(normed_mlp, d_gate).astype(low)
    grad_up = tokens_t(normed_mlp, d_up).astype(low)
    d_part, grad_gate, grad_up = lax.optimization_barrier((d_part, grad_gate, grad_up))
    d_resid, d_resid_low, gain_mlp_term = turn(n_ctx, n_fsdp, d_part, upstream, resid, gain_mlp)
    grad_gate, grad_up = scatter_sum(grad_gate, "ctx"), scatter_sum(grad_up, "ctx")
    grad_down = scatter_sum(tokens_t(hidden, upstream_all).astype(low), "ctx")

    d_attended = product_t(d_resid_low, w_out_rows).astype(low)
    d_attended = d_attended.reshape(length, kv_here, group, HEAD_DIM)
    d_probs = einsum("qhgd,khd->hgqk", d_attended, values)
    delta = jnp.sum(probs * d_probs, axis=-1, keepdims=True)
    d_score = (probs * (d_probs - delta) * factor).astype(low)
    d_query_rot = einsum("hgqk,khd->qhgd", d_score, keys)
    d_key_rot = einsum("hgqk,qhgd->khd", d_score, queries)
    d_value = einsum("hgqk,qhgd->khd", probs_low, d_attended)
    d_query = unrotate(d_query_rot.reshape(length, -1, HEAD_DIM), cosine, sine)
    d_key = unrotate(d_key_rot, cosine, sine)
    d_joined = jnp.concatenate(
        [part.reshape(length, -1).astype(low) for part in (d_query, d_key, d_value)], axis=1
    )
    d_inputs, output, gain_attn_term = last(
        n_ctx,
        n_fsdp,
        product_t(d_joined, w_joined).astype(low),
        product(hidden, w_down).astype(low),
        own_tokens,
        resid,
        d_resid,
        gain_attn,
    )
    grad_out = tokens_t(attended_low, d_resid_low).astype(low)
    grad_joined = tokens_t(normed_attn, d_joined).astype(low)
    grad_gate, grad_up, grad_down, grad_attn = tail(
        n_ctx, n_fsdp, grad_gate, grad_up, grad_down, grad_joined, grad_out
    )
    grad_attn = grad_attn.reshape(n_ctx, rows_model, -1)
    grad_query, grad_key, grad_value, grad_out = spread(
        grad_attn, (query_width, kv_width, kv_width, out_width), (1, sharers, sharers, 1)
    )

    terms = lax.psum(jnp.concatenate([gain_attn_term, gain_mlp_term]), ("ctx", "fsdp"))
    terms = lax.dynamic_slice_in_dim(terms, lax.axis_index("fsdp") * rows_model, rows_model, 1)
    return (
        output[None],
        d_inputs[None],
        terms[0],
        grad_query,
        grad_key,
        grad_value,
        grad_out,
        terms[1],
        grad_gate.astype(jnp.float32),
        grad_up.astype(jnp.float32),
        grad_down.astype(jnp.float32),
    )


def solution(mesh):
    return jax.shard_map(
        on_device,
        mesh=mesh,
        in_specs=(
            P("fsdp", "ctx", None),
            P("fsdp", "ctx", None),
            P(),
            P("fsdp"),
            P("fsdp", None),
            P("fsdp", None),
            P("fsdp", None),
            P("fsdp", None),
            P("fsdp"),
            P("fsdp", None),
            P("fsdp", None),
            P("fsdp", None),
        ),
        out_specs=(
            P("fsdp", "ctx", None),
            P("fsdp", "ctx", None),
            P("fsdp"),
            P("fsdp", None),
            P("fsdp", None),
            P("fsdp", None),
            P("fsdp", None),
            P("fsdp"),
            P("fsdp", None),
            P("fsdp", None),
            P("fsdp", None),
        ),
        check_vma=False,
    )
```

time: 1330 us -> 897 us (0.67)
  waiting for transfers between devices: 826 us -> 35 us
  Pallas kernels: 0 us -> 527 us
  local copies, waits for them, and re-layouts: 197 us -> 44.4 us
  other arithmetic: 77.2 us -> 57.8 us
  starting transfers between devices: 14.7 us -> 28.7 us
    pallas_call x0 -> x6, Pallas kernels: none -> 527 us  [the longest x5 522 us: communicate(): pl.pallas_call(kernel, out_shape=outs, in_specs=in_specs, out_specs=out_s...]
    unnamed x16 -> x5, waiting for transfers between devices: 313 us -> 0.08 us
    all_gather x7 -> x2, waiting for transfers between devices: 232 us -> 0.01 us  [gather(): return lax.all_gather(array, axis, axis=0, tiled=True)]
    reduce_scatter x5 -> x3, waiting for transfers between devices: 105 us -> 0.06 us  [scatter_sum(): return lax.psum_scatter(array, axis, scatter_dimension=0, tiled=True)]
    unnamed x128 -> x106, local copies, waits for them, and re-layouts: 110 us -> 18.9 us
    dot_general x12 -> x6, matrix products: 113 us -> 36 us  [einsum(): return jnp.einsum(spec, left, right, preferred_element_type=jnp.float32)]
    all_gather x2 -> x0, waiting for transfers between devices: 64 us -> none  [the longest x1 32.3 us: on_device(): grad_attn = lax.all_gather(grad_attn, 'ctx', axis=0).astype(jnp.float32)]
    ppermute x6 -> x9, waiting for transfers between devices: 89.1 us -> 34.9 us  [by_permutes(): lax.ppermute(piece, axis, [(i, (i + shift) % count) for i in range(count)])]
  transfers between devices with their start and end apart: 23 -> 14, of which waited for: 20 -> 6; matrix products, arithmetic and copies ran while one was open for 15% -> 18% of each run, Pallas kernels for 0% -> 27%
where the time goes in v2:
time: 897 us; the launch traced here: 892 us
  Pallas kernels  527 us (59%)
  matrix products  144 us (16%)
  other arithmetic  57.8 us (6%)
  local copies, waits for them, and re-layouts  44.4 us (5%)
  blocking collectives  39.4 us (4%)
  waiting for transfers between devices  35 us (4%)
  starting transfers between devices  28.7 us (3%)
  between operations  14.9 us (2%)
    pallas_call x5, Pallas kernels, communicate(): pl.pallas_call(kernel, out_shape=outs, in_specs=in_specs, out_specs=out_s...  522 us
    dot_general x5, matrix products, product_t(): lax.dot_general(left, right, (((1,), (1,)), ((), ())), preferred_element_...  40.8 us
    psum x1, blocking collectives, on_device(): lax.psum(jnp.concatenate([gain_attn_term, gain_mlp_term]), ('ctx', 'fsdp'))  39.4 us
    dot_general x6, matrix products, einsum(): return jnp.einsum(spec, left, right, preferred_element_type=jnp.float32)  36 us
    dot_general x5, matrix products, product(): return jnp.dot(left, right, preferred_element_type=jnp.float32)  35 us
    ppermute x9, waiting for transfers between devices, by_permutes(): lax.ppermute(piece, axis, [(i, (i + shift) % count) for i in range(count)])  34.9 us
    dot_general x5, matrix products, tokens_t(): lax.dot_general(left, right, (((0,), (0,)), ((), ())), preferred_element_...  32.4 us
    ppermute x9, starting transfers between devices, by_permutes(): lax.ppermute(piece, axis, [(i, (i + shift) % count) for i in range(count)])  28.5 us
  transfers between devices with their start and end apart: 14, of which 6 were waited for; matrix products, arithmetic and copies ran while one was open for 18% of the time, Pallas kernels for 27%

profile of v2, /device:TPU:17, one launch (start us, length us, event | category | flops | bytes accessed | tf_op | source)
XLA Modules:
  0.0 891.6 jit_solution(13706028729724169988)
XLA Ops:
  10.9 73.2 %front.1 = (bf16[1024,2048]{1,0:T(8,128)(2,1)}, bf16[2048,256]{1,0:T(8,128)(2,1)S(1)}, bf16[2048,128]{1,0:T(8,128)(2,1)S(1)}, f32[32,512]{1,0:T(8,128)S(1)}, bf1...) custom-call(bf16[128,2048]{1,0:T(8,128)(2,1)S(1)} %bitcast.174, bf16[512,2048]{1,0:T(8,128)(2,1)} %w_query.1, ...), custom_call_target="tpu_custom_call" | custom-call | bytes 150000000 | tf_op jit(solution)/shard_map/front/pallas_call | solution.py:351
  85.4 2.1 fusion.61
  87.5 15.7 %collective-permute-start.6 = (bf16[64,2048]{1,0:T(8,128)(2,1)S(1)}, bf16[64,2048]{1,0:T(8,128)(2,1)S(1)}, u32[]{:S(2)}, u32[]{:S(2)}) collective-permute-start(bf16[64,2048]{1,0:T(8,128)(2,1)S(1)} %get-tuple-element.100), channel_id=1, source_target_pairs={{0,1},{1,2},{2,3},{3,0},{4,5},{5,6},{6,7},{7,4},{8,9},{9,10},{10,1... | collective-permute-start | bytes 786440 | tf_op jit(solution)/shard_map/ppermute | solution.py:103
  104.2 2.4 collective-permute-start.8
  106.6 4.6 collective-permute-done.6
  113.6 8.3 collective-permute-done.7
  123.5 3.2 collective-permute-done.8
  129.6 2.0 fusion.60
  132.0 2.8 collective-permute-start.4
  134.8 5.6 collective-permute-done.3
  141.0 8.4 collective-permute-done.4
  150.1 4.9 collective-permute-done.5
  155.8 2.3 collective-permute-start.2
  158.1 3.8 collective-permute-start.1
  162.3 3.2 fusion.7
  165.8 2.1 fusion.21
  170.7 3.0 fusion.4
  173.7 4.2 fusion.6
  179.9 5.6 fusion.17
  186.3 3.3 convolution_convert_fusion.4.part
  192.0 79.1 %middle.1 = (f32[128,2048]{1,0:T(8,128)S(1)}, bf16[512,2048]{1,0:T(8,128)(2,1)S(1)}) custom-call(bf16[1024,2048]{1,0:T(8,128)(2,1)} %convolution_convert_fusion.4.part, bf16[128,2048]{1,0:T(8,128)(2,1)S(1)} %bitcast.175, f32[1,2048]{1,0:T(1,128)S(1)} %bitcast.184), custom_call_target="tpu_custom_call" | custom-call | bytes 180000000 | tf_op jit(solution)/shard_map/middle/pallas_call | solution.py:351
  271.1 2.3 constant_dynamic-update-slice_fusion.10
  277.1 10.6 %fusion.66 = f32[512,2048]{1,0:T(8,128)} fusion(bf16[512,2048]{1,0:T(8,128)(2,1)} %constant_dynamic-update-slice_fusion.8, bf16[2048,2048]{1,0:T(8,128)(2,1)} %param.27), kind=kOutput, calls=%fused_computation.124 | convolution fusion | flops 4294967296 | bytes 14680064 | tf_op jit(solution)/shard_map/dot_general | solution.py:61
  287.7 10.5 %fusion.67 = f32[512,2048]{1,0:T(8,128)} fusion(bf16[512,2048]{1,0:T(8,128)(2,1)} %copy-done.15, bf16[2048,2048]{1,0:T(8,128)(2,1)} %all-gather.5.cloned.1.call-done), kind=kOutput, calls=%fused_computation.125 | convolution fusion | flops 4294967296 | bytes 14680064 | tf_op jit(solution)/shard_map/dot_general | solution.py:57
  298.2 14.3 %multiply_convert_fusion = (bf16[512,2048]{1,0:T(8,128)(2,1)S(1)}, bf16[512,2048]{1,0:T(8,128)(2,1)}, bf16[512,2048]{1,0:T(8,128)(2,1)}) fusion(f32[512,2048]{1,0:T(8,128)} %fusion.67, f32[512,2048]{1,0:T(8,128)} %fusion.66, bf16[512,2048]{1,0:T(8,128)(2,1)} %copy-done.15, bf16[2048,2048]{1,0:T(8,128)(2,1)} %all-gather.3.cloned.1.call-done), kind=kOutput, calls=%fused_computation.25 | convolution fusion | flops 4310695936 | bytes 25165824 | tf_op jit(solution)/shard_map/dot_general | solution.py:57
  313.9 8.3 convolution_convert_fusion
  322.3 10.7 %fusion.68 = f32[512,2048]{1,0:T(8,128)} fusion(bf16[512,2048]{1,0:T(8,128)(2,1)} %get-tuple-element.93, bf16[2048,2048]{1,0:T(8,128)(2,1)} %all-gather.3.cloned.1.call-done), kind=kOutput, calls=%fused_computation.126 | convolution fusion | flops 4294967296 | bytes 14680064 | tf_op jit(solution)/shard_map/dot_general | solution.py:61
  333.0 7.0 convolution_convert_fusion.1
  340.0 10.4 %convolution_convert_fusion.2 = bf16[2048,2048]{1,0:T(8,128)(2,1)} fusion(bf16[512,2048]{1,0:T(8,128)(2,1)} %copy-done.15, bf16[512,2048]{1,0:T(8,128)(2,1)} %get-tuple-element.92), kind=kOutput, calls=%fused_computation.23 | convolution fusion | flops 4299161600 | bytes 12582912 | tf_op jit(solution)/shard_map/dot_general | solution.py:67
  350.4 11.1 %add_convert_fusion.part = bf16[512,2048]{1,0:T(8,128)(2,1)} fusion(f32[512,2048]{1,0:T(8,128)} %fusion.68, bf16[512,2048]{1,0:T(8,128)(2,1)} %get-tuple-element.92, bf16[2048,2048]{1,0:T(8,128)(2,1)} %all-gather.5.cloned.1.call-done), kind=kOutput, calls=%fused_computation.26 | convolution fusion | flops 4297064448 | bytes 16777216 | tf_op jit(solution)/shard_map/dot_general | solution.py:61
  363.2 66.9 %turn.1 = (f32[128,2048]{1,0:T(8,128)S(1)}, bf16[1024,2048]{1,0:T(8,128)(2,1)}, f32[1,2048]{1,0:T(1,128)S(1)}) custom-call(bf16[512,2048]{1,0:T(8,128)(2,1)S(1)} %copy-done.3, bf16[128,2048]{1,0:T(8,128)(2,1)S(1)} %bitcast.181, f32[128,2048]{1,0:T(8,128)S(1)} %get-tuple-element.74.resid, f32[1,2048]{1,0:T(1,128)S(1)} %bitcast.185), custom_call_target="tpu_custom_call" | custom-call | bytes 195000000 | tf_op jit(solution)/shard_map/turn/pallas_call | solution.py:351
  430.1 4.0 convolution_convert_fusion.8
  434.1 13.8 %fusion = (f32[4,1024]{1,0:T(4,128)S(1)}, f32[1024,1024,4]{1,0,2:T(8,128)}) fusion(f32[4,1024]{1,0:T(4,128)S(1)} %fusion.6, f32[4,1024]{1,0:T(4,128)S(1)} %get-tuple-element.121, f32[1024,1024,4]{1,0,2:T(8,128)} %copy-done.17, pred[1024,1024]{0,1:T(8,128)(4,1)} %copy-done.18, bf16[1024,4,64]{0,2,1:T(8,128)(2,1)S(1)} %bitcast.201, f32[1024,384]{0,1:T(8,128)} %copy-done.24), kind=kOutput, calls=%fused_computation.3 | convolution fusion | flops 566226944 | bytes 35307520 | tf_op jit(solution)/shard_map/qhgd,khd->hgqk/dot_general | solution.py:92
  448.0 12.7 %fusion.10 = bf16[4,1024,1024]{1,2,0:T(8,128)(2,1)S(1)} fusion(f32[1024,1024,4]{1,0,2:T(8,128)} %get-tuple-element.124, f32[4,1024]{1,0:T(4,128)S(1)} %get-tuple-element.123, f32[4,1024]{1,0:T(4,128)S(1)} %fusion.6, f32[4,1024]{1,0:T(4,128)S(1)} %get-tuple-element.121, f32[1024,1024,4]{1,0,2:T(8,128)} %copy-done.17, pred[1024,1024]{0,1:T(8,128)(4,1)S(1)} %copy-done.19), kind=kLoop, calls=%fused_computation.16 | loop fusion | flops 37748736 | bytes 43040768 | tf_op jit(solution)/shard_map/reshape.83
  464.0 2.7 bitcast_multiply_fusion.4
  466.8 9.4 %fusion.29 = bf16[1024,64]{0,1:T(8,128)(2,1)S(1)} fusion(bf16[1024,4,64]{0,2,1:T(8,128)(2,1)S(1)} %bitcast.202, f32[4,1024]{1,0:T(4,128)S(1)} %fusion.6, f32[4,1024]{1,0:T(4,128)S(1)} %get-tuple-element.121, f32[1024,1024,4]{1,0,2:T(8,128)} %copy-done.17, pred[1024,1024]{0,1:T(8,128)(4,1)S(1)} %copy-done.19), kind=kOutput, calls=%fused_computation.45 | convolution fusion | flops 562102272 | bytes 18513920 | tf_op jit(solution)/shard_map/hgqk,qhgd->khd/dot_general | solution.py:92
  476.2 4.4 convolution_convert_fusion.3.part
  480.6 4.7 convolution_convert_fusion.5.down_part
  485.3 91.4 %last.1 = (bf16[128,2048]{1,0:T(8,128)(2,1)S(1)}, bf16[128,2048]{1,0:T(8,128)(2,1)S(1)}, f32[1,2048]{1,0:T(1,128)S(1)}) custom-call(bf16[1024,2048]{1,0:T(8,128)(2,1)} %convolution_convert_fusion.3.part, bf16[512,2048]{1,0:T(8,128)(2,1)S(1)} %convolution_convert_fusion.5.down_part, bf16[128,2048]{1,0:T(8,128)(2,1)S(1)} %bitcast.176, ...), custom_call_target="tpu_custom_call" | custom-call | bytes 135000000 | tf_op jit(solution)/shard_map/last/pallas_call | solution.py:351
  578.3 39.4 %psum.7 = f32[2,2048]{1,0:T(2,128)S(1)} all-reduce(f32[2,2048]{1,0:T(2,128)S(1)} %pad_maximum_fusion.7), channel_id=1, replica_groups=mesh['ctx'=8,'fsdp'=4] {'ctx','fsdp'}, use_global_device_ids=true, to_apply=%region_5.6 | all-reduce | flops 4096 | bytes 32768 | tf_op jit(solution)/shard_map/psum | solution.py:866
  618.4 3.9 convolution_convert_fusion.7.out_part
  622.4 2.8 convolution_convert_fusion.6.joined
  628.9 211.2 %tail.1 = (bf16[512,8192]{1,0:T(8,128)(2,1)}, bf16[512,8192]{1,0:T(8,128)(2,1)}, bf16[2048,2048]{1,0:T(8,128)(2,1)}, bf16[4096,640]{1,0:T(8,128)(2,1)}) custom-call(bf16[256,2048]{1,0:T(8,128)(2,1)S(1)} %copy-done.6, bf16[256,2048]{1,0:T(8,128)(2,1)S(1)} %copy-done.7, bf16[256,2048]{1,0:T(8,128)(2,1)S(1)} %copy-done.5, ...), custom_call_target="tpu_custom_call" | custom-call | bytes 450000000 | tf_op jit(solution)/shard_map/tail/pallas_call | solution.py:351
  840.1 2.5 copy-done
  842.6 5.3 spread.1
  847.9 11.7 %convert_element_type.150 = f32[512,8192]{1,0:T(8,128)} convert(bf16[512,8192]{1,0:T(8,128)(2,1)} %get-tuple-element.88) | non-fusion elementwise | flops 4194304 | bytes 25165824 | tf_op jit(solution)/shard_map/convert_element_type | solution.py:877
  859.7 11.7 %convert_element_type.151 = f32[512,8192]{1,0:T(8,128)} convert(bf16[512,8192]{1,0:T(8,128)(2,1)} %get-tuple-element.89) | non-fusion elementwise | flops 4194304 | bytes 25165824 | tf_op jit(solution)/shard_map/convert_element_type | solution.py:878
  871.4 11.8 %convert_element_type.152 = f32[2048,2048]{1,0:T(8,128)} convert(bf16[2048,2048]{1,0:T(8,128)(2,1)} %get-tuple-element.90) | non-fusion elementwise | flops 4194304 | bytes 25165824 | tf_op jit(solution)/shard_map/convert_element_type | solution.py:879
  (169 shorter events, 41.5 us)
Async XLA Ops:
  7.2 280.5 %all-gather.5.cloned.1.call-start = ((), (), s32[]{:S(2)}) async-start(), calls=%async_computation.4 | async-start | bytes 9437184 | tf_op jit(solution)/shard_map/all_gather | solution.py:84
  84.2 101.3 %copy-start.8 = (bf16[256,2048]{1,0:T(8,128)(2,1)}, bf16[256,2048]{1,0:T(8,128)(2,1)S(1)}, u32[]{:S(2)}) copy-start(bf16[256,2048]{1,0:T(8,128)(2,1)S(1)} %get-tuple-element.69) | copy-start | bytes 3145732
  87.5 23.7 %collective-permute-start.6 = (bf16[64,2048]{1,0:T(8,128)(2,1)S(1)}, bf16[64,2048]{1,0:T(8,128)(2,1)S(1)}, u32[]{:S(2)}, u32[]{:S(2)}) collective-permute-start(bf16[64,2048]{1,0:T(8,128)(2,1)S(1)} %get-tuple-element.100), channel_id=1, source_target_pairs={{0,1},{1,2},{2,3},{3,0},{4,5},{5,6},{6,7},{7,4},{8,9},{9,10},{10,1... | collective-permute-start | bytes 786440 | tf_op jit(solution)/shard_map/ppermute | solution.py:103
  103.2 18.7 %collective-permute-start.7 = (bf16[64,2048]{1,0:T(8,128)(2,1)}, bf16[64,2048]{1,0:T(8,128)(2,1)}, u32[]{:S(2)}, u32[]{:S(2)}) collective-permute-start(bf16[64,2048]{1,0:T(8,128)(2,1)} %get-tuple-element.99), channel_id=1, source_target_pairs={{0,2},{1,3},{2,0},{3,1},{4,6},{5,7},{6,4},{7,5},{8,10},{9,11},{10,... | collective-permute-start | bytes 786440 | tf_op jit(solution)/shard_map/ppermute | solution.py:103
  104.2 22.5 %collective-permute-start.8 = (bf16[64,2048]{1,0:T(8,128)(2,1)S(1)}, bf16[64,2048]{1,0:T(8,128)(2,1)}, u32[]{:S(2)}, u32[]{:S(2)}) collective-permute-start(bf16[64,2048]{1,0:T(8,128)(2,1)S(1)} %get-tuple-element.98), channel_id=1, source_target_pairs={{0,3},{1,0},{2,1},{3,2},{4,7},{5,4},{6,5},{7,6},{8,11},{9,8},{10,9... | collective-permute-start | bytes 786440 | tf_op jit(solution)/shard_map/ppermute | solution.py:103
  111.8 44.0 %copy-start.4 = (bf16[1,128,2048]{2,1,0:T(8,128)(2,1)S(1)}, bf16[1,128,2048]{2,1,0:T(8,128)(2,1)}, u32[]{:S(2)}) copy-start(bf16[1,128,2048]{2,1,0:T(8,128)(2,1)} %param.17) | copy-start | bytes 1572868
  111.8 50.2 %copy-start.45 = (s32[8,2]{0,1:T(2,128)S(1)}, s32[8,2]{0,1:T(2,128)}, u32[]{:S(2)}) copy-start(s32[8,2]{0,1:T(2,128)} %param.18) | copy-start | bytes 196
  128.4 169.8 %all-gather.3.cloned.1.call-start = ((), (), s32[]{:S(2)}) async-start(), calls=%async_computation.3 | async-start | bytes 9437184 | tf_op jit(solution)/shard_map/all_gather | solution.py:84
  131.6 8.8 collective-permute-start.3
  132.0 17.4 %collective-permute-start.4 = (bf16[64,2048]{1,0:T(8,128)(2,1)S(1)}, bf16[64,2048]{1,0:T(8,128)(2,1)S(1)}, u32[]{:S(2)}, u32[]{:S(2)}) collective-permute-start(bf16[64,2048]{1,0:T(8,128)(2,1)S(1)} %get-tuple-element.95), channel_id=1, source_target_pairs={{0,2},{1,3},{2,0},{3,1},{4,6},{5,7},{6,4},{7,5},{8,10},{9,11},{10,... | collective-permute-start | bytes 786440 | tf_op jit(solution)/shard_map/ppermute | solution.py:103
  134.8 20.3 %collective-permute-start.5 = (bf16[64,2048]{1,0:T(8,128)(2,1)S(1)}, bf16[64,2048]{1,0:T(8,128)(2,1)S(1)}, u32[]{:S(2)}, u32[]{:S(2)}) collective-permute-start(bf16[64,2048]{1,0:T(8,128)(2,1)S(1)} %get-tuple-element.94), channel_id=1, source_target_pairs={{0,3},{1,0},{2,1},{3,2},{4,7},{5,4},{6,5},{7,6},{8,11},{9,8},{10,9... | collective-permute-start | bytes 786440 | tf_op jit(solution)/shard_map/ppermute | solution.py:103
  155.8 469.4 %reduce-scatter.8.cloned.1.call-start = ((), (), s32[]{:S(2)}) async-start(), calls=%async_computation.7 | async-start | bytes 9437184 | tf_op jit(solution)/shard_map/reduce_scatter | solution.py:88
  155.8 119.4 %collective-permute-start.2 = (bf16[128,2048]{1,0:T(8,128)(2,1)S(1)}, bf16[128,2048]{1,0:T(8,128)(2,1)}, u32[]{:S(2)}, u32[]{:S(2)}) collective-permute-start(bf16[128,2048]{1,0:T(8,128)(2,1)S(1)} %bitcast.177), channel_id=1, source_target_pairs={{0,3},{1,0},{2,1},{3,2},{4,7},{5,4},{6,5},{7,6},{8,11},{9,8},{10,9... | collective-permute-start | bytes 1572872 | tf_op jit(solution)/shard_map/ppermute | solution.py:103
  158.1 115.3 %collective-permute-start.1 = (bf16[128,2048]{1,0:T(8,128)(2,1)S(1)}, bf16[128,2048]{1,0:T(8,128)(2,1)}, u32[]{:S(2)}, u32[]{:S(2)}) collective-permute-start(bf16[128,2048]{1,0:T(8,128)(2,1)S(1)} %bitcast.178), channel_id=1, source_target_pairs={{0,2},{1,3},{2,0},{3,1},{4,6},{5,7},{6,4},{7,5},{8,10},{9,11},{10,... | collective-permute-start | bytes 1572872 | tf_op jit(solution)/shard_map/ppermute | solution.py:103
  161.9 109.2 %collective-permute-start = (bf16[128,2048]{1,0:T(8,128)(2,1)S(1)}, bf16[128,2048]{1,0:T(8,128)(2,1)}, u32[]{:S(2)}, u32[]{:S(2)}) collective-permute-start(bf16[128,2048]{1,0:T(8,128)(2,1)S(1)} %bitcast.179), channel_id=1, source_target_pairs={{0,1},{1,2},{2,3},{3,0},{4,5},{5,6},{6,7},{7,4},{8,9},{9,10},{10,1... | collective-permute-start | bytes 1572872 | tf_op jit(solution)/shard_map/ppermute | solution.py:103
  162.3 3.6 copy-start.25
  165.5 2.4 copy-start.43
  165.5 2.4 copy-start.13
  165.8 2.2 copy-start.36
  168.0 10.0 %copy-start.24 = (f32[1024,384]{0,1:T(8,128)}, f32[1024,384]{0,1:T(8,128)S(1)}, u32[]{:S(2)}) copy-start(f32[1024,384]{0,1:T(8,128)S(1)} %fusion.21) | copy-start | bytes 4718596
  168.9 1.7 copy-start.27
  168.9 1.8 copy-start.38
  170.6 7.3 copy-start.18
  173.7 6.2 copy-start.17
  186.3 5.7 copy-start.2
  271.1 4.2 copy-start.15
  322.2 303.0 %reduce-scatter.4.cloned.1.call-start = ((), (), s32[]{:S(2)}) async-start(), calls=%async_computation.5 | async-start | bytes 9437184 | tf_op jit(solution)/shard_map/reduce_scatter | solution.py:88
  322.3 10.7 %copy-start.16 = (bf16[512,2048]{1,0:T(8,128)(2,1)S(1)}, bf16[512,2048]{1,0:T(8,128)(2,1)}, u32[]{:S(2)}) copy-start(bf16[512,2048]{1,0:T(8,128)(2,1)} %copy-done.15) | copy-start | bytes 6291460
  322.3 10.7 %copy-start.48 = (bf16[512,2048]{1,0:T(8,128)(2,1)S(1)}, bf16[512,2048]{1,0:T(8,128)(2,1)}, u32[]{:S(2)}) copy-start(bf16[512,2048]{1,0:T(8,128)(2,1)} %get-tuple-element.93) | copy-start | bytes 6291460
  361.5 263.7 %reduce-scatter.6.cloned.1.call-start = ((), (), s32[]{:S(2)}) async-start(), calls=%async_computation.6 | async-start | bytes 9437184 | tf_op jit(solution)/shard_map/reduce_scatter | solution.py:88
  434.1 13.8 %copy-start.19 = (pred[1024,1024]{0,1:T(8,128)(4,1)S(1)}, pred[1024,1024]{0,1:T(8,128)(4,1)}, u32[]{:S(2)}) copy-start(pred[1024,1024]{0,1:T(8,128)(4,1)} %copy-done.18) | copy-start | bytes 3145732
  448.0 12.8 %copy-start.30 = (f32[1024,64]{0,1:T(8,128)S(1)}, f32[1024,64]{0,1:T(8,128)}, u32[]{:S(2)}) copy-start(f32[1024,64]{0,1:T(8,128)} %copy-done.29) | copy-start | bytes 786436
  448.0 12.8 %copy-start.39 = (bf16[1024,64,1]{0,1,2:T(8,128)(2,1)S(1)}, bf16[1024,64,1]{0,1,2:T(8,128)(2,1)}, u32[]{:S(2)}) copy-start(bf16[1024,64,1]{0,1,2:T(8,128)(2,1)} %copy-done.38) | copy-start | bytes 393220
  462.4 1.6 copy-start.23
  462.4 1.6 copy-start.32
  464.0 12.2 %copy-start.40 = (bf16[1024,256]{0,1:T(8,128)(2,1)}, bf16[1024,256]{0,1:T(8,128)(2,1)S(1)}, u32[]{:S(2)}) copy-start(bf16[1024,256]{0,1:T(8,128)(2,1)S(1)} %fusion.35) | copy-start | bytes 1572868
  464.0 2.7 copy-start.34
  464.0 16.6 %slice-start = ((s8[8388608]{0:T(1024)(128)(4,1)}), s8[4194304]{0:T(1024)(128)(4,1)S(1)}, s32[]{:S(2)}) async-start(s8[8388608]{0:T(1024)(128)(4,1)} %bitcast.199), calls=%async_computation.8 | async-start | bytes 8388608
  466.7 9.4 %copy-start.37 = (bf16[2048,384]{1,0:T(8,128)(2,1)S(1)}, bf16[2048,384]{1,0:T(8,128)(2,1)}, u32[]{:S(2)}) copy-start(bf16[2048,384]{1,0:T(8,128)(2,1)} %copy-done.36) | copy-start | bytes 4718596
  466.7 13.8 %slice-start.1 = ((s8[8388608]{0:T(1024)(128)(4,1)}), s8[4194304]{0:T(1024)(128)(4,1)S(1)}, s32[]{:S(2)}) async-start(s8[8388608]{0:T(1024)(128)(4,1)} %bitcast.199), calls=%async_computation.9 | async-start | bytes 8388608
  476.2 4.4 copy-start.47
  480.6 4.7 copy-start.14
  578.3 44.0 %copy-start.41 = (bf16[1024,256]{0,1:T(8,128)(2,1)S(1)}, bf16[1024,256]{0,1:T(8,128)(2,1)}, u32[]{:S(2)}) copy-start(bf16[1024,256]{0,1:T(8,128)(2,1)} %copy-done.40) | copy-start | bytes 1572868
  578.3 44.0 %copy-start.44 = (f32[1024]{0:T(1024)S(1)}, f32[1024]{0:T(1024)}, u32[]{:S(2)}) copy-start(f32[1024]{0:T(1024)} %copy-done.43) | copy-start | bytes 12292
  617.7 4.6 copy-start.26
  840.1 2.5 copy-start
  871.4 11.8 %copy-start.12 = (bf16[128,2048]{1,0:T(8,128)(2,1)S(1)}, bf16[128,2048]{1,0:T(8,128)(2,1)}, u32[]{:S(2)}) copy-start(bf16[128,2048]{1,0:T(8,128)(2,1)} %copy-done.11) | copy-start | bytes 1572868
  871.4 12.6 %copy-start.10 = (bf16[128,2048]{1,0:T(8,128)(2,1)S(1)}, bf16[128,2048]{1,0:T(8,128)(2,1)}, u32[]{:S(2)}) copy-start(bf16[128,2048]{1,0:T(8,128)(2,1)} %copy-done.9) | copy-start | bytes 1572868
  (17 other events, 17.4 us)
Sparse Core Ops, SparseCore 0:
  128.5 54.4 all-gather.4
  185.5 63.5 all-gather.2
  322.3 73.2 reduce-scatter.7
  399.9 78.6 reduce-scatter.3
  481.9 86.2 reduce-scatter.5

commit v3 on v2

--- a/solution.py
+++ b/solution.py
@@ -180,94 +180,115 @@
     return ref.at[pl.ds(pl.multiple_of(index * rows, rows), rows)]
 
 
-def cube_gather(links, ref, rows, between=None):
-    held, sent = [0], []
-    to_sibling = []
-
-    def share(offset):
+def in_turns(*walks):
+    for walk in walks:
+        next(walk, None)
+
+
+def finish(*walks):
+    for walk in walks:
+        for _ in walk:
+            pass
+
+
+def cube_gather(links, ref, rows):
+    held, sent, shared = [0], [], []
+
+    def send(offset, step):
         block = rows_of(ref, links.ctx + offset, rows)
-        copy = links.copy(block, block, links.ctx + links.sibling, links.fsdp)
+        copy = links.copy(block, block, links.ctx + step, links.fsdp)
         copy.start()
-        to_sibling.append(copy)
-
-    for stage, step in enumerate(links.order):
-        copies = []
-        for offset in held:
-            block = rows_of(ref, links.ctx + offset, rows)
-            copy = links.copy(block, block, links.ctx + step, links.fsdp)
-            copy.start()
-            copies.append(copy)
-        for offset in held if stage == 0 else held[len(held) // 2 :]:
-            share(offset)
-        if stage == 0 and between is not None:
-            between()
+        return copy
+
+    fresh = held
+    for step in links.order:
+        copies = [send(offset, step) for offset in held]
+        shared += [send(offset, links.sibling) for offset in fresh]
+        yield
         for copy in copies:
             copy.wait_recv()
         sent += copies
-        held = held + [offset + step for offset in held]
-    for offset in held[len(held) // 2 :] if links.order else held:
-        share(offset)
-    for copy in to_sibling:
+        fresh = [offset + step for offset in held]
+        held = held + fresh
+    shared += [send(offset, links.sibling) for offset in fresh]
+    yield
+    for copy in shared:
         copy.wait_recv()
-    for copy in sent + to_sibling:
+    for copy in sent + shared:
         copy.wait_send()
 
 
-def cube_slots(n_ctx):
-    return n_ctx - 1
-
-
-def cube_sum(links, part, stage_ref, land, rows):
-    offsets = [0]
-    theirs = [0]
+def in_rows(rows, body):
+    size = math.gcd(rows, 64)
+
+    def step(at, carry):
+        body(pl.multiple_of(at * size, size), size)
+        return carry
+
+    lax.fori_loop(0, rows // size, step, 0)
+
+
+def cube_sum(links, part, staged, land, acc, rows):
+    offsets, theirs = [0], [0]
     for step, other in zip(links.order, links.order[::-1]):
         offsets = offsets + [offset + step for offset in offsets]
         theirs = theirs + [offset + other for offset in theirs]
-    sent = []
-    copies = []
+    wide = jnp.float32
+    sent, pending = [], []
     for at, offset in enumerate(theirs):
         source = rows_of(part, links.ctx + links.sibling + offset, rows)
-        copy = links.copy(source, land.at[pl.ds(at * rows, rows)], links.ctx + links.sibling, links.fsdp)
+        target = land.at[pl.ds(at * rows, rows)]
+        copy = links.copy(source, target, links.ctx + links.sibling, links.fsdp)
         copy.start()
-        copies.append(copy)
-    sums = {}
-    stage_at, land_at = 0, len(offsets)
-    pending = copies
-    first = True
+        pending.append(copy)
+    yield
+    stage_at, land_from, land_at = 0, 0, len(offsets)
     for level in range(len(links.order) + 1):
-        last = level == len(links.order)
         count = len(offsets)
         half = count // 2
-        step = None if last else links.order[len(links.order) - 1 - level]
         onward = []
-        for at in list(range(half, count)) + list(range(half)) if not last else [0]:
+        for at in list(range(half, count)) + list(range(half)):
             pending[at].wait_recv()
-            if first:
-                base = rows_of(part, links.ctx + offsets[at], rows)[...].astype(jnp.float32)
-            else:
-                base = sums[at]
-            start = pending_land + at * rows if not first else at * rows
-            total = base + land[pl.ds(start, rows), :].astype(jnp.float32)
-            if not last and at >= half:
-                slot = stage_ref.at[pl.ds(stage_at * rows, rows)]
-                slot[...] = total.astype(LOW)
-                copy = links.copy(
-                    slot, land.at[pl.ds((land_at + at - half) * rows, rows)], links.ctx + step, links.fsdp
-                )
+            first, place = level == 0, (land_from + at) * rows
+            goes = at >= half and count > 1
+
+            def add(start, size, at=at, place=place, first=first, goes=goes, slot=stage_at * rows):
+                landed = land[pl.ds(place + start, size), :].astype(wide)
+                if first:
+                    base = (links.ctx + offsets[at]) * rows
+                    mine = part[pl.ds(pl.multiple_of(base + start, size), size), :].astype(wide)
+                else:
+                    mine = acc[pl.ds(at * rows + start, size), :]
+                if goes:
+                    staged[pl.ds(slot + start, size), :] = (mine + landed).astype(LOW)
+                else:
+                    acc[pl.ds(at * rows + start, size), :] = mine + landed
+
+            in_rows(rows, add)
+            if goes:
+                source = staged.at[pl.ds(stage_at * rows, rows)]
+                target = land.at[pl.ds((land_at + at - half) * rows, rows)]
+                step = links.order[len(links.order) - 1 - level]
+                copy = links.copy(source, target, links.ctx + step, links.fsdp)
                 copy.start()
                 onward.append(copy)
                 stage_at += 1
-            else:
-                sums[at] = total
         sent += pending
-        pending = onward
-        pending_land = land_at * rows
+        pending, land_from = onward, land_at
         land_at += half
-        offsets = offsets[:half] if not last else offsets
-        first = False
+        offsets = offsets[: max(half, 1)]
+        if level < len(links.order):
+            yield
     for copy in sent:
         copy.wait_send()
-    return sums[0]
+
+
+def cube_scratch(n_ctx, rows, width):
+    return [
+        pltpu.VMEM((max(1, n_ctx // 2 - 1) * rows, width), LOW),
+        pltpu.VMEM(((n_ctx - 1) * rows, width), LOW),
+        pltpu.VMEM((max(1, n_ctx // 4) * rows, width), jnp.float32),
+    ]
 
 
 def line_gather(links, refs, rows):
@@ -286,17 +307,14 @@
             pl.when(down_ok)(down.start)
             sends += [(up_ok, up), (down_ok, down)]
             receives += [(me >= hop + 1, up), (me <= count - 2 - hop, down)]
+        yield
         for ok, copy in receives:
             pl.when(ok)(copy.wait_recv)
-
-    def finish():
-        for ok, copy in sends:
-            pl.when(ok)(copy.wait_send)
-
-    return finish
-
-
-def line_sum(links, part, stage_ref, land, total, rows):
+    for ok, copy in sends:
+        pl.when(ok)(copy.wait_send)
+
+
+def line_sum(links, part, staged, land, total, rows):
     count, me = links.n_fsdp, links.fsdp
     flows = []
     for hop in range(count - 1):
@@ -304,47 +322,64 @@
             goal = count - 1 - hop if side == 0 else hop
             slot = (side * (count - 1) + hop) * rows
             landing = land.at[pl.ds(slot, rows)]
-            staging = stage_ref.at[pl.ds(slot, rows)]
+            staging = staged.at[pl.ds(slot, rows)]
             onward = links.copy(staging, landing, links.ctx, me + 1 if side == 0 else me - 1)
             fed = me > 0 if side == 0 else me < count - 1
             passes = me < goal if side == 0 else me > goal
-            flows.append((side, goal, landing, staging, onward, fed, passes))
-    for side, goal, landing, staging, onward, fed, passes in flows:
+            flows.append((goal * rows, slot, onward, fed, passes, me == goal))
+    for base, slot, onward, fed, passes, _ in flows:
 
         @pl.when(jnp.logical_and(passes, jnp.logical_not(fed)))
         def _():
-            staging[...] = part[pl.ds(goal * rows, rows), :]
+            staged[pl.ds(slot, rows), :] = part[pl.ds(base, rows), :]
             onward.start()
 
-    def steps():
-        total[...] = rows_of(part, me, rows)[...].astype(jnp.float32)
-        lower = me < count // 2
+    total[...] = rows_of(part, me, rows)[...].astype(jnp.float32)
+    lower = me < count // 2
+    for hop in range(count - 1):
+        yield
         for near in (0, 1):
 
             @pl.when(lower if near == 0 else jnp.logical_not(lower))
             def _():
-                for hop in range(count - 1):
-                    for way in (near, 1 - near):
-                        side, goal, landing, staging, onward, fed, passes = flows[2 * hop + way]
-
-                        @pl.when(jnp.logical_and(passes, fed))
-                        def _():
-                            onward.wait_recv()
-                            own = part[pl.ds(goal * rows, rows), :].astype(jnp.float32)
-                            staging[...] = (own + landing[...].astype(jnp.float32)).astype(LOW)
-                            onward.start()
-
-        for side, goal, landing, staging, onward, fed, passes in flows:
-
-            @pl.when(jnp.logical_and(me == goal, fed))
-            def _():
-                onward.wait_recv()
-                total[...] += landing[...].astype(jnp.float32)
-
-        for side, goal, landing, staging, onward, fed, passes in flows:
-            pl.when(passes)(onward.wait_send)
-
-    return steps
+                for way in (near, 1 - near):
+                    base, slot, onward, fed, passes, _ = flows[2 * hop + way]
+
+                    @pl.when(jnp.logical_and(passes, fed))
+                    def _():
+                        onward.wait_recv()
+
+                        def add(start, size):
+                            own = part[pl.ds(base + start, size), :].astype(jnp.float32)
+                            landed = land[pl.ds(slot + start, size), :].astype(jnp.float32)
+                            staged[pl.ds(slot + start, size), :] = (own + landed).astype(LOW)
+
+                        in_rows(rows, add)
+                        onward.start()
+
+    yield
+    for base, slot, onward, fed, passes, mine in flows:
+
+        @pl.when(jnp.logical_and(mine, fed))
+        def _():
+            onward.wait_recv()
+
+            def add(start, size):
+                landed = land[pl.ds(slot + start, size), :].astype(jnp.float32)
+                total[pl.ds(start, size), :] += landed
+
+            in_rows(rows, add)
+
+    for base, slot, onward, fed, passes, _ in flows:
+        pl.when(passes)(onward.wait_send)
+
+
+def line_scratch(n_fsdp, rows, width):
+    return [
+        pltpu.VMEM((2 * (n_fsdp - 1) * rows, width), LOW),
+        pltpu.VMEM((2 * (n_fsdp - 1) * rows, width), LOW),
+        pltpu.VMEM((rows, width), jnp.float32),
+    ]
 
 
 def communicate(kernel, collective_id, name, operands, in_specs, outs, out_specs, scratch, copies, busy):
@@ -401,13 +436,11 @@
     links.greet(plane=True, line=True)
     for copy in local:
         copy.wait()
-    ends = []
-
-    def between():
-        refs = [gains_all, q_all, kv_all, cols_all]
-        ends.append(line_gather(links, refs, [gains.shape[0]] + [weight_rows] * 3))
-
-    cube_gather(links, seq, rows, between)
+    plane = cube_gather(links, seq, rows)
+    line = line_gather(links, [gains_all, q_all, kv_all], [gains.shape[0], weight_rows, weight_rows])
+    later = line_gather(links, [cols_all], [weight_rows])
+    in_turns(plane, line, later, plane, line, plane, later, line, later)
+    finish(later)
     column = cut(out_rows, out_width)
     mine = pltpu.make_async_copy(rows_of(cols_all, links.ctx, head_rows), column, local_sems.at[0])
     mine.start()
@@ -417,11 +450,10 @@
         copy = links.copy(rows_of(cols_all, target, head_rows), column, target, links.fsdp)
         copy.start()
         copies.append(copy)
+    finish(plane, line)
     for copy in copies:
         copy.wait()
     mine.wait()
-    for end in ends:
-        end()
 
 
 def front(n_ctx, n_fsdp, own, w_query, kv, w_out, gains):
@@ -452,17 +484,18 @@
 
 
 def middle_kernel(
-    n_ctx, n_fsdp, part, own, gain, resid, normed, staged, land, send_sems, recv_sems
+    n_ctx, n_fsdp, part, own, gain, resid, normed, staged, land, acc, send_sems, recv_sems
 ):
     links = Links(n_ctx, n_fsdp, send_sems, recv_sems)
     rows = own.shape[0]
     links.greet(cube=True, line=True)
-    value = cube_sum(links, part, staged, land, rows) + own[...].astype(jnp.float32)
+    finish(cube_sum(links, part, staged, land, acc, rows))
+    value = acc[pl.ds(0, rows), :] + own[...].astype(jnp.float32)
     resid[...] = value
     scale = lax.rsqrt(jnp.mean(value * value, axis=1, keepdims=True) + EPS)
     block = swap_order((value * scale * gain[...]).astype(LOW), n_fsdp, n_ctx)
     rows_of(normed, links.fsdp, rows)[...] = block
-    line_gather(links, [normed], [rows])()
+    finish(line_gather(links, [normed], [rows]))
 
 
 def middle(n_ctx, n_fsdp, part, own, gain):
@@ -478,22 +511,40 @@
             jax.ShapeDtypeStruct((rows * n_fsdp, width), LOW),
         ],
         [VMEM] * 2,
-        [
-            pltpu.VMEM(((n_ctx // 2 - 1) * rows, width), LOW),
-            pltpu.VMEM(((n_ctx - 1) * rows, width), LOW),
-        ],
+        cube_scratch(n_ctx, rows, width),
         n_ctx - 1 + 2 * (n_fsdp - 1),
         60,
     )
 
 
 def turn_kernel(
-    n_ctx, n_fsdp, part, upstream, resid, gain, d_resid, seq, term, staged, land, total, send_sems, recv_sems
+    n_ctx,
+    n_fsdp,
+    part,
+    down_part,
+    upstream,
+    resid,
+    gain,
+    d_resid,
+    seq,
+    down,
+    term,
+    line_staged,
+    line_land,
+    total,
+    staged,
+    land,
+    acc,
+    send_sems,
+    recv_sems,
 ):
     links = Links(n_ctx, n_fsdp, send_sems, recv_sems)
-    rows = upstream.shape[0]
+    rows, down_rows = upstream.shape[0], down.shape[0]
     links.greet(cube=True, line=True)
-    line_sum(links, part, staged, land, total, rows)()
+    line = line_sum(links, part, line_staged, line_land, total, rows)
+    plane = cube_sum(links, down_part, staged, land, acc, down_rows)
+    in_turns(line, plane, plane, line, line, plane)
+    finish(line)
     d_normed = swap_order(total[...], n_ctx, n_fsdp)
     value = resid[...]
     scale = lax.rsqrt(jnp.mean(value * value, axis=1, keepdims=True) + EPS)
@@ -502,29 +553,31 @@
     value = upstream[...].astype(jnp.float32) + norm_back(d_normed, gain[...], unit, scale)
     d_resid[...] = value
     rows_of(seq, links.ctx, rows)[...] = value.astype(LOW)
-    cube_gather(links, seq, rows)
-
-
-def turn(n_ctx, n_fsdp, part, upstream, resid, gain):
+    spread_out = cube_gather(links, seq, rows)
+    in_turns(spread_out)
+    finish(plane)
+    down[...] = acc[pl.ds(0, down_rows), :].astype(LOW)
+    finish(spread_out)
+
+
+def turn(n_ctx, n_fsdp, part, down_part, upstream, resid, gain):
     rows, width = upstream.shape
+    down_rows = down_part.shape[0] // n_ctx
     return communicate(
         functools.partial(turn_kernel, n_ctx, n_fsdp),
         3,
         "turn",
-        (part, upstream, resid, gain),
-        [VMEM] * 4,
+        (part, down_part, upstream, resid, gain),
+        [VMEM] * 5,
         [
             jax.ShapeDtypeStruct((rows, width), jnp.float32),
             jax.ShapeDtypeStruct((rows * n_ctx, width), LOW),
+            jax.ShapeDtypeStruct((down_rows, width), LOW),
             jax.ShapeDtypeStruct((1, width), jnp.float32),
         ],
-        [VMEM] * 3,
-        [
-            pltpu.VMEM((2 * (n_fsdp - 1) * rows, width), LOW),
-            pltpu.VMEM((2 * (n_fsdp - 1) * rows, width), LOW),
-            pltpu.VMEM((rows, width), jnp.float32),
-        ],
-        n_ctx - 1 + 2 * (n_fsdp - 1),
+        [VMEM] * 4,
+        line_scratch(n_fsdp, rows, width) + cube_scratch(n_ctx, down_rows, width),
+        2 * (n_ctx - 1) + 2 * (n_fsdp - 1),
         65,
     )
 
@@ -543,6 +596,7 @@
     term,
     staged,
     land,
+    acc,
     down_staged,
     down_land,
     total,
@@ -552,14 +606,17 @@
     links = Links(n_ctx, n_fsdp, send_sems, recv_sems)
     rows = own.shape[0]
     links.greet(cube=True, line=True)
-    finish = line_sum(links, down_part, down_staged, down_land, total, rows)
-    d_normed = cube_sum(links, part, staged, land, rows)
+    line = line_sum(links, down_part, down_staged, down_land, total, rows)
+    plane = cube_sum(links, part, staged, land, acc, rows)
+    in_turns(plane, line, plane, line, plane)
+    finish(plane)
+    d_normed = acc[pl.ds(0, rows), :]
     value = own[...].astype(jnp.float32)
     scale = lax.rsqrt(jnp.mean(value * value, axis=1, keepdims=True) + EPS)
     unit = value * scale
     term[...] = jnp.sum(d_normed * unit, axis=0, keepdims=True)
     d_own[...] = (d_resid[...] + norm_back(d_normed, gain[...], unit, scale)).astype(LOW)
-    finish()
+    finish(line)
     output[...] = (resid[...] + total[...]).astype(LOW)
 
 
@@ -577,13 +634,7 @@
             jax.ShapeDtypeStruct((1, width), jnp.float32),
         ],
         [VMEM] * 3,
-        [
-            pltpu.VMEM(((n_ctx // 2 - 1) * rows, width), LOW),
-            pltpu.VMEM(((n_ctx - 1) * rows, width), LOW),
-            pltpu.VMEM((2 * (n_fsdp - 1) * rows, width), LOW),
-            pltpu.VMEM((2 * (n_fsdp - 1) * rows, width), LOW),
-            pltpu.VMEM((rows, width), jnp.float32),
-        ],
+        cube_scratch(n_ctx, rows, width) + line_scratch(n_fsdp, rows, width),
         n_ctx - 1 + 2 * (n_fsdp - 1),
         45,
     )
@@ -597,6 +648,7 @@
     down,
     joined,
     out_part,
+    terms,
     gate_all,
     up_all,
     down_all,
@@ -612,9 +664,12 @@
 ):
     links = Links(n_ctx, n_fsdp, send_sems, recv_sems)
     strip, ff_rows = gate.shape[0] // n_fsdp, gate.shape[1]
-    down_rows, rows = down.shape[0], joined.shape[0] // n_fsdp
+    down_rows, model_rows = down.shape[0], joined.shape[0] // n_fsdp
+    term_rows = terms.shape[0] // n_fsdp
+    rows = model_rows + term_rows
     head_rows, joined_width = out_part.shape[0], joined.shape[1]
     out_width = attn_part.shape[1] - joined_width
+    heads_in = model_rows // head_rows
 
     def place(ref, ctx, fsdp):
         return ref.at[
@@ -625,62 +680,88 @@
     def out_column(ctx):
         return out_part.at[:, pl.ds(pl.multiple_of(ctx * out_width, out_width), out_width)]
 
-    def out_place(ctx):
-        return attn_part.at[
-            pl.ds(pl.multiple_of(ctx * head_rows, head_rows), head_rows), pl.ds(joined_width, out_width)
-        ]
-
-    local = [
+    out_from = (links.ctx // heads_in) * rows + lax.rem(links.ctx, heads_in) * head_rows
+    out_place = attn_part.at[
+        pl.ds(pl.multiple_of(out_from, 16), head_rows), pl.ds(joined_width, out_width)
+    ]
+    moves = [
         (down, rows_of(down_all, links.ctx, down_rows)),
         (rows_of(gate, links.fsdp, strip), place(gate_all, links.ctx, links.fsdp)),
         (rows_of(up, links.fsdp, strip), place(up_all, links.ctx, links.fsdp)),
-        (joined, attn_part.at[:, pl.ds(0, joined_width)]),
-        (out_column(links.ctx), out_place(links.ctx)),
+        (out_column(links.ctx), out_place),
     ]
-    local = [pltpu.make_async_copy(a, b, local_sems.at[i]) for i, (a, b) in enumerate(local)]
+    for fsdp in range(n_fsdp):
+        moves.append(
+            (
+                joined.at[pl.ds(fsdp * model_rows, model_rows)],
+                attn_part.at[pl.ds(fsdp * rows, model_rows), pl.ds(0, joined_width)],
+            )
+        )
+        moves.append(
+            (
+                terms.at[pl.ds(fsdp * term_rows, term_rows)],
+                attn_part.at[pl.ds(fsdp * rows + model_rows, term_rows)],
+            )
+        )
+    local = [pltpu.make_async_copy(a, b, local_sems.at[i]) for i, (a, b) in enumerate(moves)]
     for copy in local:
         copy.start()
     links.greet(plane=True, line=True, whole_line=True)
-    to_shards, to_plane = [], []
-    for shift in range(1, n_fsdp):
-        target = lax.rem(links.fsdp + shift, n_fsdp)
-        for source, goal in ((gate, gate_all), (up, up_all)):
+    local[0].wait()
+    plane_down = cube_gather(links, down_all, down_rows)
+    to_shards = []
+    for source, goal in ((gate, gate_all), (up, up_all)):
+        copies = []
+        for shift in range(1, n_fsdp):
+            target = lax.rem(links.fsdp + shift, n_fsdp)
             copy = links.copy(
                 rows_of(source, target, strip), place(goal, links.ctx, links.fsdp), links.ctx, target
             )
             copy.start()
-            to_shards.append(copy)
+            copies.append(copy)
+        to_shards.append(copies)
+    to_plane = []
     for shift in range(1, n_ctx):
         target = lax.rem(links.ctx + shift, n_ctx)
-        copy = links.copy(out_column(target), out_place(links.ctx), target, links.fsdp)
+        copy = links.copy(out_column(target), out_place, target, links.fsdp)
         copy.start()
         to_plane.append(copy)
-    for copy in local:
+    in_turns(plane_down)
+    for copy in local[1:]:
         copy.wait()
-    cube_gather(links, down_all, down_rows)
-    for copy in to_plane + to_shards:
+    for copy in to_plane:
         copy.wait()
-    finish = line_sum(links, attn_part, staged, land, total, rows)
-    cube_gather(links, gate_all, strip, finish)
-    cube_gather(links, up_all, strip)
+    line = line_sum(links, attn_part, staged, land, total, rows)
+    in_turns(plane_down)
+    for copy in to_shards[0]:
+        copy.wait()
+    plane_gate = cube_gather(links, gate_all, strip)
+    in_turns(plane_gate, plane_down)
+    for copy in to_shards[1]:
+        copy.wait()
+    plane_up = cube_gather(links, up_all, strip)
+    in_turns(line, plane_up, plane_gate, line, line, plane_gate, plane_up, line)
+    finish(line)
     attn_low[...] = total[...].astype(LOW)
     mine = pltpu.make_async_copy(attn_low, rows_of(attn_all, links.ctx, rows), local_sems.at[0])
     mine.start()
     mine.wait()
-    cube_gather(links, attn_all, rows)
-
-
-def tail(n_ctx, n_fsdp, gate, up, down, joined, out_part):
+    plane_attn = cube_gather(links, attn_all, rows)
+    in_turns(plane_attn, plane_up, plane_attn)
+    finish(plane_down, plane_gate, plane_up, plane_attn)
+
+
+def tail(n_ctx, n_fsdp, gate, up, down, joined, out_part, terms):
     strip, ff_rows = gate.shape[0] // n_fsdp, gate.shape[1]
-    rows = joined.shape[0] // n_fsdp
+    rows = (joined.shape[0] + terms.shape[0]) // n_fsdp
     attn_width = joined.shape[1] + out_part.shape[1] // n_ctx
     shape = lambda *dims: jax.ShapeDtypeStruct(dims, LOW)
     return communicate(
         functools.partial(tail_kernel, n_ctx, n_fsdp),
         5,
         "tail",
-        (gate, up, down, joined, out_part),
-        [ANY] * 5,
+        (gate, up, down, joined, out_part, terms),
+        [ANY] * 6,
         [
             shape(strip * n_ctx, ff_rows * n_fsdp),
             shape(strip * n_ctx, ff_rows * n_fsdp),
@@ -688,14 +769,9 @@
             shape(rows * n_ctx, attn_width),
         ],
         [ANY] * 4,
-        [
-            pltpu.VMEM((rows * n_fsdp, attn_width), LOW),
-            pltpu.VMEM((2 * (n_fsdp - 1) * rows, attn_width), LOW),
-            pltpu.VMEM((2 * (n_fsdp - 1) * rows, attn_width), LOW),
-            pltpu.VMEM((rows, attn_width), jnp.float32),
-            pltpu.VMEM((rows, attn_width), LOW),
-            pltpu.SemaphoreType.DMA((5,)),
-        ],
+        [pltpu.VMEM((rows * n_fsdp, attn_width), LOW)]
+        + line_scratch(n_fsdp, rows, attn_width)
+        + [pltpu.VMEM((rows, attn_width), LOW), pltpu.SemaphoreType.DMA((4 + 2 * n_fsdp,))],
         5 * (n_ctx - 1) + 4 * (n_fsdp - 1),
         150,
     )
@@ -714,8 +790,8 @@
         at += width
 
 
-def spread(gathered, widths, sharers):
-    n_ctx, rows, joined = gathered.shape
+def spread(gathered, rows, widths, sharers):
+    n_ctx, _, joined = gathered.shape
     step = 2 * max(sharers)
     tile = min(rows, 256)
     return pl.pallas_call(
@@ -731,6 +807,294 @@
         compiler_params=pltpu.CompilerParams(vmem_limit_bytes=32 << 20),
         name="spread",
     )(gathered)
+
+
+def lanes(shape):
+    return lax.broadcasted_iota(jnp.int32, shape, 1)
+
+
+def halves(tensor, back):
+    half = HEAD_DIM // 2
+    width = tensor.shape[1]
+    later, earlier = pltpu.roll(tensor, width - half, 1), pltpu.roll(tensor, half, 1)
+    first = lanes(tensor.shape) % HEAD_DIM < half
+    return jnp.where(first, later, -earlier) if back else jnp.where(first, -later, earlier)
+
+
+def turned(tensor, cosine, sine, back=False):
+    parts = []
+    for at in range(0, tensor.shape[1], 128):
+        piece = tensor[:, at : at + 128]
+        if back:
+            parts.append(piece * cosine + halves(piece * sine, True))
+        else:
+            parts.append(piece * cosine + halves(piece, False) * sine)
+    return parts[0] if len(parts) == 1 else jnp.concatenate(parts, axis=1)
+
+
+def dot(left, right):
+    return jnp.dot(left, right, preferred_element_type=jnp.float32)
+
+
+def dot_dims(left, right, left_dim, right_dim):
+    dims = (((left_dim,), (right_dim,)), ((), ()))
+    return lax.dot_general(left, right, dims, preferred_element_type=jnp.float32)
+
+
+def pick(ref, order, first, count, block):
+    rows = [
+        ref[pl.ds(pl.multiple_of(order[first + i] * block, block), block), :] for i in range(count)
+    ]
+    return rows[0] if count == 1 else jnp.concatenate(rows, axis=0)
+
+
+def project(seq, order, gain, w_q, w_kv, cosine, sine, normed, q_heads, k_head, v_head, block, tile):
+    kv_width = w_kv.shape[1] // 2
+
+    def step(at, carry):
+        rows = pl.ds(pl.multiple_of(at * tile, tile), tile)
+        wide = pick(seq, order, at * (tile // block), tile // block, block).astype(jnp.float32)
+        scale = lax.rsqrt(jnp.mean(wide * wide, axis=1, keepdims=True) + EPS)
+        low = (wide * scale * gain[...]).astype(LOW)
+        normed[rows, :] = low
+        cos, sin = cosine[rows, :], sine[rows, :]
+        queries = turned(dot(low, w_q[...]), cos, sin).astype(LOW)
+        for head in range(q_heads.shape[0]):
+            q_heads[head, rows, :] = queries[:, head * HEAD_DIM : (head + 1) * HEAD_DIM]
+        both = dot(low, w_kv[...])
+        keys = turned(both, cos, sin).astype(LOW)
+        both = both.astype(LOW)
+        for head in range(k_head.shape[0]):
+            cut = head * HEAD_DIM
+            k_head[head, rows, :] = keys[:, cut : cut + HEAD_DIM]
+            v_head[head, rows, :] = both[:, kv_width + cut : kv_width + cut + HEAD_DIM]
+        return carry
+
+    lax.fori_loop(0, normed.shape[0] // tile, step, 0)
+
+
+def scores_of(queries, keys, tile):
+    logits = dot_dims(queries, keys, 1, 1) * (HEAD_DIM**-0.5)
+    last = logits[:, -tile:]
+    seen = lax.broadcasted_iota(jnp.int32, last.shape, 0) >= lanes(last.shape)
+    last = jnp.where(seen, last, -1e30)
+    before = logits.shape[1] - tile
+    return last if before == 0 else jnp.concatenate([logits[:, :before], last], axis=1)
+
+
+def attend(q_heads, k_head, v_head, out_heads, logs, tile, service):
+    heads, length, _ = q_heads.shape
+    group = heads // k_head.shape[0]
+    for tile_at in range(length // tile):
+        here, keys = pl.ds(tile_at * tile, tile), (tile_at + 1) * tile
+        logs[here, :] = jnp.zeros((tile, logs.shape[1]), jnp.float32)
+
+        def step(head, carry):
+            scores = scores_of(q_heads[head, here, :], k_head[head // group, pl.ds(0, keys), :], tile)
+            largest = jnp.max(scores, axis=1, keepdims=True)
+            expo = jnp.exp(scores - largest)
+            total = jnp.sum(expo, axis=1, keepdims=True)
+            probs = (expo * (1.0 / total)).astype(LOW)
+            out = dot(probs, v_head[head // group, pl.ds(0, keys), :])
+            out_heads[head, here, :] = out.astype(LOW)
+            log = largest + jnp.log(total)
+            logs[here, :] += jnp.where(lanes((tile, logs.shape[1])) == head, log, 0.0)
+            return carry
+
+        lax.fori_loop(0, heads, step, 0)
+        service()
+
+
+def attend_back(q_heads, k_head, v_head, d_heads, logs, dq_heads, dk_head, dv_head, tile, service):
+    heads, length, _ = q_heads.shape
+    group = heads // k_head.shape[0]
+    dk_head[...] = jnp.zeros_like(dk_head)
+    dv_head[...] = jnp.zeros_like(dv_head)
+    for tile_at in range(length // tile):
+        here, keys = pl.ds(tile_at * tile, tile), (tile_at + 1) * tile
+
+        def step(head, carry):
+            queries, d_out = q_heads[head, here, :], d_heads[head, here, :]
+            kept, seen = k_head[head // group, pl.ds(0, keys), :], v_head[head // group, pl.ds(0, keys), :]
+            column = lanes((tile, logs.shape[1])) == head
+            log = jnp.sum(jnp.where(column, logs[here, :], 0.0), axis=1, keepdims=True)
+            probs = jnp.exp(scores_of(queries, kept, tile) - log)
+            d_probs = dot_dims(d_out, seen, 1, 1)
+            delta = jnp.sum(probs * d_probs, axis=1, keepdims=True)
+            d_score = (probs * (d_probs - delta) * (HEAD_DIM**-0.5)).astype(LOW)
+            dq_heads[head, here, :] = dot(d_score, kept)
+            dk_head[head // group, pl.ds(0, keys), :] += dot_dims(d_score, queries, 0, 0)
+            dv_head[head // group, pl.ds(0, keys), :] += dot_dims(probs.astype(LOW), d_out, 0, 0)
+            return carry
+
+        lax.fori_loop(0, heads, step, 0)
+        service()
+
+
+def side_by_side(ref, rows):
+    return jnp.concatenate([ref[head, rows, :] for head in range(ref.shape[0])], axis=1)
+
+
+def split_heads(value, ref, rows):
+    for head in range(ref.shape[0]):
+        ref[head, rows, :] = value[:, head * HEAD_DIM : (head + 1) * HEAD_DIM]
+
+
+def attention_kernel(
+    block,
+    tile,
+    order,
+    place,
+    seq,
+    gain,
+    w_q,
+    w_kv,
+    w_out,
+    cosine,
+    sine,
+    normed,
+    q_heads,
+    k_head,
+    v_head,
+    logs,
+    attended,
+    part,
+    out_heads,
+):
+    project(seq, order, gain, w_q, w_kv, cosine, sine, normed, q_heads, k_head, v_head, block, tile)
+    attend(q_heads, k_head, v_head, out_heads, logs, tile, lambda: None)
+    length = normed.shape[0]
+
+    def join(at, carry):
+        rows = pl.ds(pl.multiple_of(at * tile, tile), tile)
+        attended[rows, :] = side_by_side(out_heads, rows)
+        return carry
+
+    lax.fori_loop(0, length // tile, join, 0)
+
+    def out(at, carry):
+        rows = pl.ds(pl.multiple_of(at * tile, tile), tile)
+        mine = pick(attended, place, at * (tile // block), tile // block, block)
+        part[rows, :] = dot(mine, w_out[...]).astype(LOW)
+        return carry
+
+    lax.fori_loop(0, length // tile, out, 0)
+
+
+def attention(block, order, place, seq, gain, w_q, w_kv, w_out, cosine, sine):
+    length, width = seq.shape
+    heads, kv_heads = w_q.shape[1] // HEAD_DIM, w_kv.shape[1] // (2 * HEAD_DIM)
+    tile = 4 * block
+    shape = jax.ShapeDtypeStruct
+    SMEM = pl.BlockSpec(memory_space=pltpu.SMEM)
+    return pl.pallas_call(
+        functools.partial(attention_kernel, block, tile),
+        in_specs=[SMEM, SMEM] + [VMEM] * 7,
+        out_specs=[VMEM] * 7,
+        out_shape=[
+            shape((length, width), LOW),
+            shape((heads, length, HEAD_DIM), LOW),
+            shape((kv_heads, length, HEAD_DIM), LOW),
+            shape((kv_heads, length, HEAD_DIM), LOW),
+            shape((length, 128), jnp.float32),
+            shape((length, heads * HEAD_DIM), LOW),
+            shape((length, width), LOW),
+        ],
+        scratch_shapes=[pltpu.VMEM((heads, length, HEAD_DIM), LOW)],
+        compiler_params=pltpu.CompilerParams(vmem_limit_bytes=48 << 20),
+        cost_estimate=pl.CostEstimate(flops=0, bytes_accessed=90_000_000, transcendentals=0),
+        name="attention",
+    )(order, place, seq, gain, w_q, w_kv, w_out, cosine, sine)
+
+
+def back_kernel(
+    block,
+    tile,
+    order,
+    place,
+    d_seq,
+    w_q,
+    w_kv,
+    w_out,
+    cosine,
+    sine,
+    q_heads,
+    k_head,
+    v_head,
+    logs,
+    d_sorted,
+    d_joined,
+    part,
+    d_heads,
+    dq_heads,
+    dk_head,
+    dv_head,
+):
+    length = d_seq.shape[0]
+    query_width = w_q.shape[1]
+    kv_width = w_kv.shape[1] // 2
+
+    def begin(at, carry):
+        rows = pl.ds(pl.multiple_of(at * tile, tile), tile)
+        mine = pick(d_seq, order, at * (tile // block), tile // block, block)
+        d_sorted[rows, :] = mine
+        split_heads(dot_dims(mine, w_out[...], 1, 1).astype(LOW), d_heads, rows)
+        return carry
+
+    lax.fori_loop(0, length // tile, begin, 0)
+    attend_back(
+        q_heads, k_head, v_head, d_heads, logs, dq_heads, dk_head, dv_head, tile, lambda: None
+    )
+
+    def end(at, carry):
+        rows = pl.ds(pl.multiple_of(at * tile, tile), tile)
+        cos, sin = cosine[rows, :], sine[rows, :]
+        d_query = turned(side_by_side(dq_heads, rows), cos, sin, True)
+        d_joined[rows, pl.ds(0, query_width)] = d_query.astype(LOW)
+        both = jnp.concatenate([side_by_side(dk_head, rows), side_by_side(dv_head, rows)], axis=1)
+        keys = lanes(both.shape) < kv_width
+        both = jnp.where(keys, turned(both, cos, sin, True), both)
+        d_joined[rows, pl.ds(query_width, 2 * kv_width)] = both.astype(LOW)
+        return carry
+
+    lax.fori_loop(0, length // tile, end, 0)
+
+    def out(at, carry):
+        rows = pl.ds(pl.multiple_of(at * tile, tile), tile)
+        mine = pick(d_joined, place, at * (tile // block), tile // block, block)
+        total = dot_dims(mine[:, :query_width], w_q[...], 1, 1)
+        total += dot_dims(mine[:, query_width:], w_kv[...], 1, 1)
+        part[rows, :] = total.astype(LOW)
+        return carry
+
+    lax.fori_loop(0, length // tile, out, 0)
+
+
+def attention_back(block, order, place, d_seq, w_q, w_kv, w_out, cosine, sine, q_heads, k_head, v_head, logs):
+    length, width = d_seq.shape
+    heads, kv_heads = q_heads.shape[0], k_head.shape[0]
+    tile = 4 * block
+    shape = jax.ShapeDtypeStruct
+    SMEM = pl.BlockSpec(memory_space=pltpu.SMEM)
+    return pl.pallas_call(
+        functools.partial(back_kernel, block, tile),
+        in_specs=[SMEM, SMEM] + [VMEM] * 10,
+        out_specs=[VMEM] * 3,
+        out_shape=[
+            shape((length, width), LOW),
+            shape((length, w_q.shape[1] + w_kv.shape[1]), LOW),
+            shape((length, width), LOW),
+        ],
+        scratch_shapes=[
+            pltpu.VMEM((heads, length, HEAD_DIM), LOW),
+            pltpu.VMEM((heads, length, HEAD_DIM), jnp.float32),
+            pltpu.VMEM((kv_heads, length, HEAD_DIM), jnp.float32),
+            pltpu.VMEM((kv_heads, length, HEAD_DIM), jnp.float32),
+        ],
+        compiler_params=pltpu.CompilerParams(vmem_limit_bytes=48 << 20),
+        cost_estimate=pl.CostEstimate(flops=0, bytes_accessed=150_000_000, transcendentals=0),
+        name="attention_back",
+    )(order, place, d_seq, w_q, w_kv, w_out, cosine, sine, q_heads, k_head, v_head, logs)
 
 
 def on_device(
@@ -760,7 +1124,6 @@
     kv_here = max(1, heads_kv // n_ctx)
     sharers = max(1, n_ctx // heads_kv)
     kv_width = kv_here * HEAD_DIM
-    group = query_width // kv_width
     kv_start = (ctx // sharers) * kv_width
 
     def columns(matrix, start, size):
@@ -788,31 +1151,16 @@
     up_full = gather(strips(w_up), "ctx")
     upstream_all = by_permutes(lambda fsdp: upstream, "fsdp")
 
-    all_pos = slot_positions(pairing, length, tok_rows // 2)
-    cosine, sine = rotation(all_pos, HEAD_DIM)
-    factor = HEAD_DIM ** (-0.5)
-    wide = sequence.astype(jnp.float32)
-    scale_attn = lax.rsqrt(jnp.mean(wide * wide, axis=1, keepdims=True) + EPS)
-    normed_attn = (wide * scale_attn * gain_attn).astype(low)
-    w_joined = jnp.concatenate([w_q, w_kv], axis=1)
-    projected = product(normed_attn, w_joined)
-    query_pre = projected[:, :query_width].reshape(length, -1, HEAD_DIM)
-    key_pre = projected[:, query_width : query_width + kv_width].reshape(length, -1, HEAD_DIM)
-    values = projected[:, query_width + kv_width :].reshape(length, -1, HEAD_DIM).astype(low)
-    queries = rotate(query_pre, cosine, sine).astype(low).reshape(length, kv_here, group, HEAD_DIM)
-    keys = rotate(key_pre, cosine, sine).astype(low)
-    logits = einsum("qhgd,khd->hgqk", queries, keys)
-    allowed = all_pos[None, :] <= all_pos[:, None]
-    scores = jnp.where(allowed, logits * factor, -1e30)
-    largest = jnp.max(scores, axis=-1, keepdims=True)
-    expo = jnp.where(allowed, jnp.exp(scores - largest), 0.0)
-    probs = expo / jnp.sum(expo, axis=-1, keepdims=True)
-    probs_low = probs.astype(low)
-    attended = einsum("hgqk,khd->qhgd", probs_low, values)
-    attended_low = attended.reshape(length, query_width).astype(low)
-    resid, normed_mlp = middle(
-        n_ctx, n_fsdp, product(attended_low, w_out_rows).astype(low), own_tokens, gain_mlp
-    )
+    block = tok_rows // pairing.shape[1]
+    place = pairing.reshape(-1)
+    blocks = jnp.arange(place.shape[0], dtype=jnp.int32)
+    order = jnp.sum(jnp.where(place[None, :] == blocks[:, None], blocks[None, :], 0), axis=1)
+    cosine, sine = rotation(jnp.arange(length, dtype=jnp.int32), HEAD_DIM)
+    cosine, sine = [jnp.tile(t[:, 0], (1, 128 // HEAD_DIM)) for t in (cosine, sine)]
+    normed_attn, q_heads, k_head, v_head, logs, attended_low, part = attention(
+        block, order, place, sequence, gain_attn, w_q, w_kv, w_out_rows, cosine, sine
+    )
+    resid, normed_mlp = middle(n_ctx, n_fsdp, part, own_tokens, gain_mlp)
 
     gate_pre = product(normed_mlp, gate_full)
     up_pre = product(normed_mlp, up_full)
@@ -826,45 +1174,52 @@
     grad_gate = tokens_t(normed_mlp, d_gate).astype(low)
     grad_up = tokens_t(normed_mlp, d_up).astype(low)
     d_part, grad_gate, grad_up = lax.optimization_barrier((d_part, grad_gate, grad_up))
-    d_resid, d_resid_low, gain_mlp_term = turn(n_ctx, n_fsdp, d_part, upstream, resid, gain_mlp)
+    grad_down = tokens_t(hidden, upstream_all).astype(low)
+    d_resid, d_resid_low, grad_down, gain_mlp_term = turn(
+        n_ctx, n_fsdp, d_part, grad_down, upstream, resid, gain_mlp
+    )
     grad_gate, grad_up = scatter_sum(grad_gate, "ctx"), scatter_sum(grad_up, "ctx")
-    grad_down = scatter_sum(tokens_t(hidden, upstream_all).astype(low), "ctx")
-
-    d_attended = product_t(d_resid_low, w_out_rows).astype(low)
-    d_attended = d_attended.reshape(length, kv_here, group, HEAD_DIM)
-    d_probs = einsum("qhgd,khd->hgqk", d_attended, values)
-    delta = jnp.sum(probs * d_probs, axis=-1, keepdims=True)
-    d_score = (probs * (d_probs - delta) * factor).astype(low)
-    d_query_rot = einsum("hgqk,khd->qhgd", d_score, keys)
-    d_key_rot = einsum("hgqk,qhgd->khd", d_score, queries)
-    d_value = einsum("hgqk,qhgd->khd", probs_low, d_attended)
-    d_query = unrotate(d_query_rot.reshape(length, -1, HEAD_DIM), cosine, sine)
-    d_key = unrotate(d_key_rot, cosine, sine)
-    d_joined = jnp.concatenate(
-        [part.reshape(length, -1).astype(low) for part in (d_query, d_key, d_value)], axis=1
+
+    d_sorted, d_joined, part = attention_back(
+        block,
+        order,
+        place,
+        d_resid_low,
+        w_q,
+        w_kv,
+        w_out_rows,
+        cosine,
+        sine,
+        q_heads,
+        k_head,
+        v_head,
+        logs,
     )
     d_inputs, output, gain_attn_term = last(
         n_ctx,
         n_fsdp,
-        product_t(d_joined, w_joined).astype(low),
+        part,
         product(hidden, w_down).astype(low),
         own_tokens,
         resid,
         d_resid,
         gain_attn,
     )
-    grad_out = tokens_t(attended_low, d_resid_low).astype(low)
+    grad_out = tokens_t(attended_low, d_sorted).astype(low)
     grad_joined = tokens_t(normed_attn, d_joined).astype(low)
+    terms = jnp.concatenate([gain_attn_term, gain_mlp_term]).reshape(2, n_fsdp, rows_model)
+    attn_width = query_width + 2 * kv_width + out_width
+    pad = ((0, 0), (0, 14), (0, attn_width - rows_model))
+    terms = jnp.pad(terms.transpose(1, 0, 2).astype(low), pad).reshape(n_fsdp * 16, attn_width)
     grad_gate, grad_up, grad_down, grad_attn = tail(
-        n_ctx, n_fsdp, grad_gate, grad_up, grad_down, grad_joined, grad_out
-    )
-    grad_attn = grad_attn.reshape(n_ctx, rows_model, -1)
+        n_ctx, n_fsdp, grad_gate, grad_up, grad_down, grad_joined, grad_out, terms
+    )
+    grad_attn = grad_attn.reshape(n_ctx, rows_model + 16, attn_width)
+    terms = jnp.sum(grad_attn[:, rows_model : rows_model + 2, :rows_model].astype(jnp.float32), axis=0)
     grad_query, grad_key, grad_value, grad_out = spread(
-        grad_attn, (query_width, kv_width, kv_width, out_width), (1, sharers, sharers, 1)
-    )
-
-    terms = lax.psum(jnp.concatenate([gain_attn_term, gain_mlp_term]), ("ctx", "fsdp"))
-    terms = lax.dynamic_slice_in_dim(terms, lax.axis_index("fsdp") * rows_model, rows_model, 1)
+        grad_attn, rows_model, (query_width, kv_width, kv_width, out_width), (1, sharers, sharers, 1)
+    )
+
     return (
         output[None],
         d_inputs[None],

time: 897 us -> 755 us (0.84)
  matrix products: 144 us -> 92.6 us
  blocking collectives: 39.4 us -> 0 us
  other arithmetic: 57.8 us -> 36.1 us
  starting transfers between devices: 28.7 us -> 11.8 us
  Pallas kernels: 527 us -> 517 us
    pallas_call x5, Pallas kernels: 522 us -> 461 us  [communicate(): pl.pallas_call(kernel, out_shape=outs, in_specs=in_specs, out_specs=out_s...]
    pallas_call x0 -> x2, Pallas kernels: none -> 50.4 us  [the longest x1 26.8 us: attention_back(): pl.pallas_call(functools.partial(back_kernel, block, tile), in_specs=[SME...]
    psum x1 -> x0, blocking collectives: 39.4 us -> none  [on_device(): lax.psum(jnp.concatenate([gain_attn_term, gain_mlp_term]), ('ctx', 'fsdp'))]
    dot_general x6 -> x0, matrix products: 36 us -> none  [einsum(): return jnp.einsum(spec, left, right, preferred_element_type=jnp.float32)]
    ppermute x9, starting transfers between devices: 28.5 us -> 11.2 us  [by_permutes(): lax.ppermute(piece, axis, [(i, (i + shift) % count) for i in range(count)])]
    dot_general x5 -> x3, matrix products: 40.8 us -> 26.6 us  [product_t(): lax.dot_general(left, right, (((1,), (1,)), ((), ())), preferred_element_...]
    another operation x1 -> x2, other arithmetic: 12.7 us -> 0.02 us
    unnamed x106 -> x73, local copies, waits for them, and re-layouts: 18.9 us -> 22 us
  transfers between devices with their start and end apart: 14 -> 13, of which waited for: 6 -> 6; matrix products, arithmetic and copies ran while one was open for 18% -> 7% of each run, Pallas kernels for 27% -> 39%
where the time goes in v3:
time: 755 us; the launch traced here: 748 us
  Pallas kernels  517 us (68%)
  matrix products  92.6 us (12%)
  waiting for transfers between devices  40.1 us (5%)
  other arithmetic  36.1 us (5%)
  local copies, waits for them, and re-layouts  36 us (5%)
  between operations  14.6 us (2%)
  starting transfers between devices  11.8 us (2%)
    pallas_call x5, Pallas kernels, communicate(): pl.pallas_call(kernel, out_shape=outs, in_specs=in_specs, out_specs=out_s...  461 us
    ppermute x9, waiting for transfers between devices, by_permutes(): lax.ppermute(piece, axis, [(i, (i + shift) % count) for i in range(count)])  39.9 us
    dot_general x3, matrix products, product(): return jnp.dot(left, right, preferred_element_type=jnp.float32)  33 us
    dot_general x5, matrix products, tokens_t(): lax.dot_general(left, right, (((0,), (0,)), ((), ())), preferred_element_...  33 us
    pallas_call x1, Pallas kernels, attention_back(): pl.pallas_call(functools.partial(back_kernel, block, tile), in_specs=[SME...  26.8 us
    dot_general x3, matrix products, product_t(): lax.dot_general(left, right, (((1,), (1,)), ((), ())), preferred_element_...  26.6 us
    pallas_call x1, Pallas kernels, attention(): pl.pallas_call(functools.partial(attention_kernel, block, tile), in_specs...  23.6 us
    unnamed x73, local copies, waits for them, and re-layouts  22 us
  transfers between devices with their start and end apart: 13, of which 6 were waited for; matrix products, arithmetic and copies ran while one was open for 7% of the time, Pallas kernels for 39%

profile of v3, /device:TPU:17, one launch (start us, length us, event | category | flops | bytes accessed | tf_op | source)
XLA Modules:
  0.0 748.4 jit_solution(5430221004017157532)
XLA Ops:
  7.2 1.1 constant_dynamic-slice_fusion
  10.9 66.5 %front.1 = (bf16[1024,2048]{1,0:T(8,128)(2,1)}, bf16[2048,256]{1,0:T(8,128)(2,1)S(1)}, bf16[2048,128]{1,0:T(8,128)(2,1)S(1)}, f32[32,512]{1,0:T(8,128)S(1)}, bf1...) custom-call(bf16[128,2048]{1,0:T(8,128)(2,1)S(1)} %bitcast.42, bf16[512,2048]{1,0:T(8,128)(2,1)} %w_query.1, ...), custom_call_target="tpu_custom_call" | custom-call | bytes 150000000 | tf_op jit(solution)/shard_map/front/pallas_call | solution.py:386
  78.6 1.3 fusion.2
  79.9 2.3 collective-permute-start.6
  82.1 2.2 collective-permute-start.8
  84.4 4.3 collective-permute-done.6
  89.7 9.8 %collective-permute-done.7 = bf16[64,2048]{1,0:T(8,128)(2,1)} collective-permute-done((bf16[64,2048]{1,0:T(8,128)(2,1)S(1)}, bf16[64,2048]{1,0:T(8,128)(2,1)}, u32[]{:S(2)}, u32[]{:S(2)}) %collective-permute-start.7) | collective-permute-done | bytes 262176 | tf_op jit(solution)/shard_map/ppermute | solution.py:103
  100.5 4.4 collective-permute-done.8
  107.0 1.3 fusion.1
  108.4 2.0 collective-permute-start.3
  110.4 1.3 collective-permute-start.4
  111.6 5.2 collective-permute-done.3
  116.8 10.6 %collective-permute-done.4 = bf16[64,2048]{1,0:T(8,128)(2,1)S(1)} collective-permute-done((bf16[64,2048]{1,0:T(8,128)(2,1)S(1)}, bf16[64,2048]{1,0:T(8,128)(2,1)S(1)}, u32[]{:S(2)}, u32[]{:S(2)}) %collective-permute-start.4) | collective-permute-done | bytes 262176 | tf_op jit(solution)/shard_map/ppermute | solution.py:103
  127.4 5.6 collective-permute-done.5
  134.1 1.9 collective-permute-start
  136.0 1.5 collective-permute-start.1
  137.8 1.1 constant_dynamic-update-slice_fusion.8
  141.1 23.6 %attention.1 = (bf16[1024,2048]{1,0:T(8,128)(2,1)}, bf16[4,1024,64]{2,1,0:T(8,128)(2,1)S(1)}, bf16[1,1024,64]{2,1,0:T(8,128)(2,1)S(1)}, bf16[1,1024,64]{2,1,0:T(...) custom-call(s32[16]{0:T(128)S(1)} %select_reduce_fusion.order, ...), custom_call_target="tpu_custom_call" | custom-call | bytes 90000000 | tf_op jit(solution)/shard_map/attention/pallas_call | solution.py:990
  168.0 82.7 %middle.1 = (f32[128,2048]{1,0:T(8,128)S(1)}, bf16[512,2048]{1,0:T(8,128)(2,1)S(1)}) custom-call(bf16[1024,2048]{1,0:T(8,128)(2,1)} %get-tuple-element.81.part, bf16[128,2048]{1,0:T(8,128)(2,1)S(1)} %bitcast.43, f32[1,2048]{1,0:T(1,128)S(1)} %bitcast.50), custom_call_target="tpu_custom_call" | custom-call | bytes 180000000 | tf_op jit(solution)/shard_map/middle/pallas_call | solution.py:386
  251.6 1.4 copy-done.20
  253.0 1.1 constant_dynamic-update-slice_fusion.7
  254.1 1.1 constant_dynamic-update-slice_fusion.6
  255.2 1.1 constant_dynamic-update-slice_fusion.5
  256.3 1.4 copy-done.28
  257.7 9.4 %fusion.5 = f32[512,2048]{1,0:T(8,128)} fusion(bf16[512,2048]{1,0:T(8,128)(2,1)S(1)} %constant_dynamic-update-slice_fusion.5, bf16[2048,2048]{1,0:T(8,128)(2,1)} %param.27), kind=kOutput, calls=%fused_computation.42 | convolution fusion | flops 4294967296 | bytes 14680064 | tf_op jit(solution)/shard_map/dot_general | solution.py:61
  267.1 10.5 %fusion.6 = f32[512,2048]{1,0:T(8,128)} fusion(bf16[512,2048]{1,0:T(8,128)(2,1)} %copy-done.20, bf16[2048,2048]{1,0:T(8,128)(2,1)} %all-gather.5.cloned.1.call-done), kind=kOutput, calls=%fused_computation.43 | convolution fusion | flops 4294967296 | bytes 14680064 | tf_op jit(solution)/shard_map/dot_general | solution.py:57
  277.6 14.4 %multiply_convert_fusion = (bf16[512,2048]{1,0:T(8,128)(2,1)}, bf16[512,2048]{1,0:T(8,128)(2,1)}, bf16[512,2048]{1,0:T(8,128)(2,1)S(1)}) fusion(f32[512,2048]{1,0:T(8,128)} %fusion.6, f32[512,2048]{1,0:T(8,128)} %fusion.5, bf16[512,2048]{1,0:T(8,128)(2,1)} %copy-done.20, bf16[2048,2048]{1,0:T(8,128)(2,1)} %all-gather.3.cloned.1.call-done), kind=kOutput, calls=%fused_computation.3 | convolution fusion | flops 4310695936 | bytes 25165824 | tf_op jit(solution)/shard_map/dot_general | solution.py:57
  292.1 1.3 copy-done.34
  293.4 7.0 convolution_convert_fusion.1
  300.4 10.2 %convolution_convert_fusion.2 = bf16[2048,2048]{1,0:T(8,128)(2,1)} fusion(bf16[512,2048]{1,0:T(8,128)(2,1)} %copy-done.20, bf16[512,2048]{1,0:T(8,128)(2,1)} %get-tuple-element.114), kind=kOutput, calls=%fused_computation.2 | convolution fusion | flops 4299161600 | bytes 12582912 | tf_op jit(solution)/shard_map/dot_general | solution.py:67
  310.6 7.8 %fusion.7 = f32[512,2048]{1,0:T(8,128)S(1)} fusion(bf16[512,2048]{1,0:T(8,128)(2,1)} %copy-done.34, bf16[2048,2048]{1,0:T(8,128)(2,1)} %all-gather.3.cloned.1.call-done), kind=kOutput, calls=%fused_computation.44 | convolution fusion | flops 4294967296 | bytes 14680064 | tf_op jit(solution)/shard_map/dot_general | solution.py:61
  318.4 9.4 %add_convert_fusion.part = bf16[512,2048]{1,0:T(8,128)(2,1)} fusion(f32[512,2048]{1,0:T(8,128)S(1)} %fusion.7, bf16[512,2048]{1,0:T(8,128)(2,1)S(1)} %copy-done.33, bf16[2048,2048]{1,0:T(8,128)(2,1)} %all-gather.5.cloned.1.call-done), kind=kOutput, calls=%fused_computation.4 | convolution fusion | flops 4297064448 | bytes 16777216 | tf_op jit(solution)/shard_map/dot_general | solution.py:61
  328.4 11.1 %convolution_convert_fusion.down_part = bf16[2048,2048]{1,0:T(8,128)(2,1)} fusion(bf16[512,2048]{1,0:T(8,128)(2,1)} %get-tuple-element.113, bf16[512,2048]{1,0:T(8,128)(2,1)} %copy-done.28), kind=kOutput, calls=%fused_computation | convolution fusion | flops 4299161600 | bytes 12582912 | tf_op jit(solution)/shard_map/dot_general | solution.py:67
  339.5 108.4 %turn.1 = (f32[128,2048]{1,0:T(8,128)S(1)}, bf16[1024,2048]{1,0:T(8,128)(2,1)}, bf16[256,2048]{1,0:T(8,128)(2,1)S(1)}, f32[1,2048]{1,0:T(1,128)S(1)}) custom-call(bf16[512,2048]{1,0:T(8,128)(2,1)S(1)} %copy-done.7, bf16[2048,2048]{1,0:T(8,128)(2,1)} %convolution_convert_fusion.down_part, bf16[128,2048]{1,0:T(8,128)(2,1)} %bitcast.upstream, ...), custom_call_target="tpu_custom_call" | custom-call | bytes 195000000 | tf_op jit(solution)/shard_map/turn/pallas_call | solution.py:386
  448.9 26.8 %attention_back.1 = (bf16[1024,2048]{1,0:T(8,128)(2,1)}, bf16[1024,384]{1,0:T(8,128)(2,1)S(1)}, bf16[1024,2048]{1,0:T(8,128)(2,1)}) custom-call(s32[16]{0:T(128)S(1)} %select_reduce_fusion.order, s32[16]{0:T(128)S(1)} %eq.15.place, bf16[1024,2048]{1,0:T(8,128)(2,1)} %get-tuple-element.87.d_seq, bf16[2048,256]{1,0:T(8,128)(2,1)S(1)} %get-tuple-element.78.w_q, ...), custom_call_target="tpu_custom_call" | custom-call | bytes 150000000 | tf_op jit(solution)/shard_map/attention_back/pallas_call | solution.py:1079
  475.8 8.1 %convolution_convert_fusion.3.down_part = bf16[512,2048]{1,0:T(8,128)(2,1)S(1)} fusion(bf16[512,2048]{1,0:T(8,128)(2,1)S(1)} %copy-done.32, bf16[2048,2048]{1,0:T(8,128)(2,1)} %param.27), kind=kOutput, calls=%fused_computation.9 | convolution fusion | flops 4296015872 | bytes 12582912 | tf_op jit(solution)/shard_map/dot_general | solution.py:57
  483.8 48.6 %last.1 = (bf16[128,2048]{1,0:T(8,128)(2,1)S(1)}, bf16[128,2048]{1,0:T(8,128)(2,1)S(1)}, f32[1,2048]{1,0:T(1,128)S(1)}) custom-call(bf16[1024,2048]{1,0:T(8,128)(2,1)} %get-tuple-element.92.part, bf16[512,2048]{1,0:T(8,128)(2,1)S(1)} %convolution_convert_fusion.3.down_part, bf16[128,2048]{1,0:T(8,128)(2,1)S(1)} %bitcast.44, f32[128,2048]{1,0:T(8,128)S(1)} %copy-done.6, ...), custom_call_target="tpu_custom_call" | custom-call | bytes 135000000 | tf_op jit(solution)/shard_map/last/pallas_call | solution.py:386
  532.6 2.2 convolution_convert_fusion.5.out_part
  535.0 2.4 convolution_convert_fusion.4.joined
  537.5 1.2 copy-done.9
  538.7 1.2 copy-done.10
  540.0 1.2 copy-done.13
  541.2 155.2 %tail.1 = (bf16[512,8192]{1,0:T(8,128)(2,1)}, bf16[512,8192]{1,0:T(8,128)(2,1)}, bf16[2048,2048]{1,0:T(8,128)(2,1)}, bf16[4224,640]{1,0:T(8,128)(2,1)}) custom-call(bf16[256,2048]{1,0:T(8,128)(2,1)S(1)} %copy-done.9, bf16[256,2048]{1,0:T(8,128)(2,1)S(1)} %copy-done.10, bf16[256,2048]{1,0:T(8,128)(2,1)S(1)} %copy-done.12, ...), custom_call_target="tpu_custom_call" | custom-call | bytes 450000000 | tf_op jit(solution)/shard_map/tail/pallas_call | solution.py:386
  696.4 2.5 copy-done
  699.0 5.3 spread.1
  704.3 11.7 %convert_element_type.78 = f32[512,8192]{1,0:T(8,128)} convert(bf16[512,8192]{1,0:T(8,128)(2,1)} %get-tuple-element.110) | non-fusion elementwise | flops 4194304 | bytes 25165824 | tf_op jit(solution)/shard_map/convert_element_type | solution.py:1232
  716.0 11.7 %convert_element_type.79 = f32[512,8192]{1,0:T(8,128)} convert(bf16[512,8192]{1,0:T(8,128)(2,1)} %get-tuple-element.111) | non-fusion elementwise | flops 4194304 | bytes 25165824 | tf_op jit(solution)/shard_map/convert_element_type | solution.py:1233
  727.8 11.7 %convert_element_type.80 = f32[2048,2048]{1,0:T(8,128)} convert(bf16[2048,2048]{1,0:T(8,128)(2,1)} %get-tuple-element.112) | non-fusion elementwise | flops 4194304 | bytes 25165824 | tf_op jit(solution)/shard_map/convert_element_type | solution.py:1234
  (113 shorter events, 19.4 us)
Async XLA Ops:
  7.2 259.9 %all-gather.5.cloned.1.call-start = ((), (), s32[]{:S(2)}) async-start(), calls=%async_computation.3 | async-start | bytes 9437184 | tf_op jit(solution)/shard_map/all_gather | solution.py:84
  9.9 1.0 copy-start.1
  77.5 1.0 copy-start.3
  79.9 8.8 %collective-permute-start.6 = (bf16[64,2048]{1,0:T(8,128)(2,1)S(1)}, bf16[64,2048]{1,0:T(8,128)(2,1)}, u32[]{:S(2)}, u32[]{:S(2)}) collective-permute-start(bf16[64,2048]{1,0:T(8,128)(2,1)S(1)} %get-tuple-element.122), channel_id=1, source_target_pairs={{0,1},{1,2},{2,3},{3,0},{4,5},{5,6},{6,7},{7,4},{8,9},{9,10},{10,1... | collective-permute-start | bytes 786440 | tf_op jit(solution)/shard_map/ppermute | solution.py:103
  82.1 17.4 %collective-permute-start.7 = (bf16[64,2048]{1,0:T(8,128)(2,1)S(1)}, bf16[64,2048]{1,0:T(8,128)(2,1)}, u32[]{:S(2)}, u32[]{:S(2)}) collective-permute-start(bf16[64,2048]{1,0:T(8,128)(2,1)S(1)} %get-tuple-element.121), channel_id=1, source_target_pairs={{0,2},{1,3},{2,0},{3,1},{4,6},{5,7},{6,4},{7,5},{8,10},{9,11},{10,... | collective-permute-start | bytes 786440 | tf_op jit(solution)/shard_map/ppermute | solution.py:103
  82.1 22.8 %collective-permute-start.8 = (bf16[64,2048]{1,0:T(8,128)(2,1)S(1)}, bf16[64,2048]{1,0:T(8,128)(2,1)}, u32[]{:S(2)}, u32[]{:S(2)}) collective-permute-start(bf16[64,2048]{1,0:T(8,128)(2,1)S(1)} %get-tuple-element.120), channel_id=1, source_target_pairs={{0,3},{1,0},{2,1},{3,2},{4,7},{5,4},{6,5},{7,6},{8,11},{9,8},{10,9... | collective-permute-start | bytes 786440 | tf_op jit(solution)/shard_map/ppermute | solution.py:103
  105.9 1.0 copy-start.25
  106.9 170.8 %all-gather.3.cloned.1.call-start = ((), (), s32[]{:S(2)}) async-start(), calls=%async_computation.2 | async-start | bytes 9437184 | tf_op jit(solution)/shard_map/all_gather | solution.py:84
  107.0 33.2 %copy-start.29 = (s32[8,2]{0,1:T(2,128)S(1)}, s32[8,2]{0,1:T(2,128)}, u32[]{:S(2)}) copy-start(s32[8,2]{0,1:T(2,128)} %param.18) | copy-start | bytes 196
  108.4 8.5 %collective-permute-start.3 = (bf16[64,2048]{1,0:T(8,128)(2,1)S(1)}, bf16[64,2048]{1,0:T(8,128)(2,1)S(1)}, u32[]{:S(2)}, u32[]{:S(2)}) collective-permute-start(bf16[64,2048]{1,0:T(8,128)(2,1)S(1)} %get-tuple-element.118), channel_id=1, source_target_pairs={{0,1},{1,2},{2,3},{3,0},{4,5},{5,6},{6,7},{7,4},{8,9},{9,10},{10,1... | collective-permute-start | bytes 786440 | tf_op jit(solution)/shard_map/ppermute | solution.py:103
  110.4 17.0 %collective-permute-start.4 = (bf16[64,2048]{1,0:T(8,128)(2,1)S(1)}, bf16[64,2048]{1,0:T(8,128)(2,1)S(1)}, u32[]{:S(2)}, u32[]{:S(2)}) collective-permute-start(bf16[64,2048]{1,0:T(8,128)(2,1)S(1)} %get-tuple-element.117), channel_id=1, source_target_pairs={{0,2},{1,3},{2,0},{3,1},{4,6},{5,7},{6,4},{7,5},{8,10},{9,11},{10,... | collective-permute-start | bytes 786440 | tf_op jit(solution)/shard_map/ppermute | solution.py:103
  111.6 21.4 %collective-permute-start.5 = (bf16[64,2048]{1,0:T(8,128)(2,1)S(1)}, bf16[64,2048]{1,0:T(8,128)(2,1)S(1)}, u32[]{:S(2)}, u32[]{:S(2)}) collective-permute-start(bf16[64,2048]{1,0:T(8,128)(2,1)S(1)} %get-tuple-element.116), channel_id=1, source_target_pairs={{0,3},{1,0},{2,1},{3,2},{4,7},{5,4},{6,5},{7,6},{8,11},{9,8},{10,9... | collective-permute-start | bytes 786440 | tf_op jit(solution)/shard_map/ppermute | solution.py:103
  133.1 1.0 copy-start.24
  134.1 403.4 %reduce-scatter.3.cloned.1.call-start = ((), (), s32[]{:S(2)}) async-start(), calls=%async_computation.4 | async-start | bytes 9437184 | tf_op jit(solution)/shard_map/reduce_scatter | solution.py:88
  134.1 118.9 %collective-permute-start = (bf16[128,2048]{1,0:T(8,128)(2,1)}, bf16[128,2048]{1,0:T(8,128)(2,1)}, u32[]{:S(2)}, u32[]{:S(2)}) collective-permute-start(bf16[128,2048]{1,0:T(8,128)(2,1)} %bitcast.upstream), channel_id=1, source_target_pairs={{0,1},{1,2},{2,3},{3,0},{4,5},{5,6},{6,7},{7,4},{8,9},{9,10},{10,1... | collective-permute-start | bytes 1572872 | tf_op jit(solution)/shard_map/ppermute | solution.py:103
  136.0 118.1 %collective-permute-start.1 = (bf16[128,2048]{1,0:T(8,128)(2,1)}, bf16[128,2048]{1,0:T(8,128)(2,1)}, u32[]{:S(2)}, u32[]{:S(2)}) collective-permute-start(bf16[128,2048]{1,0:T(8,128)(2,1)} %bitcast.upstream), channel_id=1, source_target_pairs={{0,2},{1,3},{2,0},{3,1},{4,6},{5,7},{6,4},{7,5},{8,10},{9,11},{10,... | collective-permute-start | bytes 1572872 | tf_op jit(solution)/shard_map/ppermute | solution.py:103
  137.5 117.7 %collective-permute-start.2 = (bf16[128,2048]{1,0:T(8,128)(2,1)}, bf16[128,2048]{1,0:T(8,128)(2,1)}, u32[]{:S(2)}, u32[]{:S(2)}) collective-permute-start(bf16[128,2048]{1,0:T(8,128)(2,1)} %bitcast.upstream), channel_id=1, source_target_pairs={{0,3},{1,0},{2,1},{3,2},{4,7},{5,4},{6,5},{7,6},{8,11},{9,8},{10,9... | collective-permute-start | bytes 1572872 | tf_op jit(solution)/shard_map/ppermute | solution.py:103
  138.9 1.3 copy-start.26
  141.1 26.9 %copy-start.2 = (bf16[1,128,2048]{2,1,0:T(8,128)(2,1)S(1)}, bf16[1,128,2048]{2,1,0:T(8,128)(2,1)}, u32[]{:S(2)}) copy-start(bf16[1,128,2048]{2,1,0:T(8,128)(2,1)} %param.16) | copy-start | bytes 1572868
  164.8 1.0 copy-start.8
  165.7 0.8 copy-start.14
  166.5 0.7 copy-start.18
  167.2 0.8 copy-start.22
  168.0 85.0 %copy-start.27 = (bf16[512,2048]{1,0:T(8,128)(2,1)S(1)}, bf16[512,2048]{1,0:T(8,128)(2,1)}, u32[]{:S(2)}) copy-start(bf16[512,2048]{1,0:T(8,128)(2,1)} %copy-done.26) | copy-start | bytes 6291460
  250.7 1.0 copy-start.5
  251.6 1.4 copy-start.20
  256.3 1.4 copy-start.28
  277.6 15.8 %copy-start.21 = (bf16[512,2048]{1,0:T(8,128)(2,1)S(1)}, bf16[512,2048]{1,0:T(8,128)(2,1)}, u32[]{:S(2)}) copy-start(bf16[512,2048]{1,0:T(8,128)(2,1)} %copy-done.20) | copy-start | bytes 6291460
  292.1 1.3 copy-start.34
  310.6 7.8 %copy-start.33 = (bf16[512,2048]{1,0:T(8,128)(2,1)S(1)}, bf16[512,2048]{1,0:T(8,128)(2,1)}, u32[]{:S(2)}) copy-start(bf16[512,2048]{1,0:T(8,128)(2,1)} %get-tuple-element.114) | copy-start | bytes 6291460
  327.8 209.7 %reduce-scatter.5.cloned.1.call-start = ((), (), s32[]{:S(2)}) async-start(), calls=%async_computation.5 | async-start | bytes 9437184 | tf_op jit(solution)/shard_map/reduce_scatter | solution.py:88
  328.4 11.1 %copy-start.6 = (f32[128,2048]{1,0:T(8,128)S(1)}, f32[128,2048]{1,0:T(8,128)}, u32[]{:S(2)}) copy-start(f32[128,2048]{1,0:T(8,128)} %copy-done.5) | copy-start | bytes 3145732
  328.4 11.1 %copy-start.7 = (bf16[512,2048]{1,0:T(8,128)(2,1)S(1)}, bf16[512,2048]{1,0:T(8,128)(2,1)}, u32[]{:S(2)}) copy-start(bf16[512,2048]{1,0:T(8,128)(2,1)} %add_convert_fusion.part) | copy-start | bytes 6291460
  339.5 109.4 %copy-start.4 = (bf16[256,2048]{1,0:T(8,128)(2,1)S(1)}, bf16[256,2048]{1,0:T(8,128)(2,1)}, u32[]{:S(2)}) copy-start(bf16[256,2048]{1,0:T(8,128)(2,1)} %copy-done.3) | copy-start | bytes 3145732
  339.5 109.4 %copy-start.15 = (f32[1024,128]{1,0:T(8,128)S(1)}, f32[1024,128]{1,0:T(8,128)}, u32[]{:S(2)}) copy-start(f32[1024,128]{1,0:T(8,128)} %copy-done.14) | copy-start | bytes 1572868
  339.5 109.4 %copy-start.19 = (bf16[1,1024,64]{2,1,0:T(8,128)(2,1)S(1)}, bf16[1,1024,64]{2,1,0:T(8,128)(2,1)}, u32[]{:S(2)}) copy-start(bf16[1,1024,64]{2,1,0:T(8,128)(2,1)} %copy-done.18) | copy-start | bytes 393220
  448.0 1.0 copy-start.11
  448.9 26.8 %copy-start.32 = (bf16[512,2048]{1,0:T(8,128)(2,1)S(1)}, bf16[512,2048]{1,0:T(8,128)(2,1)}, u32[]{:S(2)}) copy-start(bf16[512,2048]{1,0:T(8,128)(2,1)} %get-tuple-element.113) | copy-start | bytes 6291460
  483.8 48.8 %copy-start.23 = (bf16[1024,256]{1,0:T(8,128)(2,1)S(1)}, bf16[1024,256]{1,0:T(8,128)(2,1)}, u32[]{:S(2)}) copy-start(bf16[1024,256]{1,0:T(8,128)(2,1)} %copy-done.22) | copy-start | bytes 1572868
  483.8 48.8 %copy-start.31 = (bf16[1024,2048]{1,0:T(8,128)(2,1)S(1)}, bf16[1024,2048]{1,0:T(8,128)(2,1)}, u32[]{:S(2)}) copy-start(bf16[1024,2048]{1,0:T(8,128)(2,1)} %get-tuple-element.102) | copy-start | bytes 12582916
  532.5 2.4 copy-start.16
  532.5 2.5 copy-start.30
  535.0 2.5 copy-start.12
  537.5 1.2 copy-start.9
  538.7 1.2 copy-start.10
  540.0 1.2 copy-start.13
  696.4 2.5 copy-start
  727.8 12.3 %copy-start.17 = (bf16[128,2048]{1,0:T(8,128)(2,1)S(1)}, bf16[128,2048]{1,0:T(8,128)(2,1)}, u32[]{:S(2)}) copy-start(bf16[128,2048]{1,0:T(8,128)(2,1)} %copy-done.16) | copy-start | bytes 1572868
Sparse Core Ops, SparseCore 0:
  107.0 55.7 all-gather.4
  165.2 65.2 all-gather.2
  328.0 90.5 reduce-scatter.2
  422.9 72.0 reduce-scatter.4

commit v4 on v3

v4 whole, which is shorter than its diff:
```python
import functools
import math

import jax
import jax.numpy as jnp
from jax import lax
from jax.experimental import pallas as pl
from jax.experimental.pallas import tpu as pltpu
from jax.sharding import PartitionSpec as P

HEAD_DIM = 64


EPS = 1e-05
THETA = 500000.0


def frequencies(head_width):
    evens = jnp.arange(0, head_width, 2, dtype=jnp.float32)
    inverse = 1.0 / THETA ** (evens / head_width)
    wavelen = 2.0 * math.pi / inverse
    smooth = (8192.0 / wavelen - 1.0) / 3.0
    middle = (1.0 - smooth) * inverse / 32.0 + smooth * inverse
    return jnp.where(wavelen < 2048.0, inverse, jnp.where(wavelen > 8192.0, inverse / 32.0, middle))


def rotation(positions, head_width):
    angles = positions.astype(jnp.float32)[:, None] * frequencies(head_width)[None, :]
    cosine = jnp.concatenate([jnp.cos(angles), jnp.cos(angles)], axis=1)[:, None, :]
    sine = jnp.concatenate([jnp.sin(angles), jnp.sin(angles)], axis=1)[:, None, :]
    return (cosine, sine)


def rotate(tensor, cosine, sine):
    middle = tensor.shape[-1] // 2
    turned = jnp.concatenate([-tensor[..., middle:], tensor[..., :middle]], axis=-1)
    return tensor * cosine + turned * sine


def unrotate(gradient, cosine, sine):
    middle = gradient.shape[-1] // 2
    moved = gradient * sine
    back_turn = jnp.concatenate([moved[..., middle:], -moved[..., :middle]], axis=-1)
    return gradient * cosine + back_turn


def slot_positions(pairing, seq_length, block_len):
    flattened = pairing.reshape(-1)
    slots = jnp.arange(seq_length, dtype=jnp.int32)
    owning = slots // block_len
    labels = jnp.arange(flattened.shape[0], dtype=jnp.int32)
    anchor = jnp.sum(jnp.where(owning[:, None] == labels[None, :], flattened[None, :], 0), axis=1)
    return anchor * block_len + slots % block_len


def product(left, right):
    return jnp.dot(left, right, preferred_element_type=jnp.float32)


def product_t(left, right):
    return lax.dot_general(
        left, right, (((1,), (1,)), ((), ())), preferred_element_type=jnp.float32
    )


def tokens_t(left, right):
    return lax.dot_general(
        left, right, (((0,), (0,)), ((), ())), preferred_element_type=jnp.float32
    )


LOW = jnp.bfloat16
MESH = pl.DeviceIdType.MESH
ANY = pl.BlockSpec(memory_space=pl.ANY)
VMEM = pl.BlockSpec(memory_space=pltpu.VMEM)


def norm_back(upstream, gain, unit, scale):
    weighted = upstream * gain
    return scale * (weighted - unit * jnp.mean(weighted * unit, axis=1, keepdims=True))


def gather(array, axis):
    return lax.all_gather(array, axis, axis=0, tiled=True)


def scatter_sum(array, axis):
    return lax.psum_scatter(array, axis, scatter_dimension=0, tiled=True)


def einsum(spec, left, right):
    return jnp.einsum(spec, left, right, preferred_element_type=jnp.float32)


def swap_order(array, first, second):
    size = array.shape[1] // (first * second)
    parts = []
    for b in range(second):
        for a in range(first):
            at = (a * second + b) * size
            parts.append(array[:, at : at + size])
    return jnp.concatenate(parts, axis=1)


class Links:
    def __init__(self, n_ctx, n_fsdp, send_sems, recv_sems):
        self.n_ctx, self.n_fsdp = n_ctx, n_fsdp
        self.ctx, self.fsdp = lax.axis_index("ctx"), lax.axis_index("fsdp")
        self.send_sems, self.recv_sems = send_sems, recv_sems
        self.used = 0
        core = self.ctx % 2
        flips = [self.flip(d) for d in range(1, n_ctx.bit_length() - 1)]
        backward = flips[::-1]
        self.order = [(1 - core) * a + core * b for a, b in zip(flips, backward)]
        self.sibling = self.flip(0)

    def flip(self, digit):
        return 2**digit * (1 - 2 * ((self.ctx // 2**digit) % 2))

    def greet(self, cube=False, plane=False, line=False, whole_line=False):
        barrier = pltpu.get_barrier_semaphore()
        count = 0

        def hail(ctx, fsdp):
            pl.semaphore_signal(barrier, inc=1, device_id=(ctx, fsdp), device_id_type=MESH)

        if plane:
            for shift in range(1, self.n_ctx):
                hail(lax.rem(self.ctx + shift, self.n_ctx), self.fsdp)
            count += self.n_ctx - 1
        elif cube:
            for step in self.order + [self.sibling]:
                hail(self.ctx + step, self.fsdp)
            count += len(self.order) + 1
        if whole_line:
            for shift in range(1, self.n_fsdp):
                hail(self.ctx, lax.rem(self.fsdp + shift, self.n_fsdp))
            count += self.n_fsdp - 1
        if line and not whole_line:
            for step in (-1, 1):
                inside = jnp.logical_and(self.fsdp + step >= 0, self.fsdp + step < self.n_fsdp)

                @pl.when(inside)
                def _():
                    hail(self.ctx, self.fsdp + step)

            ends = jnp.logical_or(self.fsdp == 0, self.fsdp == self.n_fsdp - 1)
            pl.when(ends)(lambda: pl.semaphore_wait(barrier, count + 1))
            pl.when(jnp.logical_not(ends))(lambda: pl.semaphore_wait(barrier, count + 2))
        else:
            pl.semaphore_wait(barrier, count)

    def copies(self, sources, target, ctx, fsdp):
        slot = self.used
        self.used += 1
        return [
            pltpu.make_async_remote_copy(
                src_ref=source,
                dst_ref=target,
                send_sem=self.send_sems.at[slot],
                recv_sem=self.recv_sems.at[slot],
                device_id=(ctx, fsdp),
                device_id_type=MESH,
            )
            for source in sources
        ]

    def copy(self, source, target, ctx, fsdp):
        return self.copies((source,), target, ctx, fsdp)[0]


def rows_of(ref, index, rows):
    return ref.at[pl.ds(pl.multiple_of(index * rows, rows), rows)]


def in_turns(*walks):
    for walk in walks:
        next(walk, None)


def finish(*walks):
    for walk in walks:
        for _ in walk:
            pass


def cube_gather(links, ref, rows):
    held, sent, shared = [0], [], []

    def send(offset, step):
        block = rows_of(ref, links.ctx + offset, rows)
        copy = links.copy(block, block, links.ctx + step, links.fsdp)
        copy.start()
        return copy

    fresh = held
    for step in links.order:
        copies = [send(offset, step) for offset in held]
        shared += [send(offset, links.sibling) for offset in fresh]
        yield
        for copy in copies:
            copy.wait_recv()
        sent += copies
        fresh = [offset + step for offset in held]
        held = held + fresh
    shared += [send(offset, links.sibling) for offset in fresh]
    yield
    for copy in shared:
        copy.wait_recv()
    for copy in sent + shared:
        copy.wait_send()


def in_rows(rows, body):
    size = math.gcd(rows, 64)

    def step(at, carry):
        body(pl.multiple_of(at * size, size), size)
        return carry

    lax.fori_loop(0, rows // size, step, 0)


def cube_sum(links, part, land, acc, rows):
    offsets, theirs = [0], [0]
    for step, other in zip(links.order, links.order[::-1]):
        offsets = offsets + [offset + step for offset in offsets]
        theirs = theirs + [offset + other for offset in theirs]
    wide = jnp.float32
    sent, pending = [], []
    for at, offset in enumerate(theirs):
        source = rows_of(part, links.ctx + links.sibling + offset, rows)
        target = land.at[pl.ds(at * rows, rows)]
        copy = links.copy(source, target, links.ctx + links.sibling, links.fsdp)
        copy.start()
        pending.append(copy)
    yield
    land_from, land_at = 0, len(offsets)
    for level in range(len(links.order) + 1):
        count = len(offsets)
        half = count // 2
        onward = []
        for at in list(range(half, count)) + list(range(half)):
            pending[at].wait_recv()
            first, place = level == 0, (land_from + at) * rows
            goes = at >= half and count > 1

            def add(start, size, at=at, place=place, first=first, goes=goes):
                landed = land[pl.ds(place + start, size), :].astype(wide)
                if first:
                    base = (links.ctx + offsets[at]) * rows
                    mine = part[pl.ds(pl.multiple_of(base + start, size), size), :].astype(wide)
                else:
                    mine = acc[pl.ds(at * rows + start, size), :]
                if goes:
                    land[pl.ds(place + start, size), :] = (mine + landed).astype(LOW)
                else:
                    acc[pl.ds(at * rows + start, size), :] = mine + landed

            in_rows(rows, add)
            if goes:
                source = land.at[pl.ds(place, rows)]
                target = land.at[pl.ds((land_at + at - half) * rows, rows)]
                step = links.order[len(links.order) - 1 - level]
                copy = links.copy(source, target, links.ctx + step, links.fsdp)
                copy.start()
                onward.append(copy)
        sent += pending
        pending, land_from = onward, land_at
        land_at += half
        offsets = offsets[: max(half, 1)]
        if level < len(links.order):
            yield
    for copy in sent:
        copy.wait_send()


def cube_scratch(n_ctx, rows, width):
    return [
        pltpu.VMEM(((n_ctx - 1) * rows, width), LOW),
        pltpu.VMEM((max(1, n_ctx // 4) * rows, width), jnp.float32),
    ]


def line_gather(links, refs, rows):
    count, me = links.n_fsdp, links.fsdp
    sends = []
    for hop in range(count - 1):
        receives = []
        for ref, size in zip(refs, rows):
            up_block = rows_of(ref, me - hop, size)
            down_block = rows_of(ref, me + hop, size)
            up = links.copy(up_block, up_block, links.ctx, me + 1)
            down = links.copy(down_block, down_block, links.ctx, me - 1)
            up_ok = jnp.logical_and(me >= hop, me < count - 1)
            down_ok = jnp.logical_and(me <= count - 1 - hop, me > 0)
            pl.when(up_ok)(up.start)
            pl.when(down_ok)(down.start)
            sends += [(up_ok, up), (down_ok, down)]
            receives += [(me >= hop + 1, up), (me <= count - 2 - hop, down)]
        yield
        for ok, copy in receives:
            pl.when(ok)(copy.wait_recv)
    for ok, copy in sends:
        pl.when(ok)(copy.wait_send)


def line_sum(links, part, land, total, rows):
    count, me = links.n_fsdp, links.fsdp
    flows = []
    for hop in range(count - 1):
        for side in (0, 1):
            goal = count - 1 - hop if side == 0 else hop
            slot = (side * (count - 1) + hop) * rows
            landing = land.at[pl.ds(slot, rows)]
            fed = me > 0 if side == 0 else me < count - 1
            passes = me < goal if side == 0 else me > goal
            peer = me + 1 if side == 0 else me - 1
            first, onward = links.copies((part.at[pl.ds(goal * rows, rows)], landing), landing, links.ctx, peer)
            flows.append((goal * rows, slot, onward, fed, passes, me == goal))
            pl.when(jnp.logical_and(passes, jnp.logical_not(fed)))(first.start)

    total[...] = rows_of(part, me, rows)[...].astype(jnp.float32)
    lower = me < count // 2
    for hop in range(count - 1):
        yield
        for near in (0, 1):

            @pl.when(lower if near == 0 else jnp.logical_not(lower))
            def _():
                for way in (near, 1 - near):
                    base, slot, onward, fed, passes, _ = flows[2 * hop + way]

                    @pl.when(jnp.logical_and(passes, fed))
                    def _():
                        onward.wait_recv()

                        def add(start, size):
                            own = part[pl.ds(base + start, size), :].astype(jnp.float32)
                            landed = land[pl.ds(slot + start, size), :].astype(jnp.float32)
                            land[pl.ds(slot + start, size), :] = (own + landed).astype(LOW)

                        in_rows(rows, add)
                        onward.start()

    yield
    for base, slot, onward, fed, passes, mine in flows:

        @pl.when(jnp.logical_and(mine, fed))
        def _():
            onward.wait_recv()

            def add(start, size):
                landed = land[pl.ds(slot + start, size), :].astype(jnp.float32)
                total[pl.ds(start, size), :] += landed

            in_rows(rows, add)

    for base, slot, onward, fed, passes, _ in flows:
        pl.when(passes)(onward.wait_send)


def line_scratch(n_fsdp, rows, width):
    return [
        pltpu.VMEM((2 * (n_fsdp - 1) * rows, width), LOW),
        pltpu.VMEM((rows, width), jnp.float32),
    ]


def communicate(kernel, collective_id, name, operands, in_specs, outs, out_specs, scratch, copies, busy):
    return pl.pallas_call(
        kernel,
        out_shape=outs,
        in_specs=in_specs,
        out_specs=out_specs,
        scratch_shapes=scratch
        + [pltpu.SemaphoreType.DMA((copies,)), pltpu.SemaphoreType.DMA((copies,))],
        compiler_params=pltpu.CompilerParams(
            collective_id=collective_id, has_side_effects=True, vmem_limit_bytes=62 << 20
        ),
        cost_estimate=pl.CostEstimate(flops=0, bytes_accessed=busy * 3_000_000, transcendentals=0),
        name=name,
    )(*operands)


def tail_kernel(
    n_ctx,
    n_fsdp,
    pair,
    joined,
    out_part,
    terms,
    gate_all,
    up_all,
    attn_all,
    attn_part,
    land,
    total,
    attn_low,
    local_sems,
    send_sems,
    recv_sems,
):
    links = Links(n_ctx, n_fsdp, send_sems, recv_sems)
    strip, ff_rows = pair.shape[1] // n_fsdp, pair.shape[2]
    model_rows, term_rows = joined.shape[0] // n_fsdp, terms.shape[0] // n_fsdp
    rows = model_rows + term_rows
    head_rows, joined_width = out_part.shape[0], joined.shape[1]
    out_width = attn_part.shape[1] - joined_width
    heads_in = model_rows // head_rows

    def place(ref, ctx, fsdp):
        return ref.at[
            pl.ds(pl.multiple_of(ctx * strip, strip), strip),
            pl.ds(pl.multiple_of(fsdp * ff_rows, ff_rows), ff_rows),
        ]

    def strip_of(part, fsdp):
        return pair.at[part, pl.ds(pl.multiple_of(fsdp * strip, strip), strip)]

    def out_column(ctx):
        return out_part.at[:, pl.ds(pl.multiple_of(ctx * out_width, out_width), out_width)]

    out_from = (links.ctx // heads_in) * rows + lax.rem(links.ctx, heads_in) * head_rows
    out_place = attn_part.at[
        pl.ds(pl.multiple_of(out_from, 16), head_rows), pl.ds(joined_width, out_width)
    ]
    moves = [
        (strip_of(0, links.fsdp), place(gate_all, links.ctx, links.fsdp)),
        (strip_of(1, links.fsdp), place(up_all, links.ctx, links.fsdp)),
        (out_column(links.ctx), out_place),
    ]
    for fsdp in range(n_fsdp):
        moves.append(
            (
                joined.at[pl.ds(fsdp * model_rows, model_rows)],
                attn_part.at[pl.ds(fsdp * rows, model_rows), pl.ds(0, joined_width)],
            )
        )
        moves.append(
            (
                terms.at[pl.ds(fsdp * term_rows, term_rows)],
                attn_part.at[pl.ds(fsdp * rows + model_rows, term_rows)],
            )
        )
    local = [pltpu.make_async_copy(a, b, local_sems.at[i]) for i, (a, b) in enumerate(moves)]
    for copy in local:
        copy.start()
    links.greet(plane=True, line=True, whole_line=True)
    to_shards = []
    for part, goal in enumerate((gate_all, up_all)):
        copies = []
        for shift in range(1, n_fsdp):
            target = lax.rem(links.fsdp + shift, n_fsdp)
            copy = links.copy(
                strip_of(part, target), place(goal, links.ctx, links.fsdp), links.ctx, target
            )
            copy.start()
            copies.append(copy)
        to_shards.append(copies)
    to_plane = []
    for shift in range(1, n_ctx):
        target = lax.rem(links.ctx + shift, n_ctx)
        copy = links.copy(out_column(target), out_place, target, links.fsdp)
        copy.start()
        to_plane.append(copy)
    for copy in local:
        copy.wait()
    for copy in to_plane:
        copy.wait()
    for copy in to_shards[0]:
        copy.wait()
    plane_gate = cube_gather(links, gate_all, strip)
    in_turns(plane_gate)
    line = line_sum(links, attn_part, land, total, rows)
    in_turns(line)
    for copy in to_shards[1]:
        copy.wait()
    plane_up = cube_gather(links, up_all, strip)
    in_turns(plane_gate, plane_up, line, plane_gate, line, plane_up, line)
    finish(line)
    attn_low[...] = total[...].astype(LOW)
    mine = pltpu.make_async_copy(attn_low, rows_of(attn_all, links.ctx, rows), local_sems.at[0])
    mine.start()
    mine.wait()
    plane_attn = cube_gather(links, attn_all, rows)
    in_turns(plane_attn, plane_up, plane_attn)
    finish(plane_gate, plane_up, plane_attn)


def tail(n_ctx, n_fsdp, pair, joined, out_part, terms):
    strip, ff_rows = pair.shape[1] // n_fsdp, pair.shape[2]
    rows = (joined.shape[0] + terms.shape[0]) // n_fsdp
    attn_width = joined.shape[1] + out_part.shape[1] // n_ctx
    shape = lambda *dims: jax.ShapeDtypeStruct(dims, LOW)
    return communicate(
        functools.partial(tail_kernel, n_ctx, n_fsdp),
        5,
        "tail",
        (pair, joined, out_part, terms),
        [ANY] * 4,
        [
            shape(strip * n_ctx, ff_rows * n_fsdp),
            shape(strip * n_ctx, ff_rows * n_fsdp),
            shape(rows * n_ctx, attn_width),
        ],
        [ANY] * 3,
        [pltpu.VMEM((rows * n_fsdp, attn_width), LOW)]
        + line_scratch(n_fsdp, rows, attn_width)
        + [pltpu.VMEM((rows, attn_width), LOW), pltpu.SemaphoreType.DMA((3 + 2 * n_fsdp,))],
        4 * (n_ctx - 1) + 4 * (n_fsdp - 1),
        130,
    )


def widen_kernel(*refs):
    count = len(refs) // 2
    for source, goal in zip(refs[:count], refs[count:]):
        goal[...] = source[...].astype(jnp.float32)


def widen(*arrays):
    steps = max(4, arrays[0].shape[0] // 128)
    specs = [pl.BlockSpec((a.shape[0] // steps, a.shape[1]), lambda i: (i, 0)) for a in arrays]
    return pl.pallas_call(
        widen_kernel,
        grid=(steps,),
        in_specs=specs,
        out_specs=specs,
        out_shape=[jax.ShapeDtypeStruct(a.shape, jnp.float32) for a in arrays],
        compiler_params=pltpu.CompilerParams(vmem_limit_bytes=60 << 20),
        name="widen",
    )(*arrays)


def spread_kernel(parts, widths, gathered, *outs):
    at = 0
    for out, width, sharers in zip(outs, widths, parts):
        pieces = []
        for i in range(0, gathered.shape[0], sharers):
            piece = gathered[i, :, at : at + width].astype(jnp.float32)
            for j in range(1, sharers):
                piece = piece + gathered[i + j, :, at : at + width].astype(jnp.float32)
            pieces.append(piece)
        out[...] = jnp.concatenate(pieces, axis=1)
        at += width


def spread(gathered, rows, widths, sharers):
    n_ctx, _, joined = gathered.shape
    step = 2 * max(sharers)
    tile = min(rows, 256)
    return pl.pallas_call(
        functools.partial(spread_kernel, sharers, widths),
        grid=(n_ctx // step, rows // tile),
        in_specs=[pl.BlockSpec((step, tile, joined), lambda i, j: (i, j, 0))],
        out_specs=[
            pl.BlockSpec((tile, step // s * w), lambda i, j: (j, i)) for w, s in zip(widths, sharers)
        ],
        out_shape=[
            jax.ShapeDtypeStruct((rows, n_ctx // s * w), jnp.float32) for w, s in zip(widths, sharers)
        ],
        compiler_params=pltpu.CompilerParams(vmem_limit_bytes=32 << 20),
        name="spread",
    )(gathered)


def lanes(shape):
    return lax.broadcasted_iota(jnp.int32, shape, 1)


def halves(tensor, back):
    half = HEAD_DIM // 2
    width = tensor.shape[1]
    later, earlier = pltpu.roll(tensor, width - half, 1), pltpu.roll(tensor, half, 1)
    first = lanes(tensor.shape) % HEAD_DIM < half
    return jnp.where(first, later, -earlier) if back else jnp.where(first, -later, earlier)


def turned(tensor, cosine, sine, back=False):
    parts = []
    for at in range(0, tensor.shape[1], 128):
        piece = tensor[:, at : at + 128]
        if back:
            parts.append(piece * cosine + halves(piece * sine, True))
        else:
            parts.append(piece * cosine + halves(piece, False) * sine)
    return parts[0] if len(parts) == 1 else jnp.concatenate(parts, axis=1)


def dot(left, right):
    return jnp.dot(left, right, preferred_element_type=jnp.float32)


def dot_dims(left, right, left_dim, right_dim):
    dims = (((left_dim,), (right_dim,)), ((), ()))
    return lax.dot_general(left, right, dims, preferred_element_type=jnp.float32)


def to_positions(pos_row, at, tile):
    shape = (tile, pos_row.shape[1])
    here = lax.broadcasted_iota(jnp.int32, shape, 0) + at * tile
    return jnp.where(here == pos_row[...], 1.0, 0.0).astype(LOW)


def to_slots(pos_column, rows, tile):
    shape = (tile, pos_column.shape[0])
    return jnp.where(lanes(shape) == pos_column[rows, :], 1.0, 0.0).astype(LOW)


def project(seq, gain, w_q, w_kv, cosine, sine, normed, joined, tile, start, stop):
    query_width, kv_width = w_q.shape[1], w_kv.shape[1] // 2

    def step(at, carry):
        rows = pl.ds(pl.multiple_of(at * tile, tile), tile)
        wide = seq[rows, :].astype(jnp.float32)
        scale = lax.rsqrt(jnp.mean(wide * wide, axis=1, keepdims=True) + EPS)
        low = (wide * scale * gain).astype(LOW)
        normed[rows, :] = low
        cos, sin = cosine[rows, :], sine[rows, :]
        joined[rows, pl.ds(0, query_width)] = turned(dot(low, w_q[...]), cos, sin).astype(LOW)
        both = dot(low, w_kv[...])
        both = jnp.where(lanes(both.shape) < kv_width, turned(both, cos, sin), both)
        joined[rows, pl.ds(query_width, 2 * kv_width)] = both.astype(LOW)
        return carry

    lax.fori_loop(start, stop, step, 0)


def in_order(pos_row, joined, q_heads, k_head, v_head, tile):
    query_width = q_heads.shape[0] * HEAD_DIM
    kv_width = k_head.shape[0] * HEAD_DIM

    def step(at, carry):
        rows = pl.ds(pl.multiple_of(at * tile, tile), tile)
        moved = dot(to_positions(pos_row, at, tile), joined[...]).astype(LOW)
        split_heads(moved[:, :query_width], q_heads, rows)
        split_heads(moved[:, query_width : query_width + kv_width], k_head, rows)
        split_heads(moved[:, query_width + kv_width :], v_head, rows)
        return carry

    lax.fori_loop(0, joined.shape[0] // tile, step, 0)


def scores_of(queries, keys, tile):
    logits = dot_dims(queries, keys, 1, 1) * (HEAD_DIM**-0.5)
    last = logits[:, -tile:]
    seen = lax.broadcasted_iota(jnp.int32, last.shape, 0) >= lanes(last.shape)
    last = jnp.where(seen, last, -1e30)
    before = logits.shape[1] - tile
    return last if before == 0 else jnp.concatenate([logits[:, :before], last], axis=1)


def attend(q_heads, k_head, v_head, out_heads, logs, tile, service):
    heads, length, _ = q_heads.shape
    group = heads // k_head.shape[0]
    for tile_at in range(length // tile):
        here, keys = pl.ds(tile_at * tile, tile), (tile_at + 1) * tile
        logs[here, :] = jnp.zeros((tile, logs.shape[1]), jnp.float32)

        def step(head, carry):
            scores = scores_of(q_heads[head, here, :], k_head[head // group, pl.ds(0, keys), :], tile)
            largest = jnp.max(scores, axis=1, keepdims=True)
            expo = jnp.exp(scores - largest)
            total = jnp.sum(expo, axis=1, keepdims=True)
            probs = (expo * (1.0 / total)).astype(LOW)
            out = dot(probs, v_head[head // group, pl.ds(0, keys), :])
            out_heads[head, here, :] = out.astype(LOW)
            log = largest + jnp.log(total)
            logs[here, :] += jnp.where(lanes((tile, logs.shape[1])) == head, log, 0.0)
            return carry

        lax.fori_loop(0, heads, step, 0)
        service()


def attend_back(q_heads, k_head, v_head, d_heads, logs, dq_heads, dk_head, dv_head, tile, service):
    heads, length, _ = q_heads.shape
    group = heads // k_head.shape[0]
    dk_head[...] = jnp.zeros_like(dk_head)
    dv_head[...] = jnp.zeros_like(dv_head)
    for tile_at in range(length // tile):
        here, keys = pl.ds(tile_at * tile, tile), (tile_at + 1) * tile

        def step(head, carry):
            queries, d_out = q_heads[head, here, :], d_heads[head, here, :]
            kept, seen = k_head[head // group, pl.ds(0, keys), :], v_head[head // group, pl.ds(0, keys), :]
            column = lanes((tile, logs.shape[1])) == head
            log = jnp.sum(jnp.where(column, logs[here, :], 0.0), axis=1, keepdims=True)
            probs = jnp.exp(scores_of(queries, kept, tile) - log)
            d_probs = dot_dims(d_out, seen, 1, 1)
            delta = jnp.sum(probs * d_probs, axis=1, keepdims=True)
            d_score = (probs * (d_probs - delta) * (HEAD_DIM**-0.5)).astype(LOW)
            dq_heads[head, here, :] = dot(d_score, kept)
            dk_head[head // group, pl.ds(0, keys), :] += dot_dims(d_score, queries, 0, 0)
            dv_head[head // group, pl.ds(0, keys), :] += dot_dims(probs.astype(LOW), d_out, 0, 0)
            return carry

        lax.fori_loop(0, heads, step, 0)
        service()


def side_by_side(ref, rows):
    return jnp.concatenate([ref[head, rows, :] for head in range(ref.shape[0])], axis=1)


def split_heads(value, ref, rows):
    for head in range(ref.shape[0]):
        ref[head, rows, :] = value[:, head * HEAD_DIM : (head + 1) * HEAD_DIM]


def forward_kernel(
    n_ctx,
    n_fsdp,
    tile,
    pos_row,
    pos_column,
    own,
    w_query,
    kv,
    w_out,
    gains,
    w_gate,
    w_up,
    upstream,
    cosine,
    sine,
    gate_all,
    up_all,
    upstream_all,
    q_all,
    kv_all,
    gains_all,
    out_rows,
    normed,
    q_heads,
    k_head,
    v_head,
    logs,
    attended,
    resid,
    normed_mlp,
    seq,
    cols_all,
    out_heads,
    joined,
    part,
    land,
    acc,
    local_sems,
    send_sems,
    recv_sems,
):
    links = Links(n_ctx, n_fsdp, send_sems, recv_sems)
    rows, weight_rows, query_width = own.shape[0], kv.shape[0], q_all.shape[1]
    head_rows, out_width = out_rows.shape[0], cols_all.shape[1]
    strip, ff_rows = weight_rows // n_ctx, gate_all.shape[1]
    length = normed.shape[0]

    def cut(ref, size):
        return ref.at[:, pl.ds(pl.multiple_of(links.ctx * size, size), size)]

    def strip_from(ref, fsdp):
        return ref.at[
            pl.ds(pl.multiple_of(links.ctx * strip, strip), strip),
            pl.ds(pl.multiple_of(fsdp * ff_rows, ff_rows), ff_rows),
        ]

    def strip_to(ref):
        return rows_of(ref, links.ctx * n_fsdp + links.fsdp, strip)

    moves = [
        (own, rows_of(seq, links.ctx, rows)),
        (cut(w_query, query_width), rows_of(q_all, links.fsdp, weight_rows)),
        (kv, rows_of(kv_all, links.fsdp, weight_rows)),
        (gains, rows_of(gains_all, links.fsdp, gains.shape[0])),
        (cut(w_out, out_width), rows_of(cols_all, links.fsdp, weight_rows)),
        (strip_from(w_gate, links.fsdp), strip_to(gate_all)),
        (strip_from(w_up, links.fsdp), strip_to(up_all)),
        (upstream, rows_of(upstream_all, links.fsdp, rows)),
    ]
    local = [pltpu.make_async_copy(a, b, local_sems.at[i]) for i, (a, b) in enumerate(moves)]
    for copy in local:
        copy.start()
    links.greet(plane=True, line=True, whole_line=True)
    for copy in local[:5]:
        copy.wait()
    plane = cube_gather(links, seq, rows)
    line = line_gather(links, [gains_all, q_all, kv_all], [gains.shape[0], weight_rows, weight_rows])
    cols = line_gather(links, [cols_all], [weight_rows])
    in_turns(plane, line, plane, line, plane, line)
    finish(line, plane)
    in_turns(cols)
    for copy in local[5:]:
        copy.wait()

    def gain_row(row):
        first = [gains_all[pl.ds(z * gains.shape[0] + row, 1), :] for z in range(n_fsdp)]
        return jnp.concatenate(first, axis=1)

    gain = gain_row(0)
    tiles = length // tile
    half = max(1, tiles // 2)
    slots = (seq, gain, q_all, kv_all, cosine, sine, normed, joined, tile)
    project(*slots, 0, half)
    in_turns(cols)
    project(*slots, half, tiles)
    in_order(pos_row, joined, q_heads, k_head, v_head, tile)

    to_plane, gate_strips, up_strips = [], [], []
    column = cut(out_rows, out_width)
    mine = pltpu.make_async_copy(rows_of(cols_all, links.ctx, head_rows), column, local_sems.at[0])

    def hand_out():
        finish(cols)
        mine.start()
        for shift in range(1, n_ctx):
            target = lax.rem(links.ctx + shift, n_ctx)
            copy = links.copy(rows_of(cols_all, target, head_rows), column, target, links.fsdp)
            copy.start()
            to_plane.append(copy)
        for source, goal, copies in ((w_gate, gate_all, gate_strips), (w_up, up_all, up_strips)):
            for shift in range(1, n_fsdp):
                target = lax.rem(links.fsdp + shift, n_fsdp)
                copy = links.copy(strip_from(source, target), strip_to(goal), links.ctx, target)
                copy.start()
                copies.append(copy)

    services = [lambda: in_turns(cols), lambda: in_turns(cols), hand_out]

    def service():
        if services:
            services.pop(0)()

    attend(q_heads, k_head, v_head, out_heads, logs, tile, service)
    while services:
        service()

    def join(at, carry):
        here = pl.ds(pl.multiple_of(at * tile, tile), tile)
        joined[here, pl.ds(0, query_width)] = side_by_side(out_heads, here)
        return carry

    lax.fori_loop(0, tiles, join, 0)
    mine.wait()
    for copy in to_plane:
        copy.wait()

    def out(at, carry):
        here = pl.ds(pl.multiple_of(at * tile, tile), tile)
        moved = dot(to_slots(pos_column, here, tile), joined[:, pl.ds(0, query_width)]).astype(LOW)
        attended[here, :] = moved
        part[here, :] = dot(moved, out_rows[...]).astype(LOW)
        return carry

    lax.fori_loop(0, tiles, out, 0)
    finish(cube_sum(links, part, land, acc, rows))
    value = acc[pl.ds(0, rows), :] + rows_of(seq, links.ctx, rows)[...].astype(jnp.float32)
    resid[...] = value
    scale = lax.rsqrt(jnp.mean(value * value, axis=1, keepdims=True) + EPS)
    low = swap_order((value * scale * gain_row(1)).astype(LOW), n_fsdp, n_ctx)
    rows_of(normed_mlp, links.fsdp, rows)[...] = low
    line_normed = line_gather(links, [normed_mlp], [rows])
    in_turns(line_normed)
    for copy in gate_strips:
        copy.wait()
    plane_gate = cube_gather(links, gate_all, strip * n_fsdp)
    in_turns(plane_gate, line_normed)
    for copy in up_strips:
        copy.wait()
    plane_up = cube_gather(links, up_all, strip * n_fsdp)
    line_upstream = line_gather(links, [upstream_all], [rows])
    in_turns(plane_gate, plane_up, line_normed, line_upstream)
    in_turns(plane_gate, plane_up, line_normed, line_upstream, plane_up, line_upstream)
    finish(plane_gate, line_normed, plane_up, line_upstream)


def forward(n_ctx, n_fsdp, block, positions, own, w_query, kv, w_out, gains, w_gate, w_up, upstream, tables):
    rows, width = own.shape
    length = rows * n_ctx
    weight_rows = kv.shape[0]
    total = weight_rows * n_fsdp
    query_width, out_width = w_query.shape[1] // n_ctx, width // n_ctx
    ff_rows = w_gate.shape[1] // n_fsdp
    heads, kv_heads = query_width // HEAD_DIM, kv.shape[1] // (2 * HEAD_DIM)
    tile = block * (4 if length <= 1024 else 2)
    shape = jax.ShapeDtypeStruct
    return communicate(
        functools.partial(forward_kernel, n_ctx, n_fsdp, tile),
        1,
        "forward",
        (*positions, own, w_query, kv, w_out, gains, w_gate, w_up, upstream, *tables),
        [VMEM] * 2 + [ANY] * 8 + [VMEM] * 2,
        [
            shape((total, ff_rows), LOW),
            shape((total, ff_rows), LOW),
            shape((rows * n_fsdp, width), LOW),
            shape((total, query_width), LOW),
            shape((total, kv.shape[1]), LOW),
            shape((gains.shape[0] * n_fsdp, gains.shape[1]), jnp.float32),
            shape((total // n_ctx, width), LOW),
            shape((length, width), LOW),
            shape((heads, length, HEAD_DIM), LOW),
            shape((kv_heads, length, HEAD_DIM), LOW),
            shape((kv_heads, length, HEAD_DIM), LOW),
            shape((length, 128), jnp.float32),
            shape((length, query_width), LOW),
            shape((rows, width), jnp.float32),
            shape((rows * n_fsdp, width), LOW),
        ],
        [ANY] * 3 + [VMEM] * 12,
        [
            pltpu.VMEM((length, width), LOW),
            pltpu.VMEM((total, out_width), LOW),
            pltpu.VMEM((heads, length, HEAD_DIM), LOW),
            pltpu.VMEM((length, query_width + kv.shape[1]), LOW),
            pltpu.VMEM((length, width), LOW),
        ]
        + cube_scratch(n_ctx, rows, width)
        + [pltpu.SemaphoreType.DMA((8,))],
        5 * (n_ctx - 1) + 14 * (n_fsdp - 1) + 2 * (n_fsdp - 1),
        160,
    )


def backward_kernel(
    n_ctx,
    n_fsdp,
    tile,
    pos_row,
    pos_column,
    mlp_part,
    down_part,
    out_part,
    own,
    upstream,
    resid,
    gain_mlp,
    gain_attn,
    w_q,
    w_kv,
    w_out,
    cosine,
    sine,
    q_heads,
    k_head,
    v_head,
    logs,
    attended,
    down_all,
    grad_out,
    d_joined,
    d_own,
    output,
    terms,
    seq,
    d_resid,
    line_land,
    total,
    out_land,
    out_total,
    down_land,
    land,
    acc,
    joined,
    d_heads,
    dq_heads,
    dk_head,
    dv_head,
    local_sem,
    send_sems,
    recv_sems,
):
    links = Links(n_ctx, n_fsdp, send_sems, recv_sems)
    rows, down_rows = own.shape[0], down_all.shape[0] // n_ctx
    length, query_width, kv_width = seq.shape[0], w_q.shape[1], w_kv.shape[1] // 2
    tiles = length // tile
    links.greet(cube=True, line=True)
    line = line_sum(links, mlp_part, line_land, total, rows)
    summed_here = out_part.shape[0] > rows
    line_out = line_sum(links, out_part, out_land, out_total, rows) if summed_here else iter(())
    down_here = down_part.shape[0] > down_rows
    plane_down = cube_sum(links, down_part, down_land, acc, down_rows) if down_here else iter(())
    in_turns(line, plane_down, plane_down, line, line, plane_down)
    finish(line)
    d_normed = swap_order(total[...], n_ctx, n_fsdp)
    value = resid[...]
    scale = lax.rsqrt(jnp.mean(value * value, axis=1, keepdims=True) + EPS)
    unit = value * scale
    terms[1:2, :] = jnp.sum(d_normed * unit, axis=0, keepdims=True)
    value = upstream[...].astype(jnp.float32) + norm_back(d_normed, gain_mlp[...], unit, scale)
    d_resid[...] = value
    rows_of(seq, links.ctx, rows)[...] = value.astype(LOW)
    plane = cube_gather(links, seq, rows)
    in_turns(plane, line_out)
    finish(plane_down)
    if down_here:
        down_land[pl.ds(0, down_rows), :] = acc[pl.ds(0, down_rows), :].astype(LOW)
    down_low = down_land.at[pl.ds(0, down_rows)] if down_here else down_part
    mine = pltpu.make_async_copy(down_low, rows_of(down_all, links.ctx, down_rows), local_sem)
    mine.start()
    finish(plane)
    mine.wait()
    plane_all = cube_gather(links, down_all, down_rows)
    in_turns(plane_all, line_out)
    grad_rows = pl.ds(0, query_width)
    acc[grad_rows, :] = jnp.zeros((query_width, acc.shape[1]), jnp.float32)

    def begin(at, carry):
        here = pl.ds(pl.multiple_of(at * tile, tile), tile)
        mine = seq[here, :]
        acc[grad_rows, :] += dot_dims(attended[here, :], mine, 0, 0)
        joined[here, pl.ds(0, query_width)] = dot_dims(mine, w_out[...], 1, 1).astype(LOW)
        return carry

    lax.fori_loop(0, tiles, begin, 0)

    def sort(at, carry):
        here = pl.ds(pl.multiple_of(at * tile, tile), tile)
        moved = dot(to_positions(pos_row, at, tile), joined[:, pl.ds(0, query_width)]).astype(LOW)
        split_heads(moved, d_heads, here)
        return carry

    lax.fori_loop(0, tiles, sort, 0)
    grad_out[...] = acc[grad_rows, :].astype(LOW)
    services = [
        lambda: in_turns(line_out),
        lambda: in_turns(plane_all, line_out),
        lambda: in_turns(plane_all),
    ]

    def service():
        if services:
            services.pop(0)()

    attend_back(q_heads, k_head, v_head, d_heads, logs, dq_heads, dk_head, dv_head, tile, service)
    while services:
        service()

    def end(at, carry):
        here = pl.ds(pl.multiple_of(at * tile, tile), tile)
        cos, sin = cosine[here, :], sine[here, :]
        d_query = turned(side_by_side(dq_heads, here), cos, sin, True)
        joined[here, pl.ds(0, query_width)] = d_query.astype(LOW)
        both = jnp.concatenate([side_by_side(dk_head, here), side_by_side(dv_head, here)], axis=1)
        keys = lanes(both.shape) < kv_width
        both = jnp.where(keys, turned(both, cos, sin, True), both)
        joined[here, pl.ds(query_width, 2 * kv_width)] = both.astype(LOW)
        return carry

    lax.fori_loop(0, tiles, end, 0)

    def out(at, carry):
        here = pl.ds(pl.multiple_of(at * tile, tile), tile)
        moved = dot(to_slots(pos_column, here, tile), joined[...]).astype(LOW)
        d_joined[here, :] = moved
        both = dot_dims(moved[:, :query_width], w_q[...], 1, 1)
        both += dot_dims(moved[:, query_width:], w_kv[...], 1, 1)
        seq[here, :] = both.astype(LOW)
        return carry

    lax.fori_loop(0, tiles, out, 0)
    plane = cube_sum(links, seq, land, acc, rows)
    in_turns(plane)
    finish(line_out)
    out_sum = out_total[...] if summed_here else out_part[...].astype(jnp.float32)
    output[...] = (resid[...] + out_sum).astype(LOW)
    in_turns(plane, plane)
    finish(plane)
    d_normed = acc[pl.ds(0, rows), :]
    value = own[...].astype(jnp.float32)
    scale = lax.rsqrt(jnp.mean(value * value, axis=1, keepdims=True) + EPS)
    unit = value * scale
    terms[0:1, :] = jnp.sum(d_normed * unit, axis=0, keepdims=True)
    d_own[...] = (d_resid[...] + norm_back(d_normed, gain_attn[...], unit, scale)).astype(LOW)
    finish(plane_all)


def backward(
    n_ctx, n_fsdp, block, positions, parts, own, upstream, resid, gains, weights, tables, saved
):
    rows, width = own.shape
    length = rows * n_ctx
    down_here = length <= 1024
    down_rows = parts[1].shape[0] // (n_ctx if down_here else 1)
    q_heads, k_head = saved[0], saved[1]
    joined_width = weights[0].shape[1] + weights[1].shape[1]
    tile = block * (4 if length <= 1024 else 2)
    shape = jax.ShapeDtypeStruct
    wide = jnp.float32
    return communicate(
        functools.partial(backward_kernel, n_ctx, n_fsdp, tile),
        3,
        "backward",
        (*positions, *parts, own, upstream, resid, *gains, *weights, *tables, *saved),
        [VMEM] * 20,
        [
            shape((down_rows * n_ctx, width), LOW),
            shape((weights[0].shape[1], width), LOW),
            shape((length, joined_width), LOW),
            shape((rows, width), LOW),
            shape((rows, width), LOW),
            shape((2, width), wide),
        ],
        [ANY] + [VMEM] * 5,
        [pltpu.VMEM((length, width), LOW), pltpu.VMEM((rows, width), wide)]
        + line_scratch(n_fsdp, rows, width)
        + (line_scratch(n_fsdp, rows, width) if parts[2].shape[0] > rows else line_scratch(2, 8, 128))
        + (cube_scratch(n_ctx, down_rows, width)[:1] if down_here else cube_scratch(2, 16, 128)[:1])
        + cube_scratch(n_ctx, rows, width)[:1]
        + [
            pltpu.VMEM((max(max(1, n_ctx // 4) * max(rows, down_rows), weights[0].shape[1]), width), wide),
            pltpu.VMEM((length, joined_width), LOW),
            pltpu.VMEM(q_heads.shape, LOW),
            pltpu.VMEM(q_heads.shape, wide),
            pltpu.VMEM(k_head.shape, wide),
            pltpu.VMEM(k_head.shape, wide),
            pltpu.SemaphoreType.DMA(()),
        ],
        4 * (n_ctx - 1) + 4 * (n_fsdp - 1),
        160,
    )


def feed_forward_kernel(
    normed, upstream, w_gate, w_up, w_down, d_part, out_part, down, pair, flipped, d_acc, out_acc, held, sems
):
    at, steps = pl.program_id(0), pl.num_programs(0)
    chunk, ff_rows = w_gate.shape[1], pair.shape[1] // 2
    slot = lax.rem(at, 2)

    def leave(which, part, step):
        column = pl.multiple_of(part * ff_rows + step * chunk, chunk)
        return pltpu.make_async_copy(
            held.at[which, part], pair.at[:, pl.ds(column, chunk)], sems.at[which, part]
        )

    @pl.when(at == 0)
    def _():
        flipped[...] = normed[...].T
        d_acc[...] = jnp.zeros_like(d_acc)
        out_acc[...] = jnp.zeros_like(out_acc)

    gate_pre, up_pre = dot(normed[...], w_gate[...]), dot(normed[...], w_up[...])
    sigma = 1.0 / (1.0 + jnp.exp(-gate_pre))
    swish = gate_pre * sigma
    hidden = (swish * up_pre).astype(LOW)
    d_hidden = dot_dims(upstream[...], w_down[...], 1, 1)
    d_gate = (d_hidden * up_pre * sigma * (1.0 + gate_pre * (1.0 - sigma))).astype(LOW)
    d_up = (d_hidden * swish).astype(LOW)
    down[...] = dot_dims(hidden, upstream[...], 0, 0).astype(LOW)

    @pl.when(at >= 2)
    def _():
        for part in (0, 1):
            leave(slot, part, at - 2).wait()

    held[slot, 0] = dot(flipped[...], d_gate).astype(LOW)
    held[slot, 1] = dot(flipped[...], d_up).astype(LOW)
    for part in (0, 1):
        leave(slot, part, at).start()
    d_acc[...] += dot_dims(d_gate, w_gate[...], 1, 1) + dot_dims(d_up, w_up[...], 1, 1)
    out_acc[...] += dot(hidden, w_down[...])

    @pl.when(at == steps - 1)
    def _():
        d_part[...] = d_acc[...].astype(LOW)
        out_part[...] = out_acc[...].astype(LOW)

        @pl.when(steps > 1)
        def _():
            for part in (0, 1):
                leave(1 - slot, part, at - 1).wait()

        for part in (0, 1):
            leave(slot, part, at).wait()


def feed_forward(normed, upstream, w_gate, w_up, w_down):
    count, width = normed.shape
    ff_rows = w_down.shape[0]
    chunk = min(ff_rows, 512 if count <= 512 else 256)
    whole = pl.BlockSpec((count, width), lambda f: (0, 0), pipeline_mode=pl.Buffered(1))
    tall = pl.BlockSpec((width, chunk), lambda f: (0, f))
    flat = pl.BlockSpec((chunk, width), lambda f: (f, 0))
    shape = jax.ShapeDtypeStruct
    return pl.pallas_call(
        feed_forward_kernel,
        grid=(ff_rows // chunk,),
        in_specs=[whole, whole, tall, tall, flat],
        out_specs=[whole, whole, flat, ANY],
        out_shape=[
            shape((count, width), LOW),
            shape((count, width), LOW),
            shape((ff_rows, width), LOW),
            shape((width, 2 * ff_rows), LOW),
        ],
        scratch_shapes=[
            pltpu.VMEM((width, count), LOW),
            pltpu.VMEM((count, width), jnp.float32),
            pltpu.VMEM((count, width), jnp.float32),
            pltpu.VMEM((2, 2, width, chunk), LOW),
            pltpu.SemaphoreType.DMA((2, 2)),
        ],
        compiler_params=pltpu.CompilerParams(vmem_limit_bytes=60 << 20),
        cost_estimate=pl.CostEstimate(flops=0, bytes_accessed=150_000_000, transcendentals=0),
        name="feed_forward",
    )(normed, upstream, w_gate, w_up, w_down)


class ChunkSum:
    def __init__(self, links, land, rows):
        self.links, self.land, self.rows = links, land, rows
        self.count = links.n_ctx // 2
        self.levels = len(links.order) + 1
        self.offsets, self.theirs = [0], [0]
        for step, other in zip(links.order, links.order[::-1]):
            self.offsets = self.offsets + [offset + step for offset in self.offsets]
            self.theirs = self.theirs + [offset + other for offset in self.theirs]

    def first(self, level):
        return sum(self.count >> done for done in range(level))

    def spot(self, chunk, at):
        return pl.multiple_of((chunk * (self.links.n_ctx - 1) + at) * self.rows, self.rows)

    def transfer(self, part, chunk, level, at):
        links = self.links
        target = self.land.at[pl.ds(self.spot(chunk, self.first(level) + at), self.rows)]
        if level == 0:
            source = rows_of(part, links.ctx + links.sibling + self.theirs[at], self.rows)
            step = links.sibling
        else:
            source = self.land.at[pl.ds(self.spot(chunk, at + (self.count >> level)), self.rows)]
            step = links.order[len(links.order) - level]
        links.used = chunk * (links.n_ctx - 1) + self.first(level) + at
        return links.copy(source, target, links.ctx + step, links.fsdp)

    def start(self, part, chunk):
        for at in range(self.count):
            self.transfer(part, chunk, 0, at).start()

    def sent(self, part, chunk, level):
        for at in range(self.count >> level):
            self.transfer(part, chunk, level, at).wait_send()

    def meet(self, part, chunk, level, leave):
        count = self.count >> level
        half = count // 2
        wide = jnp.float32
        for at in list(range(half, count)) + list(range(half)):
            self.transfer(part, chunk, level, at).wait_recv()
            kept, landing = self.spot(chunk, at), self.spot(chunk, self.first(level) + at)

            def add(start, size):
                landed = self.land[pl.ds(pl.multiple_of(landing + start, size), size), :].astype(wide)
                place = pl.ds(pl.multiple_of(kept + start, size), size)
                if level == 0:
                    base = (self.links.ctx + self.offsets[at]) * self.rows
                    mine = part[pl.ds(pl.multiple_of(base + start, size), size), :]
                else:
                    mine = self.land[place, :]
                total = mine.astype(wide) + landed
                if count == 1:
                    leave(start, size, total)
                else:
                    self.land[place, :] = total.astype(LOW)

            in_rows(self.rows, add)
            if count > 1 and at >= half:
                self.transfer(part, chunk, level + 1, at - half).start()


def feed_forward_sum_kernel(
    n_ctx,
    n_fsdp,
    normed,
    upstream,
    w_gate,
    w_up,
    w_down,
    d_part,
    out_part,
    down,
    pair,
    flipped,
    d_acc,
    out_acc,
    held,
    land,
    local_sems,
    send_sems,
    recv_sems,
):
    at, steps = pl.program_id(0), w_down.shape[0]
    chunk, ff_rows, width = w_gate.shape[1], pair.shape[2], normed.shape[1]
    count, steps = normed.shape[0], pair.shape[2] // w_gate.shape[1]
    links = Links(n_ctx, n_fsdp, send_sems, recv_sems)
    sums = ChunkSum(links, land, width // n_ctx)
    slot, other = lax.rem(at, 2), lax.rem(at + 1, 2)
    last = sums.levels - 1

    def meet(step, level):
        part = held.at[lax.rem(step, 2)]
        column = pl.multiple_of(step * chunk, chunk)

        def leave(start, size, total):
            low = total.astype(LOW)
            for which in (0, 1):
                pair[which, pl.ds(start, size), pl.ds(column, chunk)] = low[:, which * chunk : (which + 1) * chunk]

        sums.meet(part, step, level, leave)

    @pl.when(at == 0)
    def _():
        links.greet(cube=True)
        flipped[...] = normed[...].T
        d_acc[...] = jnp.zeros_like(d_acc)
        out_acc[...] = jnp.zeros_like(out_acc)

    gate_pre, up_pre = dot(normed[...], w_gate[...]), dot(normed[...], w_up[...])
    sigma = 1.0 / (1.0 + jnp.exp(-gate_pre))
    swish = gate_pre * sigma
    hidden = (swish * up_pre).astype(LOW)
    d_hidden = dot_dims(upstream[...], w_down[...], 1, 1)
    d_gate = (d_hidden * up_pre * sigma * (1.0 + gate_pre * (1.0 - sigma))).astype(LOW)
    d_up = (d_hidden * swish).astype(LOW)

    @pl.when(at >= 1)
    def _():
        meet(at - 1, 0)

    @pl.when(at >= 2)
    def _():
        meet(at - 2, 1)
        sums.sent(held.at[slot], at - 2, 0)

    held[slot, :, pl.ds(0, chunk)] = dot(flipped[...], d_gate).astype(LOW)
    held[slot, :, pl.ds(chunk, chunk)] = dot(flipped[...], d_up).astype(LOW)
    sums.start(held.at[slot], at)
    down[...] = dot_dims(hidden, upstream[...], 0, 0).astype(LOW)
    d_acc[...] += dot_dims(d_gate, w_gate[...], 1, 1) + dot_dims(d_up, w_up[...], 1, 1)
    out_acc[...] += dot(hidden, w_down[...])
    for level in range(2, last + 1):

        @pl.when(at >= 2)
        def _():
            meet(at - 2, level)

    @pl.when(at == steps - 1)
    def _():
        meet(at, 0)
        meet(at - 1, 1)
        sums.sent(held.at[other], at - 1, 0)
        leaving = []
        for which, (acc, goal) in enumerate(((d_acc, d_part), (out_acc, out_part))):
            for piece in range(width // (2 * chunk)):
                spot = pl.ds((which * (width // (2 * chunk)) + piece) * count, count)
                columns = pl.ds(piece * 2 * chunk, 2 * chunk)
                held[other, spot, :] = acc[:, columns].astype(LOW)
                copy = pltpu.make_async_copy(
                    held.at[other, spot], goal.at[:, columns], local_sems.at[len(leaving)]
                )
                copy.start()
                leaving.append(copy)
        for level in range(2, last + 1):
            meet(at - 1, level)
        meet(at, 1)
        for level in range(2, last + 1):
            meet(at, level)
        sums.sent(held.at[slot], at, 0)
        for copy in leaving:
            copy.wait()
        for step in range(steps):
            for level in range(1, last + 1):
                sums.sent(held.at[0], step, level)


def feed_forward_sum(n_ctx, n_fsdp, normed, upstream, w_gate, w_up, w_down):
    count, width = normed.shape
    ff_rows = w_down.shape[0]
    chunk = 512
    steps, rows = ff_rows // chunk, width // n_ctx
    whole = pl.BlockSpec((count, width), lambda f: (0, 0), pipeline_mode=pl.Buffered(1))
    tall = pl.BlockSpec((width, chunk), lambda f: (0, f))
    flat = pl.BlockSpec((chunk, width), lambda f: (f, 0))
    both = pl.BlockSpec((2, rows, ff_rows), lambda f: (0, 0, 0), pipeline_mode=pl.Buffered(1))
    shape = jax.ShapeDtypeStruct
    copies = steps * (n_ctx - 1)
    return pl.pallas_call(
        functools.partial(feed_forward_sum_kernel, n_ctx, n_fsdp),
        grid=(steps,),
        in_specs=[whole, whole, tall, tall, flat],
        out_specs=[ANY, ANY, flat, both],
        out_shape=[
            shape((count, width), LOW),
            shape((count, width), LOW),
            shape((ff_rows, width), LOW),
            shape((2, rows, ff_rows), LOW),
        ],
        scratch_shapes=[
            pltpu.VMEM((width, count), LOW),
            pltpu.VMEM((count, width), jnp.float32),
            pltpu.VMEM((count, width), jnp.float32),
            pltpu.VMEM((2, width, 2 * chunk), LOW),
            pltpu.VMEM((copies * rows, 2 * chunk), LOW),
            pltpu.SemaphoreType.DMA((2 * width // (2 * chunk),)),
            pltpu.SemaphoreType.DMA((copies,)),
            pltpu.SemaphoreType.DMA((copies,)),
        ],
        compiler_params=pltpu.CompilerParams(
            collective_id=2, has_side_effects=True, vmem_limit_bytes=62 << 20
        ),
        name="feed_forward_sum",
    )(normed, upstream, w_gate, w_up, w_down)


def on_device(
    tokens,
    cotangent,
    pairing,
    norm_attn,
    w_query,
    w_key,
    w_value,
    w_out,
    norm_mlp,
    w_gate,
    w_up,
    w_down,
):
    n_ctx, n_fsdp = lax.axis_size("ctx"), lax.axis_size("fsdp")
    ctx = lax.axis_index("ctx")
    own_tokens = tokens[0]
    tok_rows, width = own_tokens.shape
    length = tok_rows * n_ctx
    rows_model = w_gate.shape[0]
    low = LOW

    query_width = w_query.shape[1] // n_ctx
    heads_kv = w_key.shape[1] // HEAD_DIM
    kv_here = max(1, heads_kv // n_ctx)
    sharers = max(1, n_ctx // heads_kv)
    kv_width = kv_here * HEAD_DIM
    kv_start = (ctx // sharers) * kv_width

    def columns(matrix, start, size):
        return lax.dynamic_slice_in_dim(matrix, start, size, 1)

    kv = jnp.concatenate([columns(w_key, kv_start, kv_width), columns(w_value, kv_start, kv_width)], axis=1)
    gains = jnp.zeros((8, rows_model), jnp.float32).at[0].set(norm_attn).at[1].set(norm_mlp)
    upstream = cotangent[0]
    block = tok_rows // pairing.shape[1]
    all_pos = slot_positions(pairing, length, block)
    positions = (all_pos[None, :], all_pos[:, None])

    def tables_at(places):
        return [jnp.tile(t[:, 0], (1, 128 // HEAD_DIM)) for t in rotation(places, HEAD_DIM)]

    (
        gate_full,
        up_full,
        upstream_all,
        w_q,
        w_kv,
        gains,
        w_out_rows,
        normed_attn,
        q_heads,
        k_head,
        v_head,
        logs,
        attended_low,
        resid,
        normed_mlp,
    ) = forward(
        n_ctx,
        n_fsdp,
        block,
        positions,
        own_tokens,
        w_query,
        kv,
        w_out,
        gains,
        w_gate,
        w_up,
        upstream,
        tables_at(all_pos),
    )
    gains = gains.reshape(n_fsdp, 8, rows_model)
    gain_attn, gain_mlp = gains[:, 0].reshape(1, -1), gains[:, 1].reshape(1, -1)
    out_width = width // n_ctx
    ff_rows = w_down.shape[0]
    strip = rows_model // n_ctx

    if length <= 1024:
        mlp_part, out_part, down_part, pair = feed_forward_sum(
            n_ctx, n_fsdp, normed_mlp, upstream_all, gate_full, up_full, w_down
        )
    else:
        mlp_part, out_part, down_part, pair = feed_forward(
            normed_mlp, upstream_all, gate_full, up_full, w_down
        )
        pair, down_part = scatter_sum(pair, "ctx"), scatter_sum(down_part, "ctx")
        pair = jnp.stack([pair[:, :ff_rows], pair[:, ff_rows:]])
        out_part = scatter_sum(out_part, "fsdp")

    grad_down, grad_out, d_joined, d_inputs, output, terms = backward(
        n_ctx,
        n_fsdp,
        block,
        positions,
        (mlp_part, down_part, out_part),
        own_tokens,
        upstream,
        resid,
        (gain_mlp, gain_attn),
        (w_q, w_kv, w_out_rows),
        tables_at(jnp.arange(length, dtype=jnp.int32)),
        (q_heads, k_head, v_head, logs, attended_low),
    )
    grad_joined = tokens_t(normed_attn, d_joined).astype(low)
    terms = terms.reshape(2, n_fsdp, rows_model)
    attn_width = query_width + 2 * kv_width + out_width
    pad = ((0, 0), (0, 14), (0, attn_width - rows_model))
    terms = jnp.pad(terms.transpose(1, 0, 2).astype(low), pad).reshape(n_fsdp * 16, attn_width)
    grad_gate, grad_up, grad_attn = tail(n_ctx, n_fsdp, pair, grad_joined, grad_out, terms)
    grad_gate, grad_up, grad_down = widen(grad_gate, grad_up, grad_down)
    grad_attn = grad_attn.reshape(n_ctx, rows_model + 16, attn_width)
    terms = jnp.sum(grad_attn[:, rows_model : rows_model + 2, :rows_model].astype(jnp.float32), axis=0)
    grad_query, grad_key, grad_value, grad_out = spread(
        grad_attn, rows_model, (query_width, kv_width, kv_width, out_width), (1, sharers, sharers, 1)
    )

    return (
        output[None],
        d_inputs[None],
        terms[0],
        grad_query,
        grad_key,
        grad_value,
        grad_out,
        terms[1],
        grad_gate,
        grad_up,
        grad_down,
    )


def solution(mesh):
    return jax.shard_map(
        on_device,
        mesh=mesh,
        in_specs=(
            P("fsdp", "ctx", None),
            P("fsdp", "ctx", None),
            P(),
            P("fsdp"),
            P("fsdp", None),
            P("fsdp", None),
            P("fsdp", None),
            P("fsdp", None),
            P("fsdp"),
            P("fsdp", None),
            P("fsdp", None),
            P("fsdp", None),
        ),
        out_specs=(
            P("fsdp", "ctx", None),
            P("fsdp", "ctx", None),
            P("fsdp"),
            P("fsdp", None),
            P("fsdp", None),
            P("fsdp", None),
            P("fsdp", None),
            P("fsdp"),
            P("fsdp", None),
            P("fsdp", None),
            P("fsdp", None),
        ),
        check_vma=False,
    )
```

time: 755 us -> 650 us (0.86)
  Pallas kernels: 517 us -> 617 us
  matrix products: 92.6 us -> 5.93 us
  waiting for transfers between devices: 40.1 us -> 0 us
  other arithmetic: 36.1 us -> 3.45 us
  local copies, waits for them, and re-layouts: 36 us -> 13.9 us
  between operations: 14.6 us -> 1.07 us
  starting transfers between devices: 11.8 us -> 0 us
    pallas_call x2, Pallas kernels: 50.4 us -> 122 us  [the longest x1 98.6 us: feed_forward_sum(): pl.pallas_call(functools.partial(feed_forward_sum_kernel, n_ctx, n_fsdp),...]
    dot_general x6 -> x0, matrix products: 59.6 us -> none  [the longest x3 33 us: product(): return jnp.dot(left, right, preferred_element_type=jnp.float32)]
    ppermute x9 -> x0, waiting for transfers between devices: 39.9 us -> none  [by_permutes(): lax.ppermute(piece, axis, [(i, (i + shift) % count) for i in range(count)])]
    convert_element_type x3 -> x1, other arithmetic: 35.2 us -> 0.01 us  [on_device(): terms.transpose(1, 0, 2).astype(low)]
    pallas_call x5 -> x3, Pallas kernels: 461 us -> 489 us  [communicate(): pl.pallas_call(kernel, out_shape=outs, in_specs=in_specs, out_specs=out_s...]
    dot_general x5 -> x1, matrix products: 33 us -> 5.93 us  [tokens_t(): lax.dot_general(left, right, (((0,), (0,)), ((), ())), preferred_element_...]
    unnamed x73 -> x17, local copies, waits for them, and re-layouts: 22 us -> 5.49 us
    ppermute x9 -> x0, starting transfers between devices: 11.2 us -> none  [by_permutes(): lax.ppermute(piece, axis, [(i, (i + shift) % count) for i in range(count)])]
  transfers between devices with their start and end apart: 13 -> 0, of which waited for: 6 -> 0; matrix products, arithmetic and copies ran while one was open for 7% -> 0% of each run, Pallas kernels for 39% -> 0%
where the time goes in v4:
time: 650 us; the launch traced here: 641 us
  Pallas kernels  617 us (95%)
  local copies, waits for them, and re-layouts  13.9 us (2%)
    pallas_call x3, Pallas kernels, communicate(): pl.pallas_call(kernel, out_shape=outs, in_specs=in_specs, out_specs=out_s...  489 us
    pallas_call x1, Pallas kernels, feed_forward_sum(): pl.pallas_call(functools.partial(feed_forward_sum_kernel, n_ctx, n_fsdp),...  98.6 us
    pallas_call x1, Pallas kernels, widen(): pl.pallas_call(widen_kernel, grid=(steps,), in_specs=specs, out_specs=spe...  23.7 us

profile of v4, /device:TPU:17, one launch (start us, length us, event | category | flops | bytes accessed | tf_op | source)
XLA Modules:
  0.0 641.1 jit_solution(3864900284698507268)
XLA Ops:
  0.6 0.0 copy-start.5
  0.7 0.0 copy-start.6
  0.7 1.1 constant_dynamic-slice_fusion
  1.8 0.8 pad_maximum_fusion.4.kv
  2.6 0.8 copy.36
  3.3 0.1 broadcast_in_dim.18
  3.4 0.1 select_reduce_fusion
  3.5 1.0 multiply_sine_fusion
  4.6 1.0 copy.38.cosine
  5.7 1.0 copy.39.sine
  6.7 0.2 copy.37
  6.9 0.9 fusion.pos_column
  7.8 0.6 fusion.10.pos_row
  8.4 0.0 copy-done.5
  8.4 0.0 copy-done.6
  8.4 0.1 scatter.9.gains
  8.4 0.0 copy-start.3
  8.4 0.6 copy-done.3
  9.0 185.2 %forward.1 = (bf16[2048,2048]{1,0:T(8,128)(2,1)}, bf16[2048,2048]{1,0:T(8,128)(2,1)}, bf16[512,2048]{1,0:T(8,128)(2,1)}, bf16[2048,256]{1,0:T(8,128)(2,1)}, bf16...) custom-call(s32[1,1024]{1,0:T(1,128)} %fusion.10.pos_row, ...), custom_call_target="tpu_custom_call" | custom-call | bytes 480000000 | tf_op jit(solution)/shard_map/forward/pallas_call | solution.py:371
  194.3 98.6 %feed_forward_sum.1 = (bf16[512,2048]{1,0:T(8,128)(2,1)}, bf16[512,2048]{1,0:T(8,128)(2,1)}, bf16[2048,2048]{1,0:T(8,128)(2,1)}, bf16[2,256,2048]{2,1,0:T(8,128)(2,1)}) custom-call(bf16[512,2048]{1,0:T(8,128)(2,1)} %get-tuple-element.70.normed, bf16[512,2048]{1,0:T(8,128)(2,1)} %get-tuple-element.71.upstream, bf16[2048,2048]{1,0:T(8,128)(2,1)} %get-tuple-element.72.w_gate, ...), custom_call_target="tpu_custom_call" | custom-call | tf_op jit(solution)/shard_map/feed_forward_sum/pallas_call | solution.py:1390
  292.9 1.5 fusion.14
  294.5 1.0 copy.42.cosine
  295.6 1.0 copy.43.sine
  296.6 164.7 %backward.1 = (bf16[2048,2048]{1,0:T(8,128)(2,1)}, bf16[256,2048]{1,0:T(8,128)(2,1)}, bf16[1024,384]{1,0:T(8,128)(2,1)}, bf16[128,2048]{1,0:T(8,128)(2,1)}, bf16...) custom-call(s32[1,1024]{1,0:T(1,128)} %fusion.10.pos_row, s32[1024,1]{1,0:T(8,128)} %fusion.pos_column, ...), custom_call_target="tpu_custom_call" | custom-call | bytes 480000000 | tf_op jit(solution)/shard_map/backward/pallas_call | solution.py:371
  461.3 0.0 copy-start.4
  461.3 5.9 convolution_convert_fusion.joined
  467.2 0.0 copy-done.4
  467.2 0.6 pad.9
  467.9 139.2 %tail.1 = (bf16[512,8192]{1,0:T(8,128)(2,1)}, bf16[512,8192]{1,0:T(8,128)(2,1)}, bf16[4224,640]{1,0:T(8,128)(2,1)}) custom-call(bf16[2,256,2048]{2,1,0:T(8,128)(2,1)} %get-tuple-element.89.pair, bf16[2048,384]{1,0:T(8,128)(2,1)} %convolution_convert_fusion.joined, bf16[256,2048]{1,0:T(8,128)(2,1)} %get-tuple-element.92.out_part, bf16[64,640]{1,0:T(8,128)(2,1)} %bitcast.36), custom_call_target="tpu_custom_call" | custom-call | bytes 390000000 | tf_op jit(solution)/shard_map/tail/pallas_call | solution.py:371
  607.1 0.0 copy-start.2
  607.1 0.0 copy-start.1
  607.1 23.7 %widen.1 = (f32[512,8192]{1,0:T(8,128)}, f32[512,8192]{1,0:T(8,128)}, f32[2048,2048]{1,0:T(8,128)}) custom-call(bf16[512,8192]{1,0:T(8,128)(2,1)} %get-tuple-element.99.refs_0_, bf16[512,8192]{1,0:T(8,128)(2,1)} %get-tuple-element.100.refs_1_, bf16[2048,2048]{1,0:T(8,128)(2,1)} %get-tuple-element.101.refs_2_), custom_call_target="tpu_custom_call" | custom-call | tf_op jit(solution)/shard_map/widen/pallas_call | solution.py:525
  630.8 0.0 copy-start
  630.8 2.5 copy-done
  633.3 5.3 spread.1
  638.6 0.6 fusion.15
  639.2 0.0 copy-done.2
  639.2 0.8 copy.50
  640.0 0.0 copy-done.1
  640.0 0.8 copy.51
  (13 shorter events, 0.3 us)
Async XLA Ops:
  0.6 7.7 %copy-start.5 = (f32[512]{0:T(512)S(1)}, f32[512]{0:T(512)}, u32[]{:S(2)}) copy-start(f32[512]{0:T(512)} %param.19) | copy-start | bytes 6148
  0.7 7.7 %copy-start.6 = (f32[512]{0:T(512)S(1)}, f32[512]{0:T(512)}, u32[]{:S(2)}) copy-start(f32[512]{0:T(512)} %param.24) | copy-start | bytes 6148
  8.4 0.6 copy-start.3
  461.3 5.9 copy-start.4
  607.1 32.1 %copy-start.2 = (bf16[128,2048]{1,0:T(8,128)(2,1)S(1)}, bf16[128,2048]{1,0:T(8,128)(2,1)}, u32[]{:S(2)}) copy-start(bf16[128,2048]{1,0:T(8,128)(2,1)} %get-tuple-element.87) | copy-start | bytes 1572868
  607.1 32.9 %copy-start.1 = (bf16[128,2048]{1,0:T(8,128)(2,1)S(1)}, bf16[128,2048]{1,0:T(8,128)(2,1)}, u32[]{:S(2)}) copy-start(bf16[128,2048]{1,0:T(8,128)(2,1)} %get-tuple-element.88) | copy-start | bytes 1572868
  630.8 2.5 copy-start

commit v5 on v4

--- a/solution.py
+++ b/solution.py
@@ -477,7 +477,7 @@
     for copy in to_shards[1]:
         copy.wait()
     plane_up = cube_gather(links, up_all, strip)
-    in_turns(plane_gate, plane_up, line, plane_gate, line, plane_up, line)
+    in_turns(plane_up, plane_gate, line, line, plane_gate, plane_up, line)
     finish(line)
     attn_low[...] = total[...].astype(LOW)
     mine = pltpu.make_async_copy(attn_low, rows_of(attn_all, links.ctx, rows), local_sems.at[0])
@@ -513,56 +513,39 @@
     )
 
 
-def widen_kernel(*refs):
-    count = len(refs) // 2
-    for source, goal in zip(refs[:count], refs[count:]):
+def widen_kernel(widths, sharers, gathered, *refs):
+    count = (len(refs) - len(widths)) // 2
+    for source, goal in zip(refs[:count], refs[count : 2 * count]):
         goal[...] = source[...].astype(jnp.float32)
-
-
-def widen(*arrays):
-    steps = max(4, arrays[0].shape[0] // 128)
-    specs = [pl.BlockSpec((a.shape[0] // steps, a.shape[1]), lambda i: (i, 0)) for a in arrays]
-    return pl.pallas_call(
-        widen_kernel,
-        grid=(steps,),
-        in_specs=specs,
-        out_specs=specs,
-        out_shape=[jax.ShapeDtypeStruct(a.shape, jnp.float32) for a in arrays],
-        compiler_params=pltpu.CompilerParams(vmem_limit_bytes=60 << 20),
-        name="widen",
-    )(*arrays)
-
-
-def spread_kernel(parts, widths, gathered, *outs):
     at = 0
-    for out, width, sharers in zip(outs, widths, parts):
+    for out, width, group in zip(refs[2 * count :], widths, sharers):
         pieces = []
-        for i in range(0, gathered.shape[0], sharers):
+        for i in range(0, gathered.shape[0], group):
             piece = gathered[i, :, at : at + width].astype(jnp.float32)
-            for j in range(1, sharers):
+            for j in range(1, group):
                 piece = piece + gathered[i + j, :, at : at + width].astype(jnp.float32)
             pieces.append(piece)
         out[...] = jnp.concatenate(pieces, axis=1)
         at += width
 
 
-def spread(gathered, rows, widths, sharers):
+def widen(gathered, rows, widths, sharers, *arrays):
     n_ctx, _, joined = gathered.shape
     step = 2 * max(sharers)
-    tile = min(rows, 256)
+    steps = n_ctx // step
+    specs = [pl.BlockSpec((a.shape[0] // steps, a.shape[1]), lambda i: (i, 0)) for a in arrays]
+    shape = lambda *dims: jax.ShapeDtypeStruct(dims, jnp.float32)
     return pl.pallas_call(
-        functools.partial(spread_kernel, sharers, widths),
-        grid=(n_ctx // step, rows // tile),
-        in_specs=[pl.BlockSpec((step, tile, joined), lambda i, j: (i, j, 0))],
-        out_specs=[
-            pl.BlockSpec((tile, step // s * w), lambda i, j: (j, i)) for w, s in zip(widths, sharers)
-        ],
-        out_shape=[
-            jax.ShapeDtypeStruct((rows, n_ctx // s * w), jnp.float32) for w, s in zip(widths, sharers)
-        ],
-        compiler_params=pltpu.CompilerParams(vmem_limit_bytes=32 << 20),
-        name="spread",
-    )(gathered)
+        functools.partial(widen_kernel, widths, sharers),
+        grid=(steps,),
+        in_specs=[pl.BlockSpec((step, rows, joined), lambda i: (i, 0, 0))] + specs,
+        out_specs=specs
+        + [pl.BlockSpec((rows, step // s * w), lambda i: (0, i)) for w, s in zip(widths, sharers)],
+        out_shape=[shape(*a.shape) for a in arrays]
+        + [shape(rows, n_ctx // s * w) for w, s in zip(widths, sharers)],
+        compiler_params=pltpu.CompilerParams(vmem_limit_bytes=60 << 20),
+        name="widen",
+    )(gathered, *arrays)
 
 
 def lanes(shape):
@@ -870,8 +853,8 @@
         copy.wait()
     plane_up = cube_gather(links, up_all, strip * n_fsdp)
     line_upstream = line_gather(links, [upstream_all], [rows])
-    in_turns(plane_gate, plane_up, line_normed, line_upstream)
-    in_turns(plane_gate, plane_up, line_normed, line_upstream, plane_up, line_upstream)
+    in_turns(plane_gate, plane_up, line_normed, line_upstream, line_normed, line_upstream)
+    in_turns(plane_up, plane_gate, line_upstream, plane_up, line_upstream)
     finish(plane_gate, line_normed, plane_up, line_upstream)
 
 
@@ -1526,13 +1509,17 @@
     pad = ((0, 0), (0, 14), (0, attn_width - rows_model))
     terms = jnp.pad(terms.transpose(1, 0, 2).astype(low), pad).reshape(n_fsdp * 16, attn_width)
     grad_gate, grad_up, grad_attn = tail(n_ctx, n_fsdp, pair, grad_joined, grad_out, terms)
-    grad_gate, grad_up, grad_down = widen(grad_gate, grad_up, grad_down)
     grad_attn = grad_attn.reshape(n_ctx, rows_model + 16, attn_width)
     terms = jnp.sum(grad_attn[:, rows_model : rows_model + 2, :rows_model].astype(jnp.float32), axis=0)
-    grad_query, grad_key, grad_value, grad_out = spread(
-        grad_attn, rows_model, (query_width, kv_width, kv_width, out_width), (1, sharers, sharers, 1)
+    grad_gate, grad_up, grad_down, grad_query, grad_key, grad_value, grad_out = widen(
+        grad_attn,
+        rows_model,
+        (query_width, kv_width, kv_width, out_width),
+        (1, sharers, sharers, 1),
+        grad_gate,
+        grad_up,
+        grad_down,
     )
-
     return (
         output[None],
         d_inputs[None],

time: 650 us -> 641 us (0.986)
  Pallas kernels: 617 us -> 609 us
    pallas_call x2 -> x1, Pallas kernels: 29 us -> 28.6 us  [widen(): pl.pallas_call(functools.partial(widen_kernel, widths, sharers), grid=(st...]
where the time goes in v5:
time: 641 us; the launch traced here: 632 us
  Pallas kernels  609 us (95%)
  local copies, waits for them, and re-layouts  11.4 us (2%)
    pallas_call x3, Pallas kernels, communicate(): pl.pallas_call(kernel, out_shape=outs, in_specs=in_specs, out_specs=out_s...  483 us
    pallas_call x1, Pallas kernels, feed_forward_sum(): pl.pallas_call(functools.partial(feed_forward_sum_kernel, n_ctx, n_fsdp),...  97.8 us
    pallas_call x1, Pallas kernels, widen(): pl.pallas_call(functools.partial(widen_kernel, widths, sharers), grid=(st...  28.6 us

profile of v5, /device:TPU:17, one launch (start us, length us, event | category | flops | bytes accessed | tf_op | source)
XLA Modules:
  0.0 632.1 jit_solution(12689549021793864543)
XLA Ops:
  0.6 0.0 copy-start.4
  0.7 0.0 copy-start.5
  0.7 1.1 constant_dynamic-slice_fusion
  1.8 0.8 pad_maximum_fusion.4.kv
  2.6 0.8 copy.36
  3.3 0.1 broadcast_in_dim.18
  3.4 0.1 select_reduce_fusion
  3.5 1.0 multiply_sine_fusion
  4.6 1.0 copy.38.cosine
  5.7 1.0 copy.39.sine
  6.7 0.2 copy.37
  6.9 0.9 fusion.pos_column
  7.8 0.6 fusion.10.pos_row
  8.4 0.0 copy-done.4
  8.4 0.0 copy-done.5
  8.4 0.1 scatter.9.gains
  8.4 0.0 copy-start.2
  8.4 0.6 copy-done.2
  9.0 176.0 %forward.1 = (bf16[2048,2048]{1,0:T(8,128)(2,1)}, bf16[2048,2048]{1,0:T(8,128)(2,1)}, bf16[512,2048]{1,0:T(8,128)(2,1)}, bf16[2048,256]{1,0:T(8,128)(2,1)}, bf16...) custom-call(s32[1,1024]{1,0:T(1,128)} %fusion.10.pos_row, ...), custom_call_target="tpu_custom_call" | custom-call | bytes 480000000 | tf_op jit(solution)/shard_map/forward/pallas_call | solution.py:371
  185.0 97.8 %feed_forward_sum.1 = (bf16[512,2048]{1,0:T(8,128)(2,1)}, bf16[512,2048]{1,0:T(8,128)(2,1)}, bf16[2048,2048]{1,0:T(8,128)(2,1)}, bf16[2,256,2048]{2,1,0:T(8,128)(2,1)}) custom-call(bf16[512,2048]{1,0:T(8,128)(2,1)} %get-tuple-element.70.normed, bf16[512,2048]{1,0:T(8,128)(2,1)} %get-tuple-element.71.upstream, bf16[2048,2048]{1,0:T(8,128)(2,1)} %get-tuple-element.72.w_gate, ...), custom_call_target="tpu_custom_call" | custom-call | tf_op jit(solution)/shard_map/feed_forward_sum/pallas_call | solution.py:1373
  282.9 1.5 fusion.14
  284.5 1.0 copy.42.cosine
  285.5 1.0 copy.43.sine
  286.5 169.6 %backward.1 = (bf16[2048,2048]{1,0:T(8,128)(2,1)}, bf16[256,2048]{1,0:T(8,128)(2,1)}, bf16[1024,384]{1,0:T(8,128)(2,1)}, bf16[128,2048]{1,0:T(8,128)(2,1)}, bf16...) custom-call(s32[1,1024]{1,0:T(1,128)} %fusion.10.pos_row, s32[1024,1]{1,0:T(8,128)} %fusion.pos_column, ...), custom_call_target="tpu_custom_call" | custom-call | bytes 480000000 | tf_op jit(solution)/shard_map/backward/pallas_call | solution.py:371
  456.1 0.0 copy-start.3
  456.2 5.9 convolution_convert_fusion.joined
  462.1 0.0 copy-done.3
  462.1 0.6 pad.9
  462.7 137.2 %tail.1 = (bf16[512,8192]{1,0:T(8,128)(2,1)}, bf16[512,8192]{1,0:T(8,128)(2,1)}, bf16[4224,640]{1,0:T(8,128)(2,1)}) custom-call(bf16[2,256,2048]{2,1,0:T(8,128)(2,1)} %get-tuple-element.89.pair, bf16[2048,384]{1,0:T(8,128)(2,1)} %convolution_convert_fusion.joined, bf16[256,2048]{1,0:T(8,128)(2,1)} %get-tuple-element.92.out_part, bf16[64,640]{1,0:T(8,128)(2,1)} %bitcast.36), custom_call_target="tpu_custom_call" | custom-call | bytes 390000000 | tf_op jit(solution)/shard_map/tail/pallas_call | solution.py:371
  600.0 0.0 copy-start.1
  600.0 0.0 copy-start
  600.0 28.6 %widen.1 = (f32[512,8192]{1,0:T(8,128)}, f32[512,8192]{1,0:T(8,128)}, f32[2048,2048]{1,0:T(8,128)}, f32[512,2048]{1,0:T(8,128)}, f32[512,512]{1,0:T(8,128)}, /*index=5*/f32[512,512]{1,0:T(8,128)}, f32[512,2048]{1,0:T(8,128)}) custom-call(bf16[8,528,640]{2,1,0:T(8,128)(2,1)} %bitcast.24, bf16[512,8192]{1,0:T(8,128)(2,1)} %get-tuple-element.95.refs_0_, ...), custom_call_target="tpu_custom_call" | custom-call | tf_op jit(solution)/shard_map/widen/pallas_call | solution.py:538
  628.6 0.9 convert_reduce_fusion
  629.5 0.6 fusion.15
  630.1 0.0 copy-done.1
  630.1 0.8 copy.50
  630.9 0.0 copy-done
  630.9 0.8 copy.51
  (12 shorter events, 0.3 us)
Async XLA Ops:
  0.6 7.7 %copy-start.4 = (f32[512]{0:T(512)S(1)}, f32[512]{0:T(512)}, u32[]{:S(2)}) copy-start(f32[512]{0:T(512)} %param.19) | copy-start | bytes 6148
  0.7 7.7 %copy-start.5 = (f32[512]{0:T(512)S(1)}, f32[512]{0:T(512)}, u32[]{:S(2)}) copy-start(f32[512]{0:T(512)} %param.24) | copy-start | bytes 6148
  8.4 0.6 copy-start.2
  456.1 5.9 copy-start.3
  600.0 30.1 %copy-start.1 = (bf16[128,2048]{1,0:T(8,128)(2,1)S(1)}, bf16[128,2048]{1,0:T(8,128)(2,1)}, u32[]{:S(2)}) copy-start(bf16[128,2048]{1,0:T(8,128)(2,1)} %get-tuple-element.87) | copy-start | bytes 1572868
  600.0 30.9 %copy-start = (bf16[128,2048]{1,0:T(8,128)(2,1)S(1)}, bf16[128,2048]{1,0:T(8,128)(2,1)}, u32[]{:S(2)}) copy-start(bf16[128,2048]{1,0:T(8,128)(2,1)} %get-tuple-element.88) | copy-start | bytes 1572868
